TPU v7x, 256 devices: a whole 4x4x8 slice. The times are simulated.
256 devices in a mesh: group: 32 (over x, z), expert: 8 (over y, core).
Axes of the slice: x: 4, y: 4, z: 8, core: 2. Of those that a mesh axis runs over, the one named last changes fastest.
Arguments:
- hidden_in: bfloat16 [16384, 2048], P(('group', 'expert')), may hold values from -6 to 6
- cache_len: int32 [32], replicated, may hold values from 1 to 2048, 32768 in all
- page_table: int32 [32, 128], replicated, may hold values from 0 to 4095, as said below
- pool: bfloat16 [4096, 2, 16, 2048], P('group', None, None, 'expert'), may hold values from -200 to 200
- attn_gain: float32 [2048], replicated, may hold values from 0.1 to 1.9
- w_qkv: bfloat16 [2048, 3, 2048], P(None, None, 'expert'), may hold values from -0.125 to 0.125
- w_out: bfloat16 [2048, 2048], P('expert'), may hold values from -0.125 to 0.125
- moe_gain: float32 [2048], replicated, may hold values from 0.1 to 1.9
- w_gate: bfloat16 [8, 2048, 512], P('expert'), may hold values from -0.125 to 0.125
- w_up: bfloat16 [8, 2048, 512], P('expert'), may hold values from -0.125 to 0.125
- w_down: bfloat16 [8, 512, 2048], P('expert'), may hold values from -0.25 to 0.25
- expert_ids: int32 [16384, 2], P(('group', 'expert')), may hold values from 0 to 7, all different within a row; in each aligned block of 64 rows (0 to 63, 64 to 127, ...) at most 32 rows name the same one
- gate_weights: float32 [16384, 2], P(('group', 'expert')), may hold values from 0.05 to 0.8
Outputs:
- hidden_out: float32 [16384, 2048], P(('group', 'expert'))
Inputs may be any that keep to these rules, and one draw needn't show every extreme that they name: `cache_len`: the longest request holds exactly 2048 cached tokens. `page_table`: every pool page is named exactly once; rows g * 128 to (g + 1) * 128 - 1 of the pool form group g's part, and each group's part that holds pages of a request holds exactly 8 of them. `expert_ids`: a token names 2 different experts; within the rows of one device no expert is named more than 32 times.
All inputs are finite; a program needn't handle non-finite values.
Results may differ from a plain program's by a relative error of at most 0.012.
The roundings to bfloat16 on the way count: a program that leaves them out, or rounds other values in their place, can miss the bound.
Values may be sent and summed in bfloat16 or wider, within the bound.
A program may use at most 128 MiB of HBM per device.

v0:
```python
import jax
import jax.numpy as jnp
from jax import lax
from jax.sharding import PartitionSpec as P

HEAD_DIM = 128
NBLK = 8
CTX = 2048


def norm_rows(inputs, gain_vector):
    values = inputs.astype(jnp.float32)
    factor = lax.rsqrt(jnp.mean(values * values, axis=-1, keepdims=True) + 1e-05)
    return (values * factor * gain_vector).astype(jnp.bfloat16)


def rotate(vectors, positions):
    half_dim = vectors.shape[-1] // 2
    frequency = 10000.0 ** (-jnp.arange(half_dim).astype(jnp.float32) / half_dim)
    angles = positions[:, None] * frequency[None, :]
    cosine = jnp.cos(angles)[:, None, :]
    sine_part = jnp.sin(angles)[:, None, :]
    first_half = vectors[..., :half_dim]
    second_half = vectors[..., half_dim:]
    return jnp.concatenate(
        [
            first_half * cosine - second_half * sine_part,
            first_half * sine_part + second_half * cosine,
        ],
        axis=-1,
    )


def attend_block(softmax_state, queries, key_block, value_block, key_valid):
    old_peak, old_total, old_mixed = softmax_state
    score_scale = queries.shape[-1] ** (-0.5)
    scores = (
        jnp.einsum("qhd,khd->hqk", queries, key_block, preferred_element_type=jnp.float32)
        * score_scale
    )
    scores = jnp.where(key_valid[None], scores, -1e30)
    new_peak = jnp.maximum(old_peak, jnp.max(scores, axis=-1))
    weights = jnp.exp(scores - new_peak[..., None])
    factor = jnp.exp(old_peak - new_peak)
    new_total = old_total * factor + jnp.sum(weights, axis=-1)
    new_mixed = old_mixed * factor[..., None] + jnp.einsum(
        "hqk,khd->hqd",
        weights.astype(jnp.bfloat16),
        value_block,
        preferred_element_type=jnp.float32,
    )
    return (new_peak, new_total, new_mixed)


def cache_pass(
    softmax_state,
    queries,
    all_keys,
    all_values,
    length,
    turn_count,
    array_step,
    array_first,
    position_step,
    position_first,
    block_len,
):

    def step_once(turn_index, running):
        array_start = (array_first + array_step * turn_index) * block_len
        position_start = (position_first + position_step * turn_index) * block_len
        key_block = lax.dynamic_slice_in_dim(all_keys, array_start, block_len, 0)
        value_block = lax.dynamic_slice_in_dim(all_values, array_start, block_len, 0)
        key_valid = (position_start + jnp.arange(block_len, dtype=jnp.int32) < length)[None, :]
        return attend_block(running, queries, key_block, value_block, key_valid)

    return lax.fori_loop(0, turn_count, step_once, softmax_state)


def shards(
    hidden_in,
    cache_len,
    page_table,
    pool,
    attn_gain,
    w_qkv,
    w_out,
    moe_gain,
    w_gate,
    w_up,
    w_down,
    expert_ids,
    gate_weights,
):
    groups = lax.axis_size("group")
    expert_lanes = lax.axis_size("expert")
    group_index = lax.axis_index("group")
    tok_rows = hidden_in.shape[0]
    model_width = hidden_in.shape[1]
    local_width = w_out.shape[0]
    head_size = HEAD_DIM
    local_heads = local_width // head_size
    new_count = tok_rows * expert_lanes
    block_len = CTX // NBLK
    length = cache_len[group_index]
    normed = norm_rows(hidden_in, attn_gain)
    projection = w_qkv.reshape(model_width, 3 * local_width)
    projected = jnp.dot(
        lax.all_gather(normed, "expert", axis=0, tiled=True),
        projection,
        preferred_element_type=jnp.float32,
    )
    projected = projected.reshape(new_count, 3, local_heads, head_size)
    positions = (length + jnp.arange(new_count, dtype=jnp.int32)).astype(jnp.float32)
    queries = rotate(projected[:, 0], positions).astype(jnp.bfloat16)
    new_keys = rotate(projected[:, 1], positions).astype(jnp.bfloat16)
    new_values = projected[:, 2].astype(jnp.bfloat16)
    pages_per = page_table.shape[1]
    page_most = max(1, pages_per // min(groups, 16))
    owner_group = page_table // pages_per
    local_slot = page_table % pages_per
    page_order = jnp.arange(pages_per, dtype=jnp.int32)
    before = page_order[None, :] < page_order[:, None]
    same_owner = owner_group[:, :, None] == owner_group[:, None, :]
    slot_rank = jnp.sum(jnp.logical_and(same_owner, before[None]), axis=-1)
    requests = jnp.arange(page_table.shape[0], dtype=jnp.int32)
    target = jnp.where(owner_group == group_index, requests[:, None], groups)
    send_index = (
        jnp.zeros((groups, page_most), jnp.int32).at[target, slot_rank].set(local_slot, mode="drop")
    )
    outgoing = pool[send_index]
    arrived = lax.all_to_all(outgoing, "group", split_axis=0, concat_axis=0, tiled=True)
    arrived = arrived.reshape((groups * page_most,) + pool.shape[1:])
    cache_pages = arrived[owner_group[group_index] * page_most + slot_rank[group_index]]
    cache_keys = cache_pages[:, 0].reshape(CTX, local_heads, head_size)
    cache_values = cache_pages[:, 1].reshape(CTX, local_heads, head_size)
    row_order = jnp.arange(new_count, dtype=jnp.int32)
    causal = row_order[None, :] <= row_order[:, None]
    start_state = (
        jnp.full((local_heads, new_count), -1e30, jnp.float32),
        jnp.zeros((local_heads, new_count), jnp.float32),
        jnp.zeros((local_heads, new_count, head_size), jnp.float32),
    )
    softmax_state = attend_block(start_state, queries, new_keys, new_values, causal)
    block_count = (length + block_len - 1) // block_len
    softmax_state = cache_pass(
        softmax_state, queries, cache_keys, cache_values, length, block_count, 1, 0, 1, 0, block_len
    )
    row_total = softmax_state[1]
    row_mixed = softmax_state[2]
    attended = (
        jnp.transpose(row_mixed / row_total[..., None], (1, 0, 2))
        .reshape(new_count, local_width)
        .astype(jnp.bfloat16)
    )
    rows_piece = attended
    head_sum = lax.psum_scatter(
        jnp.dot(rows_piece, w_out, preferred_element_type=jnp.float32).astype(jnp.bfloat16),
        "expert",
        scatter_dimension=0,
        tiled=True,
    ).astype(jnp.float32)
    residual = hidden_in.astype(jnp.float32) + head_sum
    moe_in = norm_rows(residual, moe_gain)
    route_count = expert_ids.shape[1]
    capacity = 2 * tok_rows * route_count // expert_lanes
    flat_expert = expert_ids.reshape(-1)
    assign_index = jnp.arange(flat_expert.shape[0], dtype=jnp.int32)
    earlier = assign_index[None, :] < assign_index[:, None]
    slot_index = jnp.sum(
        jnp.logical_and(flat_expert[:, None] == flat_expert[None, :], earlier), axis=-1
    )
    token_of = assign_index // route_count
    outgoing_rows = (
        jnp.zeros((expert_lanes, capacity, model_width), jnp.bfloat16)
        .at[flat_expert, slot_index]
        .set(moe_in[token_of])
    )
    rows_piece = lax.all_to_all(outgoing_rows, "expert", split_axis=0, concat_axis=0, tiled=True)
    flat_rows = rows_piece.reshape(-1, rows_piece.shape[-1])
    gate_part = jnp.dot(flat_rows, w_gate[0], preferred_element_type=jnp.float32)
    up_part = jnp.dot(flat_rows, w_up[0], preferred_element_type=jnp.float32)
    hidden = (jax.nn.silu(gate_part) * up_part).astype(jnp.bfloat16)
    result = (
        jnp.dot(hidden, w_down[0], preferred_element_type=jnp.float32)
        .astype(jnp.bfloat16)
        .reshape(rows_piece.shape)
    )
    returned = lax.all_to_all(result, "expert", split_axis=0, concat_axis=0, tiled=True)
    picked = returned.reshape(expert_lanes * capacity, model_width)[
        flat_expert * capacity + slot_index
    ]
    weighted = jnp.sum(
        picked.reshape(tok_rows, route_count, model_width).astype(jnp.float32)
        * gate_weights[..., None],
        axis=1,
    )
    return residual + weighted


def solution(mesh):
    placed = (
        P(("group", "expert"), None),
        P(),
        P(),
        P("group", None, None, "expert"),
        P(),
        P(None, None, "expert"),
        P("expert", None),
        P(),
        P("expert", None, None),
        P("expert", None, None),
        P("expert", None, None),
        P(("group", "expert"), None),
        P(("group", "expert"), None),
    )
    return jax.shard_map(
        shards, mesh=mesh, in_specs=placed, out_specs=P(("group", "expert"), None), check_vma=False
    )
```

profile of v0, /device:TPU:1, one launch (start us, length us, event | category | flops | bytes accessed | tf_op | source)
XLA Modules:
  0.0 290.4 jit_solution(8206114922236137174)
XLA Ops:
  10.2 15.5 %scatter_custom_fusion.1 = s32[256]{0:T(256)S(1)} fusion(s32[4096]{0:T(1024)S(1)} %select_bitcast_fusion, s32[4096]{0:T(1024)S(1)} %get-tuple-element.128, s32[]{:T(128)} %constant.99.clone.1), kind=kCustom, calls=%fused_computation.118 | custom fusion | bytes 1028
  26.0 2.8 gather_fusion
  28.8 12.1 %all-to-all-start = ((bf16[32,8,2,16,256]{4,3,2,1,0:T(8,128)(2,1)}), bf16[32,8,2,16,256]{4,3,2,1,0:T(8,128)(2,1)}, u32[]{:S(2)}, u32[]{:S(2)}) async-start(bf16[32,8,2,16,256]{4,3,2,1,0:T(8,128)(2,1)} %bitcast.83), calls=%async_computation | async-start | bytes 8388608 | tf_op jit(solution)/shard_map/all_to_all | solution.py:132
  43.3 4.8 %copy.51 = bf16[2048,3,256]{0,2,1:T(8,128)(2,1)} copy(bf16[2048,3,256]{2,0,1:T(8,128)(2,1)} %param.20) | data formatting | bytes 6291456 | tf_op args[5]
  49.3 24.3 %all-gather.2.cloned.1.call-done = bf16[512,2048]{1,0:T(8,128)(2,1)} async-done(((bf16[64,2048]{1,0:T(8,128)(2,1)}), bf16[512,2048]{1,0:T(8,128)(2,1)}) %all-gather.2.cloned.1.call-update) | async-done | bytes 2097168 | tf_op jit(solution)/shard_map/all_gather | solution.py:109
  73.6 4.3 %fusion.8 = f32[512,3,2,128]{0,3,2,1:T(8,128)S(1)} fusion(bf16[3,2,128,2048]{3,2,1,0:T(8,128)(2,1)} %bitcast.84, bf16[512,2048]{1,0:T(8,128)(2,1)} %all-gather.2.cloned.1.call-done), kind=kOutput, calls=%fused_computation.23 | convolution fusion | flops 1610612736 | bytes 6815744 | tf_op jit(solution)/shard_map/dot_general | solution.py:108
  81.5 1.9 convolution_add_fusion.1
  83.4 50.1 %all-to-all-done = bf16[32,8,2,16,256]{4,3,2,1,0:T(8,128)(2,1)} async-done(((bf16[32,8,2,16,256]{4,3,2,1,0:T(8,128)(2,1)}), bf16[32,8,2,16,256]{4,3,2,1,0:T(8,128)(2,1)}, u32[]{:S(2)}, u32[]{:S(2)}) %all-to-all-start) | async-done | bytes 4194336 | tf_op jit(solution)/shard_map/all_to_all | solution.py:132
  133.5 4.2 %gather_fusion.1 = bf16[128,2,16,256]{3,2,1,0:T(8,128)(2,1)} fusion(bf16[256,2,16,256]{3,2,1,0:T(8,128)(2,1)} %bitcast.16, s32[1024]{0:T(1024)S(1)} %pad_clamp_fusion.2), kind=kCustom, calls=%fused_computation.1 | custom fusion | bytes 4194816 | tf_op jit(solution)/shard_map/gather | solution.py:134
  137.7 3.1 %fusion.63 = (bf16[128,1,16,256]{3,2,1,0:T(8,128)(2,1)}, bf16[128,1,16,256]{3,2,1,0:T(8,128)(2,1)}) fusion(bf16[128,2,16,256]{3,2,1,0:T(8,128)(2,1)} %gather_fusion.1), kind=kLoop, calls=%fused_computation.130 | loop fusion | bytes 4194304 | tf_op jit(solution)/shard_map/slice | solution.py:136
  140.8 2.2 reshape_squeeze.6
  142.9 2.2 reshape_squeeze.7
  145.1 22.8 %while.14 = (s32[]{:T(128)}, f32[2,512]{1,0:T(2,128)S(1)}, f32[2,512]{1,0:T(2,128)S(1)}, f32[2,512,128]{2,1,0:T(8,128)S(1)}, s32[]{:T(128)}, /*index=5*/s32[]{:T...) while((s32[]{:T(128)}, f32[2,512]{1,0:T(2,128)S(1)}, ...), condition=%wide.region_8.9_spmd, body=%wide.region_5.8_spmd.sunk | while | flops 136317440 | bytes 5309111 | solution.py:77
  170.0 3.3 %convolution_convert_fusion = bf16[512,2048]{1,0:T(8,128)(2,1)} fusion(bf16[512,256]{0,1:T(8,128)(2,1)S(1)} %bitcast.85, bf16[256,2048]{1,0:T(8,128)(2,1)} %param.21), kind=kOutput, calls=%fused_computation.21 | convolution fusion | flops 537919488 | bytes 3407872 | tf_op jit(solution)/shard_map/dot_general | solution.py:158
  174.6 34.2 %reduce-scatter.2.cloned.1.call-done = bf16[64,2048]{1,0:T(8,128)(2,1)} async-done(((bf16[512,2048]{1,0:T(8,128)(2,1)}), bf16[64,2048]{1,0:T(8,128)(2,1)}) %reduce-scatter.2.cloned.1.call-update) | async-done | bytes 262160 | tf_op jit(solution)/shard_map/reduce_scatter | solution.py:157
  211.1 1.7 gather_fusion.2
  212.9 17.0 %scatter_fusion = bf16[8,32,2048]{2,1,0:T(8,128)(2,1)S(1)} fusion(bf16[8,32,2048]{2,1,0:T(8,128)(2,1)S(1)} %broadcast_in_dim.54, s32[128]{0:T(128)S(1)} %get-tuple-element.134, bf16[128,2048]{1,0:T(8,128)(2,1)} %gather_fusion.2), kind=kCustom, calls=%fused_computation.4 | custom fusion | bytes 1573888 | tf_op jit(solution)/shard_map/scatter | solution.py:177
  229.9 20.6 %all_to_all.15 = bf16[8,32,2048]{2,1,0:T(8,128)(2,1)S(1)} all-to-all(bf16[8,32,2048]{2,1,0:T(8,128)(2,1)S(1)} %scatter_fusion), channel_id=1, replica_groups=mesh['group'=32,'expert'=8] {'expert'}, dimensions={0} | all-to-all | bytes 2097152 | tf_op jit(solution)/shard_map/all_to_all | solution.py:179
  252.2 4.9 %convolution_convert_fusion.1 = bf16[256,2048]{1,0:T(8,128)(2,1)} fusion(bf16[1,512,2048]{2,1,0:T(8,128)(2,1)} %param.25, bf16[256,2048]{1,0:T(8,128)(2,1)} %bitcast.88, bf16[1,2048,512]{2,1,0:T(8,128)(2,1)} %param.24, f32[256,512]{1,0:T(8,128)S(1)} %fusion.13), kind=kOutput, calls=%fused_computation.22 | convolution fusion | flops 1075052544 | bytes 6815744 | tf_op jit(solution)/shard_map/dot_general | solution.py:185
  257.1 4.6 %all-to-all-start.2 = ((bf16[8,32,2048]{2,1,0:T(8,128)(2,1)}), bf16[8,32,2048]{2,1,0:T(8,128)(2,1)S(1)}, u32[]{:S(2)}, u32[]{:S(2)}) async-start(bf16[8,32,2048]{2,1,0:T(8,128)(2,1)} %bitcast.86), calls=%async_computation.3 | async-start | bytes 2097152 | tf_op jit(solution)/shard_map/all_to_all | solution.py:189
  261.9 14.9 %all-to-all-done.2 = bf16[8,32,2048]{2,1,0:T(8,128)(2,1)S(1)} async-done(((bf16[8,32,2048]{2,1,0:T(8,128)(2,1)}), bf16[8,32,2048]{2,1,0:T(8,128)(2,1)S(1)}, u32[]{:S(2)}, u32[]{:S(2)}) %all-to-all-start.2) | async-done | bytes 1048608 | tf_op jit(solution)/shard_map/all_to_all | solution.py:189
  276.8 1.7 gather_fusion.3
  278.5 1.7 reshape.312
  281.7 1.8 fusion.39
  (134 shorter events, 41.5 us)
Async XLA Ops:
  6.5 19.5 %copy-start = (bf16[128,2,16,256]{3,2,1,0:T(8,128)(2,1)S(1)}, bf16[128,2,16,256]{3,2,1,0:T(8,128)(2,1)}, u32[]{:S(2)}) copy-start(bf16[128,2,16,256]{3,2,1,0:T(8,128)(2,1)} %param.18) | copy-start | bytes 6291460
  28.8 12.2 %copy-start.1 = (bf16[64,2048]{1,0:T(8,128)(2,1)S(1)}, bf16[64,2048]{1,0:T(8,128)(2,1)}, u32[]{:S(2)}) copy-start(bf16[64,2048]{1,0:T(8,128)(2,1)} %param.15) | copy-start | bytes 786436
  28.8 12.3 %copy-start.4 = (f32[2048]{0:T(1024)S(1)}, f32[2048]{0:T(1024)}, u32[]{:S(2)}) copy-start(f32[2048]{0:T(1024)} %param.19) | copy-start | bytes 24580
  28.8 13.3 %copy-start.9 = (s32[32]{0:T(128)S(1)}, s32[32]{0:T(128)}, u32[]{:S(2)}) copy-start(s32[32]{0:T(128)} %param.16) | copy-start | bytes 388
  28.8 104.7 %all-to-all-start = ((bf16[32,8,2,16,256]{4,3,2,1,0:T(8,128)(2,1)}), bf16[32,8,2,16,256]{4,3,2,1,0:T(8,128)(2,1)}, u32[]{:S(2)}, u32[]{:S(2)}) async-start(bf16[32,8,2,16,256]{4,3,2,1,0:T(8,128)(2,1)} %bitcast.83), calls=%async_computation | async-start | bytes 8388608 | tf_op jit(solution)/shard_map/all_to_all | solution.py:132
  40.9 32.6 %all-gather.2.cloned.1.call-start = ((), (), s32[]{:S(2)}) async-start(), calls=%async_computation.4 | async-start | bytes 2359296 | tf_op jit(solution)/shard_map/all_gather | solution.py:109
  42.0 166.8 %reduce-scatter.2.cloned.1.call-start = ((), (), s32[]{:S(2)}) async-start(), calls=%async_computation.5 | async-start | bytes 2359296 | tf_op jit(solution)/shard_map/reduce_scatter | solution.py:157
  77.9 1.3 copy-start.3
  173.3 0.7 copy-start.6
  173.3 36.6 %copy-start.5 = (f32[2048]{0:T(1024)S(1)}, f32[2048]{0:T(1024)}, u32[]{:S(2)}) copy-start(f32[2048]{0:T(1024)} %param.22) | copy-start | bytes 24580
  229.9 21.6 %copy-start.8 = (bf16[1,2048,512]{2,1,0:T(8,128)(2,1)S(1)}, bf16[1,2048,512]{2,1,0:T(8,128)(2,1)}, u32[]{:S(2)}) copy-start(bf16[1,2048,512]{2,1,0:T(8,128)(2,1)} %param.23) | copy-start | bytes 6291460
  250.5 1.0 copy-start.2
  257.1 4.6 %copy-start.7 = (f32[64,2]{0,1:T(2,128)S(1)}, f32[64,2]{0,1:T(2,128)}, u32[]{:S(2)}) copy-start(f32[64,2]{0,1:T(2,128)} %param.27) | copy-start | bytes 1540
  257.1 19.6 %all-to-all-start.2 = ((bf16[8,32,2048]{2,1,0:T(8,128)(2,1)}), bf16[8,32,2048]{2,1,0:T(8,128)(2,1)S(1)}, u32[]{:S(2)}, u32[]{:S(2)}) async-start(bf16[8,32,2048]{2,1,0:T(8,128)(2,1)} %bitcast.86), calls=%async_computation.3 | async-start | bytes 2097152 | tf_op jit(solution)/shard_map/all_to_all | solution.py:189
Sparse Core Ops, SparseCore 0:
  43.6 29.9 all-gather.1
  173.5 35.2 reduce-scatter.1
where the time goes:
time: 292 us; the launch traced here: 290 us
  waiting for transfers between devices  123 us (42%)
  local copies, waits for them, and re-layouts  70.5 us (24%)
  matrix products  23.5 us (8%)
  other arithmetic  20.6 us (7%)
  blocking collectives  20.6 us (7%)
  starting transfers between devices  16.8 us (6%)
  between operations  14.3 us (5%)
    all_to_all x1, waiting for transfers between devices, shards(): lax.all_to_all(outgoing, 'group', split_axis=0, concat_axis=0, tiled=True)  50.1 us
    reduce_scatter x1, waiting for transfers between devices, shards(): lax.psum_scatter(jnp.dot(rows_piece, w_out, preferred_element_type=jnp.fl...  34.2 us
    all_gather x1, waiting for transfers between devices, shards(): lax.all_gather(normed, 'expert', axis=0, tiled=True)  24.3 us
    unnamed x25, local copies, waits for them, and re-layouts  22.3 us
    all_to_all x1, blocking collectives, shards(): lax.all_to_all(outgoing_rows, 'expert', split_axis=0, concat_axis=0, tile...  20.6 us
    scatter x1, local copies, waits for them, and re-layouts, shards(): outgoing_rows = jnp.zeros((expert_lanes, capacity, model_width), jnp.bflo...  17 us
    all_to_all x1, waiting for transfers between devices, shards(): lax.all_to_all(result, 'expert', split_axis=0, concat_axis=0, tiled=True)  14.9 us
    all_to_all x1, starting transfers between devices, shards(): lax.all_to_all(outgoing, 'group', split_axis=0, concat_axis=0, tiled=True)  12.1 us
  transfers between devices with their start and end apart: 4, of which 4 were waited for; matrix products, arithmetic and copies ran while one was open for 6% of the time, Pallas kernels for 0%

commit v1 on v0

--- a/solution.py
+++ b/solution.py
@@ -120,18 +120,18 @@
     owner_group = page_table // pages_per
     local_slot = page_table % pages_per
     page_order = jnp.arange(pages_per, dtype=jnp.int32)
-    before = page_order[None, :] < page_order[:, None]
-    same_owner = owner_group[:, :, None] == owner_group[:, None, :]
-    slot_rank = jnp.sum(jnp.logical_and(same_owner, before[None]), axis=-1)
-    requests = jnp.arange(page_table.shape[0], dtype=jnp.int32)
-    target = jnp.where(owner_group == group_index, requests[:, None], groups)
-    send_index = (
-        jnp.zeros((groups, page_most), jnp.int32).at[target, slot_rank].set(local_slot, mode="drop")
-    )
+    mine = (owner_group == group_index).astype(jnp.int32)
+    mine_rank = jnp.cumsum(mine, axis=1) - mine
+    slot_ids = jnp.arange(page_most, dtype=jnp.int32)
+    pick = (mine[:, None, :] > 0) & (mine_rank[:, None, :] == slot_ids[None, :, None])
+    send_index = jnp.sum(jnp.where(pick, local_slot[:, None, :], 0), axis=-1)
     outgoing = pool[send_index]
     arrived = lax.all_to_all(outgoing, "group", split_axis=0, concat_axis=0, tiled=True)
     arrived = arrived.reshape((groups * page_most,) + pool.shape[1:])
-    cache_pages = arrived[owner_group[group_index] * page_most + slot_rank[group_index]]
+    my_owner = owner_group[group_index]
+    before = page_order[None, :] < page_order[:, None]
+    my_rank = jnp.sum(jnp.logical_and(my_owner[:, None] == my_owner[None, :], before), axis=-1)
+    cache_pages = arrived[my_owner * page_most + my_rank]
     cache_keys = cache_pages[:, 0].reshape(CTX, local_heads, head_size)
     cache_values = cache_pages[:, 1].reshape(CTX, local_heads, head_size)
     row_order = jnp.arange(new_count, dtype=jnp.int32)
@@ -171,10 +171,17 @@
         jnp.logical_and(flat_expert[:, None] == flat_expert[None, :], earlier), axis=-1
     )
     token_of = assign_index // route_count
+    slot_of = flat_expert * capacity + slot_index
+    dest_ids = jnp.arange(expert_lanes * capacity, dtype=jnp.int32)
+    token_ids = jnp.arange(tok_rows, dtype=jnp.int32)
+    hit = (slot_of[None, :] == dest_ids[:, None])
+    source_token = jnp.sum(jnp.where(hit, token_of[None, :], 0), axis=-1)
+    has_source = jnp.any(hit, axis=-1)
+    select = ((source_token[:, None] == token_ids[None, :]) & has_source[:, None]).astype(jnp.bfloat16)
     outgoing_rows = (
-        jnp.zeros((expert_lanes, capacity, model_width), jnp.bfloat16)
-        .at[flat_expert, slot_index]
-        .set(moe_in[token_of])
+        jnp.dot(select, moe_in, preferred_element_type=jnp.float32)
+        .astype(jnp.bfloat16)
+        .reshape(expert_lanes, capacity, model_width)
     )
     rows_piece = lax.all_to_all(outgoing_rows, "expert", split_axis=0, concat_axis=0, tiled=True)
     flat_rows = rows_piece.reshape(-1, rows_piece.shape[-1])

time: 292 us -> 255 us (0.87)
  local copies, waits for them, and re-layouts: 70.5 us -> 35.1 us
    scatter x1 -> x0, local copies, waits for them, and re-layouts: 17 us -> none  [shards(): outgoing_rows = jnp.zeros((expert_lanes, capacity, model_width), jnp.bflo...]
    unnamed x25 -> x21, local copies, waits for them, and re-layouts: 22.3 us -> 5.69 us
    gather x2 -> x1, local copies, waits for them, and re-layouts: 5.92 us -> 4.2 us  [shards(): cache_pages = arrived[my_owner * page_most + my_rank]]
  transfers between devices with their start and end apart: 4 -> 4, of which waited for: 4 -> 4; matrix products, arithmetic and copies ran while one was open for 6% -> 7% of each run, Pallas kernels for 0% -> 0%
where the time goes in v1:
time: 255 us; the launch traced here: 254 us
  waiting for transfers between devices  123 us (48%)
  local copies, waits for them, and re-layouts  35.1 us (14%)
  matrix products  25.6 us (10%)
  blocking collectives  20.5 us (8%)
  other arithmetic  19 us (7%)
  starting transfers between devices  16.8 us (7%)
  between operations  14.2 us (6%)
    all_to_all x1, waiting for transfers between devices, shards(): lax.all_to_all(outgoing, 'group', split_axis=0, concat_axis=0, tiled=True)  50.1 us
    reduce_scatter x1, waiting for transfers between devices, shards(): lax.psum_scatter(jnp.dot(rows_piece, w_out, preferred_element_type=jnp.fl...  33.9 us
    all_gather x1, waiting for transfers between devices, shards(): lax.all_gather(normed, 'expert', axis=0, tiled=True)  24.1 us
    all_to_all x1, blocking collectives, shards(): lax.all_to_all(outgoing_rows, 'expert', split_axis=0, concat_axis=0, tile...  20.5 us
    all_to_all x1, waiting for transfers between devices, shards(): lax.all_to_all(result, 'expert', split_axis=0, concat_axis=0, tiled=True)  14.6 us
    all_to_all x1, starting transfers between devices, shards(): lax.all_to_all(outgoing, 'group', split_axis=0, concat_axis=0, tiled=True)  12.1 us
    dynamic_slice x8, local copies, waits for them, and re-layouts, step_once(): lax.dynamic_slice_in_dim(all_values, array_start, block_len, 0)  9.23 us
    dot_general x9, matrix products, attend_block(): jnp.einsum('hqk,khd->hqd', weights.astype(jnp.bfloat16), value_block, pre...  6.17 us
  transfers between devices with their start and end apart: 4, of which 4 were waited for; matrix products, arithmetic and copies ran while one was open for 7% of the time, Pallas kernels for 0%

profile of v1, /device:TPU:1, one launch (start us, length us, event | category | flops | bytes accessed | tf_op | source)
XLA Modules:
  0.0 254.3 jit_solution(17402991465970283972)
XLA Ops:
  9.2 2.8 %gather_fusion = bf16[256,2,16,256]{3,2,1,0:T(8,128)(2,1)} fusion(bf16[128,2,16,256]{3,2,1,0:T(8,128)(2,1)S(1)} %copy-done, s32[1024]{0:T(1024)S(1)} %pad_clamp_fusion.2), kind=kCustom, calls=%fused_computation | custom fusion | bytes 8389632 | tf_op jit(solution)/shard_map/gather | solution.py:128
  12.0 12.1 %all-to-all-start = ((bf16[32,8,2,16,256]{4,3,2,1,0:T(8,128)(2,1)}), bf16[32,8,2,16,256]{4,3,2,1,0:T(8,128)(2,1)}, u32[]{:S(2)}, u32[]{:S(2)}) async-start(bf16[32,8,2,16,256]{4,3,2,1,0:T(8,128)(2,1)} %bitcast.77), calls=%async_computation | async-start | bytes 8388608 | tf_op jit(solution)/shard_map/all_to_all | solution.py:129
  26.4 4.8 %copy.50 = bf16[2048,3,256]{0,2,1:T(8,128)(2,1)} copy(bf16[2048,3,256]{2,0,1:T(8,128)(2,1)} %param.20) | data formatting | bytes 6291456 | tf_op args[5]
  32.7 24.1 %all-gather.2.cloned.1.call-done = bf16[512,2048]{1,0:T(8,128)(2,1)} async-done(((bf16[64,2048]{1,0:T(8,128)(2,1)}), bf16[512,2048]{1,0:T(8,128)(2,1)}) %all-gather.2.cloned.1.call-update) | async-done | bytes 2097168 | tf_op jit(solution)/shard_map/all_gather | solution.py:109
  56.7 4.3 %fusion.8 = f32[512,3,2,128]{0,3,2,1:T(8,128)S(1)} fusion(bf16[3,2,128,2048]{3,2,1,0:T(8,128)(2,1)} %bitcast.79, bf16[512,2048]{1,0:T(8,128)(2,1)} %all-gather.2.cloned.1.call-done), kind=kOutput, calls=%fused_computation.21 | convolution fusion | flops 1610612736 | bytes 6815744 | tf_op jit(solution)/shard_map/dot_general | solution.py:108
  62.6 1.5 fusion.15
  64.7 1.9 convolution_add_fusion.1
  66.6 50.1 %all-to-all-done = bf16[32,8,2,16,256]{4,3,2,1,0:T(8,128)(2,1)} async-done(((bf16[32,8,2,16,256]{4,3,2,1,0:T(8,128)(2,1)}), bf16[32,8,2,16,256]{4,3,2,1,0:T(8,128)(2,1)}, u32[]{:S(2)}, u32[]{:S(2)}) %all-to-all-start) | async-done | bytes 4194336 | tf_op jit(solution)/shard_map/all_to_all | solution.py:129
  116.7 4.2 %gather_fusion.1 = bf16[128,2,16,256]{3,2,1,0:T(8,128)(2,1)} fusion(bf16[256,2,16,256]{3,2,1,0:T(8,128)(2,1)} %bitcast.12, s32[1024]{0:T(1024)S(1)} %pad_clamp_fusion.1), kind=kCustom, calls=%fused_computation.1 | custom fusion | bytes 4194816 | tf_op jit(solution)/shard_map/gather | solution.py:134
  120.9 3.1 %fusion.68 = (bf16[128,1,16,256]{3,2,1,0:T(8,128)(2,1)}, bf16[128,1,16,256]{3,2,1,0:T(8,128)(2,1)}) fusion(bf16[128,2,16,256]{3,2,1,0:T(8,128)(2,1)} %gather_fusion.1), kind=kLoop, calls=%fused_computation.130 | loop fusion | bytes 4194304 | tf_op jit(solution)/shard_map/slice | solution.py:136
  123.9 2.2 reshape_squeeze.6
  126.1 2.2 reshape_squeeze.7
  128.3 22.6 %while.14 = (s32[]{:T(128)}, f32[2,512]{1,0:T(2,128)S(1)}, f32[2,512]{1,0:T(2,128)S(1)}, f32[2,512,128]{2,1,0:T(8,128)S(1)}, s32[]{:T(128)}, /*index=5*/s32[]{:T...) while((s32[]{:T(128)}, f32[2,512]{1,0:T(2,128)S(1)}, ...), condition=%wide.region_9.10_spmd, body=%wide.region_6.9_spmd.sunk | while | flops 136317440 | bytes 5309111 | solution.py:77
  153.0 3.3 %convolution_convert_fusion = bf16[512,2048]{1,0:T(8,128)(2,1)} fusion(bf16[512,256]{0,1:T(8,128)(2,1)S(1)} %bitcast.80, bf16[256,2048]{1,0:T(8,128)(2,1)} %param.21), kind=kOutput, calls=%fused_computation.18 | convolution fusion | flops 537919488 | bytes 3407872 | tf_op jit(solution)/shard_map/dot_general | solution.py:158
  157.7 33.9 %reduce-scatter.2.cloned.1.call-done = bf16[64,2048]{1,0:T(8,128)(2,1)} async-done(((bf16[512,2048]{1,0:T(8,128)(2,1)}), bf16[64,2048]{1,0:T(8,128)(2,1)}) %reduce-scatter.2.cloned.1.call-update) | async-done | bytes 262160 | tf_op jit(solution)/shard_map/reduce_scatter | solution.py:157
  194.3 20.5 %all_to_all.15 = bf16[8,32,2048]{2,1,0:T(8,128)(2,1)S(1)} all-to-all(bf16[8,32,2048]{2,1,0:T(8,128)(2,1)S(1)} %bitcast.78), channel_id=1, replica_groups=mesh['group'=32,'expert'=8] {'expert'}, dimensions={0} | all-to-all | bytes 2097152 | tf_op jit(solution)/shard_map/all_to_all | solution.py:186
  214.8 1.5 fusion.13
  216.3 4.7 %convolution_convert_fusion.1 = bf16[256,2048]{1,0:T(8,128)(2,1)} fusion(bf16[1,512,2048]{2,1,0:T(8,128)(2,1)} %param.25, bf16[256,2048]{1,0:T(8,128)(2,1)S(1)} %bitcast.83, bf16[1,2048,512]{2,1,0:T(8,128)(2,1)} %param.24, f32[256,512]{1,0:T(8,128)} %fusion.13), kind=kOutput, calls=%fused_computation.19 | convolution fusion | flops 1075052544 | bytes 6815744 | tf_op jit(solution)/shard_map/dot_general | solution.py:192
  221.0 4.6 %all-to-all-start.2 = ((bf16[8,32,2048]{2,1,0:T(8,128)(2,1)}), bf16[8,32,2048]{2,1,0:T(8,128)(2,1)S(1)}, u32[]{:S(2)}, u32[]{:S(2)}) async-start(bf16[8,32,2048]{2,1,0:T(8,128)(2,1)} %bitcast.81), calls=%async_computation.3 | async-start | bytes 2097152 | tf_op jit(solution)/shard_map/all_to_all | solution.py:196
  226.0 14.6 %all-to-all-done.2 = bf16[8,32,2048]{2,1,0:T(8,128)(2,1)S(1)} async-done(((bf16[8,32,2048]{2,1,0:T(8,128)(2,1)}), bf16[8,32,2048]{2,1,0:T(8,128)(2,1)S(1)}, u32[]{:S(2)}, u32[]{:S(2)}) %all-to-all-start.2) | async-done | bytes 1048608 | tf_op jit(solution)/shard_map/all_to_all | solution.py:196
  240.6 1.7 gather_fusion.2
  242.4 1.7 reshape.240
  244.0 1.5 multiply_reduce_fusion
  245.6 1.8 fusion.39
  (130 shorter events, 36.4 us)
Async XLA Ops:
  6.5 2.7 %copy-start = (bf16[128,2,16,256]{3,2,1,0:T(8,128)(2,1)S(1)}, bf16[128,2,16,256]{3,2,1,0:T(8,128)(2,1)}, u32[]{:S(2)}) copy-start(bf16[128,2,16,256]{3,2,1,0:T(8,128)(2,1)} %param.18) | copy-start | bytes 6291460
  12.0 12.2 %copy-start.1 = (bf16[64,2048]{1,0:T(8,128)(2,1)S(1)}, bf16[64,2048]{1,0:T(8,128)(2,1)}, u32[]{:S(2)}) copy-start(bf16[64,2048]{1,0:T(8,128)(2,1)} %param.15) | copy-start | bytes 786436
  12.0 12.4 %copy-start.3 = (f32[2048]{0:T(1024)S(1)}, f32[2048]{0:T(1024)}, u32[]{:S(2)}) copy-start(f32[2048]{0:T(1024)} %param.19) | copy-start | bytes 24580
  12.0 13.3 %copy-start.8 = (s32[32]{0:T(128)S(1)}, s32[32]{0:T(128)}, u32[]{:S(2)}) copy-start(s32[32]{0:T(128)} %param.16) | copy-start | bytes 388
  12.0 104.7 %all-to-all-start = ((bf16[32,8,2,16,256]{4,3,2,1,0:T(8,128)(2,1)}), bf16[32,8,2,16,256]{4,3,2,1,0:T(8,128)(2,1)}, u32[]{:S(2)}, u32[]{:S(2)}) async-start(bf16[32,8,2,16,256]{4,3,2,1,0:T(8,128)(2,1)} %bitcast.77), calls=%async_computation | async-start | bytes 8388608 | tf_op jit(solution)/shard_map/all_to_all | solution.py:129
  24.1 32.6 %all-gather.2.cloned.1.call-start = ((), (), s32[]{:S(2)}) async-start(), calls=%async_computation.4 | async-start | bytes 2359296 | tf_op jit(solution)/shard_map/all_gather | solution.py:109
  25.2 166.3 %reduce-scatter.2.cloned.1.call-start = ((), (), s32[]{:S(2)}) async-start(), calls=%async_computation.5 | async-start | bytes 2359296 | tf_op jit(solution)/shard_map/reduce_scatter | solution.py:157
  61.1 1.3 copy-start.2
  156.3 0.7 copy-start.5
  156.3 36.5 %copy-start.4 = (f32[2048]{0:T(1024)S(1)}, f32[2048]{0:T(1024)}, u32[]{:S(2)}) copy-start(f32[2048]{0:T(1024)} %param.22) | copy-start | bytes 24580
  191.5 23.2 %copy-start.7 = (bf16[1,2048,512]{2,1,0:T(8,128)(2,1)S(1)}, bf16[1,2048,512]{2,1,0:T(8,128)(2,1)}, u32[]{:S(2)}) copy-start(bf16[1,2048,512]{2,1,0:T(8,128)(2,1)} %param.23) | copy-start | bytes 6291460
  221.0 4.9 %copy-start.6 = (f32[64,2]{0,1:T(2,128)S(1)}, f32[64,2]{0,1:T(2,128)}, u32[]{:S(2)}) copy-start(f32[64,2]{0,1:T(2,128)} %param.27) | copy-start | bytes 1540
  221.0 19.6 %all-to-all-start.2 = ((bf16[8,32,2048]{2,1,0:T(8,128)(2,1)}), bf16[8,32,2048]{2,1,0:T(8,128)(2,1)S(1)}, u32[]{:S(2)}, u32[]{:S(2)}) async-start(bf16[8,32,2048]{2,1,0:T(8,128)(2,1)} %bitcast.81), calls=%async_computation.3 | async-start | bytes 2097152 | tf_op jit(solution)/shard_map/all_to_all | solution.py:196
Sparse Core Ops, SparseCore 0:
  26.8 29.9 all-gather.1
  156.5 35.0 reduce-scatter.1

commit v2 on v1

--- a/solution.py
+++ b/solution.py
@@ -1,6 +1,8 @@
 import jax
 import jax.numpy as jnp
 from jax import lax
+from jax.experimental import pallas as pl
+from jax.experimental.pallas import tpu as pltpu
 from jax.sharding import PartitionSpec as P
 
 HEAD_DIM = 128
@@ -75,6 +77,92 @@
         return attend_block(running, queries, key_block, value_block, key_valid)
 
     return lax.fori_loop(0, turn_count, step_once, softmax_state)
+
+
+def attention_kernel(
+    slots_ref, len_ref, q_ref, nk_ref, nv_ref, arr_ref, o_ref, kbuf, vbuf, m_sc, l_sc, acc_sc
+):
+    head = pl.program_id(0)
+    rows, width = q_ref.shape
+    page = arr_ref.shape[2]
+    block_len = kbuf.shape[0]
+    pages_per_block = block_len // page
+    score_scale = width ** (-0.5)
+    lanes = pl.ds(pl.multiple_of(head * width, width), width)
+    q = q_ref[...]
+    dims = (((1,), (1,)), ((), ()))
+    scores = lax.dot_general(q, nk_ref[...], dims, preferred_element_type=jnp.float32) * score_scale
+    row_i = lax.broadcasted_iota(jnp.int32, (rows, rows), 0)
+    col_i = lax.broadcasted_iota(jnp.int32, (rows, rows), 1)
+    scores = jnp.where(col_i <= row_i, scores, -1e30)
+    peak = jnp.max(scores, axis=-1, keepdims=True)
+    weights = jnp.exp(scores - peak)
+    m_sc[...] = peak
+    l_sc[...] = jnp.sum(weights, axis=-1, keepdims=True)
+    acc_sc[...] = jnp.dot(weights.astype(jnp.bfloat16), nv_ref[...], preferred_element_type=jnp.float32)
+    length = len_ref[0]
+    block_count = (length + block_len - 1) // block_len
+
+    def one_block(b, carry):
+        for i in range(pages_per_block):
+            slot = slots_ref[b * pages_per_block + i]
+            kbuf[pl.ds(i * page, page), :] = arr_ref[slot, 0, :, lanes]
+            vbuf[pl.ds(i * page, page), :] = arr_ref[slot, 1, :, lanes]
+        block_scores = (
+            lax.dot_general(q, kbuf[...], dims, preferred_element_type=jnp.float32) * score_scale
+        )
+        position = b * block_len + lax.broadcasted_iota(jnp.int32, (rows, block_len), 1)
+        block_scores = jnp.where(position < length, block_scores, -1e30)
+        old_peak = m_sc[...]
+        new_peak = jnp.maximum(old_peak, jnp.max(block_scores, axis=-1, keepdims=True))
+        block_weights = jnp.exp(block_scores - new_peak)
+        factor = jnp.exp(old_peak - new_peak)
+        l_sc[...] = l_sc[...] * factor + jnp.sum(block_weights, axis=-1, keepdims=True)
+        acc_sc[...] = acc_sc[...] * factor + jnp.dot(
+            block_weights.astype(jnp.bfloat16), vbuf[...], preferred_element_type=jnp.float32
+        )
+        m_sc[...] = new_peak
+        return carry
+
+    lax.fori_loop(0, block_count, one_block, 0)
+    o_ref[...] = (acc_sc[...] / l_sc[...]).astype(o_ref.dtype)
+
+
+def paged_attention(slots, length, queries, new_keys, new_values, arrived, block_len):
+    rows, local_width = queries.shape
+    heads = local_width // HEAD_DIM
+    slot_count, _, page, _ = arrived.shape
+    column = lambda h, *_: (0, h)
+    spec = pl.BlockSpec((rows, HEAD_DIM), column)
+    cost = pl.CostEstimate(
+        flops=4 * rows * (rows + CTX) * local_width,
+        transcendentals=rows * (rows + CTX) * heads,
+        bytes_accessed=arrived.size * 2 + 4 * rows * local_width * 2,
+    )
+    return pl.pallas_call(
+        attention_kernel,
+        out_shape=jax.ShapeDtypeStruct((rows, local_width), jnp.bfloat16),
+        grid_spec=pltpu.PrefetchScalarGridSpec(
+            num_scalar_prefetch=2,
+            grid=(heads,),
+            in_specs=[
+                spec,
+                spec,
+                spec,
+                pl.BlockSpec(arrived.shape, lambda h, *_: (0, 0, 0, 0)),
+            ],
+            out_specs=spec,
+            scratch_shapes=[
+                pltpu.VMEM((block_len, HEAD_DIM), jnp.bfloat16),
+                pltpu.VMEM((block_len, HEAD_DIM), jnp.bfloat16),
+                pltpu.VMEM((rows, 1), jnp.float32),
+                pltpu.VMEM((rows, 1), jnp.float32),
+                pltpu.VMEM((rows, HEAD_DIM), jnp.float32),
+            ],
+        ),
+        compiler_params=pltpu.CompilerParams(vmem_limit_bytes=48 * 1024 * 1024),
+        cost_estimate=cost,
+    )(slots, length, queries, new_keys, new_values, arrived)
 
 
 def shards(
@@ -131,27 +219,15 @@
     my_owner = owner_group[group_index]
     before = page_order[None, :] < page_order[:, None]
     my_rank = jnp.sum(jnp.logical_and(my_owner[:, None] == my_owner[None, :], before), axis=-1)
-    cache_pages = arrived[my_owner * page_most + my_rank]
-    cache_keys = cache_pages[:, 0].reshape(CTX, local_heads, head_size)
-    cache_values = cache_pages[:, 1].reshape(CTX, local_heads, head_size)
-    row_order = jnp.arange(new_count, dtype=jnp.int32)
-    causal = row_order[None, :] <= row_order[:, None]
-    start_state = (
-        jnp.full((local_heads, new_count), -1e30, jnp.float32),
-        jnp.zeros((local_heads, new_count), jnp.float32),
-        jnp.zeros((local_heads, new_count, head_size), jnp.float32),
-    )
-    softmax_state = attend_block(start_state, queries, new_keys, new_values, causal)
-    block_count = (length + block_len - 1) // block_len
-    softmax_state = cache_pass(
-        softmax_state, queries, cache_keys, cache_values, length, block_count, 1, 0, 1, 0, block_len
-    )
-    row_total = softmax_state[1]
-    row_mixed = softmax_state[2]
-    attended = (
-        jnp.transpose(row_mixed / row_total[..., None], (1, 0, 2))
-        .reshape(new_count, local_width)
-        .astype(jnp.bfloat16)
+    slots = (my_owner * page_most + my_rank).astype(jnp.int32)
+    attended = paged_attention(
+        slots,
+        jnp.reshape(length, (1,)).astype(jnp.int32),
+        queries.reshape(new_count, local_width),
+        new_keys.reshape(new_count, local_width),
+        new_values.reshape(new_count, local_width),
+        arrived,
+        block_len,
     )
     rows_piece = attended
     head_sum = lax.psum_scatter(

time: 255 us -> 242 us (0.949)
  local copies, waits for them, and re-layouts: 35.1 us -> 12.8 us
  Pallas kernels: 0 us -> 15.5 us
  waiting for transfers between devices: 123 us -> 138 us
  matrix products: 25.6 us -> 14.1 us
  other arithmetic: 19 us -> 10.1 us
    pallas_call x0 -> x1, Pallas kernels: none -> 15.5 us  [paged_attention(): pl.pallas_call(attention_kernel, out_shape=jax.ShapeDtypeStruct((rows, lo...]
    dot_general x18 -> x0, matrix products: 10.2 us -> none  [the longest x9 6.17 us: attend_block(): jnp.einsum('hqk,khd->hqd', weights.astype(jnp.bfloat16), value_block, pre...]
    reduce_scatter x1, waiting for transfers between devices: 33.9 us -> 44 us  [shards(): lax.psum_scatter(jnp.dot(rows_piece, w_out, preferred_element_type=jnp.fl...]
    dynamic_slice x8 -> x0, local copies, waits for them, and re-layouts: 9.23 us -> none  [step_once(): lax.dynamic_slice_in_dim(all_values, array_start, block_len, 0)]
    all_to_all x1, waiting for transfers between devices: 50.1 us -> 54.8 us  [shards(): lax.all_to_all(outgoing, 'group', split_axis=0, concat_axis=0, tiled=True)]
    lt x8 -> x0, other arithmetic: 4.6 us -> none  [step_once(): position_start + jnp.arange(block_len, dtype=jnp.int32) < length]
    another operation x2 -> x0, local copies, waits for them, and re-layouts: 4.36 us -> none  [the longest x1 2.2 us: shards(): cache_values = cache_pages[:, 1].reshape(CTX, local_heads, head_size)]
    gather x1 -> x0, local copies, waits for them, and re-layouts: 4.2 us -> none  [shards(): cache_pages = arrived[my_owner * page_most + my_rank]]
  transfers between devices with their start and end apart: 4 -> 4, of which waited for: 4 -> 4; matrix products, arithmetic and copies ran while one was open for 7% -> 6% of each run, Pallas kernels for 0% -> 0%
where the time goes in v2:
time: 242 us
  waiting for transfers between devices  138 us (57%)
  blocking collectives  20.5 us (8%)
  starting transfers between devices  16.8 us (7%)
  Pallas kernels  15.5 us (6%)
  matrix products  14.1 us (6%)
  between operations  13.7 us (6%)
  local copies, waits for them, and re-layouts  12.8 us (5%)
  other arithmetic  10.1 us (4%)
    all_to_all x1, waiting for transfers between devices, shards(): lax.all_to_all(outgoing, 'group', split_axis=0, concat_axis=0, tiled=True)  54.8 us
    reduce_scatter x1, waiting for transfers between devices, shards(): lax.psum_scatter(jnp.dot(rows_piece, w_out, preferred_element_type=jnp.fl...  44 us
    all_gather x1, waiting for transfers between devices, shards(): lax.all_gather(normed, 'expert', axis=0, tiled=True)  24.7 us
    all_to_all x1, blocking collectives, shards(): lax.all_to_all(outgoing_rows, 'expert', split_axis=0, concat_axis=0, tile...  20.5 us
    pallas_call x1, Pallas kernels, paged_attention(): pl.pallas_call(attention_kernel, out_shape=jax.ShapeDtypeStruct((rows, lo...  15.5 us
    all_to_all x1, waiting for transfers between devices, shards(): lax.all_to_all(result, 'expert', split_axis=0, concat_axis=0, tiled=True)  14.6 us
    all_to_all x1, starting transfers between devices, shards(): lax.all_to_all(outgoing, 'group', split_axis=0, concat_axis=0, tiled=True)  12.1 us
    unnamed x21, local copies, waits for them, and re-layouts  5.03 us
  transfers between devices with their start and end apart: 4, of which 4 were waited for; matrix products, arithmetic and copies ran while one was open for 6% of the time, Pallas kernels for 0%

profile of v2, /device:TPU:1, one launch (start us, length us, event | category | flops | bytes accessed | tf_op | source)
XLA Modules:
  0.0 241.7 jit_solution(80330882153702316)
XLA Ops:
  6.5 0.9 add_select_fusion
  7.4 0.7 broadcast_compare_fusion
  8.4 0.6 select_reduce_fusion.1
  9.2 2.8 %gather_fusion = bf16[256,2,16,256]{3,2,1,0:T(8,128)(2,1)} fusion(bf16[128,2,16,256]{3,2,1,0:T(8,128)(2,1)S(1)} %copy-done, s32[1024]{0:T(1024)S(1)} %pad_clamp_fusion.1), kind=kCustom, calls=%fused_computation | custom fusion | bytes 8389632 | tf_op jit(solution)/shard_map/gather | solution.py:216
  12.0 12.1 %all-to-all-start = ((bf16[32,8,2,16,256]{4,3,2,1,0:T(8,128)(2,1)}), bf16[32,8,2,16,256]{4,3,2,1,0:T(8,128)(2,1)}, u32[]{:S(2)}, u32[]{:S(2)}) async-start(bf16[32,8,2,16,256]{4,3,2,1,0:T(8,128)(2,1)} %bitcast.59), calls=%async_computation | async-start | bytes 8388608 | tf_op jit(solution)/shard_map/all_to_all | solution.py:217
  24.3 0.8 fusion.17
  25.3 4.8 %copy.27 = bf16[2048,3,256]{0,2,1:T(8,128)(2,1)} copy(bf16[2048,3,256]{2,0,1:T(8,128)(2,1)} %param.18) | data formatting | bytes 6291456 | tf_op args[5]
  32.0 24.7 %all-gather.2.cloned.1.call-done = bf16[512,2048]{1,0:T(8,128)(2,1)} async-done(((bf16[64,2048]{1,0:T(8,128)(2,1)}), bf16[512,2048]{1,0:T(8,128)(2,1)}) %all-gather.2.cloned.1.call-update) | async-done | bytes 2097168 | tf_op jit(solution)/shard_map/all_gather | solution.py:197
  56.7 4.3 %fusion = f32[512,3,2,128]{0,3,2,1:T(8,128)S(1)} fusion(bf16[3,2,128,2048]{3,2,1,0:T(8,128)(2,1)} %bitcast.61, bf16[512,2048]{1,0:T(8,128)(2,1)} %all-gather.2.cloned.1.call-done), kind=kOutput, calls=%fused_computation.5 | convolution fusion | flops 1610612736 | bytes 6815744 | tf_op jit(solution)/shard_map/dot_general | solution.py:196
  61.9 54.8 %all-to-all-done = bf16[32,8,2,16,256]{4,3,2,1,0:T(8,128)(2,1)} async-done(((bf16[32,8,2,16,256]{4,3,2,1,0:T(8,128)(2,1)}), bf16[32,8,2,16,256]{4,3,2,1,0:T(8,128)(2,1)}, u32[]{:S(2)}, u32[]{:S(2)}) %all-to-all-start) | async-done | bytes 4194336 | tf_op jit(solution)/shard_map/all_to_all | solution.py:217
  116.7 15.5 %shard_map.127 = bf16[512,256]{1,0:T(8,128)(2,1)S(1)} custom-call(s32[128]{0:T(128)S(1)} %multiply_add_fusion.1.slots_ref, s32[1]{0:T(128)} %dynamic_slice.7.len_ref, bf16[512,256]{1,0:T(8,128)(2,1)S(1)} %copy.35.q_ref, bf16[512,256]{1,0:T(8,128)(2,1)S(1)} %copy.36.nk_ref, bf16[512,256]{1,0:T(8,128)(2,1)S(1)} %copy.37.nv_ref, ...), custom_call_target="tpu_custom_call" | custom-call | flops 1342177280 | bytes 5242880 | tf_op jit(solution)/shard_map/pallas_call | solution.py:142
  132.2 2.1 convolution_convert_fusion
  135.0 44.0 %reduce-scatter.2.cloned.1.call-done = bf16[64,2048]{1,0:T(8,128)(2,1)} async-done(((bf16[512,2048]{1,0:T(8,128)(2,1)}), bf16[64,2048]{1,0:T(8,128)(2,1)}) %reduce-scatter.2.cloned.1.call-update) | async-done | bytes 262160 | tf_op jit(solution)/shard_map/reduce_scatter | solution.py:233
  179.0 1.3 multiply_reduce_fusion.1
  180.3 1.4 convolution_convert_fusion.2
  181.7 20.5 %all_to_all.15 = bf16[8,32,2048]{2,1,0:T(8,128)(2,1)S(1)} all-to-all(bf16[8,32,2048]{2,1,0:T(8,128)(2,1)S(1)} %bitcast.60), channel_id=1, replica_groups=mesh['group'=32,'expert'=8] {'expert'}, dimensions={0} | all-to-all | bytes 2097152 | tf_op jit(solution)/shard_map/all_to_all | solution.py:262
  202.2 1.5 fusion.5
  203.7 4.7 %convolution_convert_fusion.1 = bf16[256,2048]{1,0:T(8,128)(2,1)} fusion(bf16[1,512,2048]{2,1,0:T(8,128)(2,1)} %param.23, bf16[256,2048]{1,0:T(8,128)(2,1)S(1)} %bitcast.64, bf16[1,2048,512]{2,1,0:T(8,128)(2,1)} %param.22, f32[256,512]{1,0:T(8,128)} %fusion.5), kind=kOutput, calls=%fused_computation.3 | convolution fusion | flops 1075052544 | bytes 6815744 | tf_op jit(solution)/shard_map/dot_general | solution.py:268
  208.4 4.6 %all-to-all-start.2 = ((bf16[8,32,2048]{2,1,0:T(8,128)(2,1)}), bf16[8,32,2048]{2,1,0:T(8,128)(2,1)S(1)}, u32[]{:S(2)}, u32[]{:S(2)}) async-start(bf16[8,32,2048]{2,1,0:T(8,128)(2,1)} %bitcast.62), calls=%async_computation.3 | async-start | bytes 2097152 | tf_op jit(solution)/shard_map/all_to_all | solution.py:272
  213.4 14.6 %all-to-all-done.2 = bf16[8,32,2048]{2,1,0:T(8,128)(2,1)S(1)} async-done(((bf16[8,32,2048]{2,1,0:T(8,128)(2,1)}), bf16[8,32,2048]{2,1,0:T(8,128)(2,1)S(1)}, u32[]{:S(2)}, u32[]{:S(2)}) %all-to-all-start.2) | async-done | bytes 1048608 | tf_op jit(solution)/shard_map/all_to_all | solution.py:272
  228.1 1.7 gather_fusion.1
  229.8 1.7 reshape.191
  231.5 1.5 multiply_reduce_fusion
  233.0 1.8 fusion.23
  (56 shorter events, 4.3 us)
Async XLA Ops:
  6.5 2.7 %copy-start = (bf16[128,2,16,256]{3,2,1,0:T(8,128)(2,1)S(1)}, bf16[128,2,16,256]{3,2,1,0:T(8,128)(2,1)}, u32[]{:S(2)}) copy-start(bf16[128,2,16,256]{3,2,1,0:T(8,128)(2,1)} %param.16) | copy-start | bytes 6291460
  12.0 12.2 %copy-start.1 = (bf16[64,2048]{1,0:T(8,128)(2,1)S(1)}, bf16[64,2048]{1,0:T(8,128)(2,1)}, u32[]{:S(2)}) copy-start(bf16[64,2048]{1,0:T(8,128)(2,1)} %param.13) | copy-start | bytes 786436
  12.0 12.4 %copy-start.3 = (f32[2048]{0:T(1024)S(1)}, f32[2048]{0:T(1024)}, u32[]{:S(2)}) copy-start(f32[2048]{0:T(1024)} %param.17) | copy-start | bytes 24580
  12.0 104.7 %all-to-all-start = ((bf16[32,8,2,16,256]{4,3,2,1,0:T(8,128)(2,1)}), bf16[32,8,2,16,256]{4,3,2,1,0:T(8,128)(2,1)}, u32[]{:S(2)}, u32[]{:S(2)}) async-start(bf16[32,8,2,16,256]{4,3,2,1,0:T(8,128)(2,1)} %bitcast.59), calls=%async_computation | async-start | bytes 8388608 | tf_op jit(solution)/shard_map/all_to_all | solution.py:217
  24.1 32.6 %all-gather.2.cloned.1.call-start = ((), (), s32[]{:S(2)}) async-start(), calls=%async_computation.4 | async-start | bytes 2359296 | tf_op jit(solution)/shard_map/all_gather | solution.py:197
  25.2 153.8 %reduce-scatter.2.cloned.1.call-start = ((), (), s32[]{:S(2)}) async-start(), calls=%async_computation.5 | async-start | bytes 2359296 | tf_op jit(solution)/shard_map/reduce_scatter | solution.py:233
  25.3 4.8 %copy-start.8 = (s32[32]{0:T(128)S(1)}, s32[32]{0:T(128)}, u32[]{:S(2)}) copy-start(s32[32]{0:T(128)} %param.14) | copy-start | bytes 388
  116.7 15.5 %copy-start.2 = (bf16[256,2048]{1,0:T(8,128)(2,1)S(1)}, bf16[256,2048]{1,0:T(8,128)(2,1)}, u32[]{:S(2)}) copy-start(bf16[256,2048]{1,0:T(8,128)(2,1)} %param.19) | copy-start | bytes 3145732
  132.2 2.1 copy-start.5
  134.3 46.0 %copy-start.4 = (f32[2048]{0:T(1024)S(1)}, f32[2048]{0:T(1024)}, u32[]{:S(2)}) copy-start(f32[2048]{0:T(1024)} %param.20) | copy-start | bytes 24580
  179.0 23.2 %copy-start.7 = (bf16[1,2048,512]{2,1,0:T(8,128)(2,1)S(1)}, bf16[1,2048,512]{2,1,0:T(8,128)(2,1)}, u32[]{:S(2)}) copy-start(bf16[1,2048,512]{2,1,0:T(8,128)(2,1)} %param.21) | copy-start | bytes 6291460
  208.4 4.9 %copy-start.6 = (f32[64,2]{0,1:T(2,128)S(1)}, f32[64,2]{0,1:T(2,128)}, u32[]{:S(2)}) copy-start(f32[64,2]{0,1:T(2,128)} %param.25) | copy-start | bytes 1540
  208.4 19.6 %all-to-all-start.2 = ((bf16[8,32,2048]{2,1,0:T(8,128)(2,1)}), bf16[8,32,2048]{2,1,0:T(8,128)(2,1)S(1)}, u32[]{:S(2)}, u32[]{:S(2)}) async-start(bf16[8,32,2048]{2,1,0:T(8,128)(2,1)} %bitcast.62), calls=%async_computation.3 | async-start | bytes 2097152 | tf_op jit(solution)/shard_map/all_to_all | solution.py:272
Sparse Core Ops, SparseCore 0:
  26.8 29.9 all-gather.1
  134.4 44.4 reduce-scatter.1

commit v3 on v2

--- a/solution.py
+++ b/solution.py
@@ -6,6 +6,7 @@
 from jax.sharding import PartitionSpec as P
 
 HEAD_DIM = 128
+EXPERT = ("ey", "ec")
 NBLK = 8
 CTX = 2048
 
@@ -181,7 +182,7 @@
     gate_weights,
 ):
     groups = lax.axis_size("group")
-    expert_lanes = lax.axis_size("expert")
+    expert_lanes = lax.axis_size(EXPERT)
     group_index = lax.axis_index("group")
     tok_rows = hidden_in.shape[0]
     model_width = hidden_in.shape[1]
@@ -194,7 +195,7 @@
     normed = norm_rows(hidden_in, attn_gain)
     projection = w_qkv.reshape(model_width, 3 * local_width)
     projected = jnp.dot(
-        lax.all_gather(normed, "expert", axis=0, tiled=True),
+        lax.all_gather(normed, EXPERT, axis=0, tiled=True),
         projection,
         preferred_element_type=jnp.float32,
     )
@@ -230,12 +231,14 @@
         block_len,
     )
     rows_piece = attended
-    head_sum = lax.psum_scatter(
-        jnp.dot(rows_piece, w_out, preferred_element_type=jnp.float32).astype(jnp.bfloat16),
-        "expert",
-        scatter_dimension=0,
-        tiled=True,
-    ).astype(jnp.float32)
+    head_parts = jnp.dot(rows_piece, w_out, preferred_element_type=jnp.float32).astype(jnp.bfloat16)
+    chips = lax.axis_size("ey")
+    cores = lax.axis_size("ec")
+    head_parts = head_parts.reshape(chips, cores, tok_rows, model_width)
+    head_parts = lax.all_to_all(head_parts, "ec", split_axis=1, concat_axis=1, tiled=True)
+    head_parts = jnp.sum(head_parts.astype(jnp.float32), axis=1).astype(jnp.bfloat16)
+    head_parts = lax.all_to_all(head_parts, "ey", split_axis=0, concat_axis=0, tiled=True)
+    head_sum = jnp.sum(head_parts.astype(jnp.float32), axis=0)
     residual = hidden_in.astype(jnp.float32) + head_sum
     moe_in = norm_rows(residual, moe_gain)
     route_count = expert_ids.shape[1]
@@ -259,7 +262,7 @@
         .astype(jnp.bfloat16)
         .reshape(expert_lanes, capacity, model_width)
     )
-    rows_piece = lax.all_to_all(outgoing_rows, "expert", split_axis=0, concat_axis=0, tiled=True)
+    rows_piece = lax.all_to_all(outgoing_rows, EXPERT, split_axis=0, concat_axis=0, tiled=True)
     flat_rows = rows_piece.reshape(-1, rows_piece.shape[-1])
     gate_part = jnp.dot(flat_rows, w_gate[0], preferred_element_type=jnp.float32)
     up_part = jnp.dot(flat_rows, w_up[0], preferred_element_type=jnp.float32)
@@ -269,7 +272,7 @@
         .astype(jnp.bfloat16)
         .reshape(rows_piece.shape)
     )
-    returned = lax.all_to_all(result, "expert", split_axis=0, concat_axis=0, tiled=True)
+    returned = lax.all_to_all(result, EXPERT, split_axis=0, concat_axis=0, tiled=True)
     picked = returned.reshape(expert_lanes * capacity, model_width)[
         flat_expert * capacity + slot_index
     ]
@@ -282,21 +285,27 @@
 
 
 def solution(mesh):
+    lanes = mesh.shape["expert"]
+    cores = 2 if lanes % 2 == 0 else 1
+    split = jax.sharding.Mesh(
+        mesh.devices.reshape(mesh.shape["group"], lanes // cores, cores), ("group",) + EXPERT
+    )
+    rows = ("group",) + EXPERT
     placed = (
-        P(("group", "expert"), None),
+        P(rows, None),
         P(),
         P(),
-        P("group", None, None, "expert"),
+        P("group", None, None, EXPERT),
         P(),
-        P(None, None, "expert"),
-        P("expert", None),
+        P(None, None, EXPERT),
+        P(EXPERT, None),
         P(),
-        P("expert", None, None),
-        P("expert", None, None),
-        P("expert", None, None),
-        P(("group", "expert"), None),
-        P(("group", "expert"), None),
+        P(EXPERT, None, None),
+        P(EXPERT, None, None),
+        P(EXPERT, None, None),
+        P(rows, None),
+        P(rows, None),
     )
     return jax.shard_map(
-        shards, mesh=mesh, in_specs=placed, out_specs=P(("group", "expert"), None), check_vma=False
-    )
+        shards, mesh=split, in_specs=placed, out_specs=P(rows, None), check_vma=False
+    )

time: 242 us -> 235 us (0.971)
  the two profiles are of different devices: /device:TPU:1 before, /device:TPU:2 now
where the time goes in v3:
time: 235 us
  waiting for transfers between devices  112 us (48%)
  Pallas kernels  25.7 us (11%)
  blocking collectives  24.8 us (11%)
  starting transfers between devices  20.3 us (9%)
  local copies, waits for them, and re-layouts  14.1 us (6%)
  between operations  13.7 us (6%)
  other arithmetic  12.8 us (5%)
  matrix products  11.8 us (5%)
    all_to_all x1, waiting for transfers between devices, shards(): lax.all_to_all(outgoing, 'group', split_axis=0, concat_axis=0, tiled=True)  57.7 us
    pallas_call x1, Pallas kernels, paged_attention(): pl.pallas_call(attention_kernel, out_shape=jax.ShapeDtypeStruct((rows, lo...  25.7 us
    all_gather x1, waiting for transfers between devices, shards(): lax.all_gather(normed, EXPERT, axis=0, tiled=True)  23.9 us
    all_to_all x1, blocking collectives, shards(): lax.all_to_all(outgoing_rows, EXPERT, split_axis=0, concat_axis=0, tiled=...  18.5 us
    all_to_all x1, waiting for transfers between devices, shards(): lax.all_to_all(result, EXPERT, split_axis=0, concat_axis=0, tiled=True)  15.3 us
    all_to_all x1, waiting for transfers between devices, shards(): lax.all_to_all(head_parts, 'ey', split_axis=0, concat_axis=0, tiled=True)  14.7 us
    all_to_all x1, starting transfers between devices, shards(): lax.all_to_all(outgoing, 'group', split_axis=0, concat_axis=0, tiled=True)  11.8 us
    all_to_all x1, blocking collectives, shards(): lax.all_to_all(head_parts, 'ec', split_axis=1, concat_axis=1, tiled=True)  6.31 us
  transfers between devices with their start and end apart: 4, of which 4 were waited for; matrix products, arithmetic and copies ran while one was open for 6% of the time, Pallas kernels for 0%

profile of v3, /device:TPU:2, one launch (start us, length us, event | category | flops | bytes accessed | tf_op | source)
XLA Modules:
  0.0 234.8 jit_solution(13092525467724855403)
XLA Ops:
  6.5 0.9 add_select_fusion
  7.4 0.7 broadcast_compare_fusion
  9.2 2.8 %gather_fusion = bf16[256,2,16,256]{3,2,1,0:T(8,128)(2,1)} fusion(bf16[128,2,16,256]{3,2,1,0:T(8,128)(2,1)S(1)} %copy-done, s32[1024]{0:T(1024)S(1)} %pad_clamp_fusion.1), kind=kCustom, calls=%fused_computation | custom fusion | bytes 8389632 | tf_op jit(solution)/shard_map/gather | solution.py:217
  12.0 11.8 %all-to-all-start = ((bf16[32,8,2,16,256]{4,3,2,1,0:T(8,128)(2,1)}), bf16[32,8,2,16,256]{4,3,2,1,0:T(8,128)(2,1)}, u32[]{:S(2)}, u32[]{:S(2)}) async-start(bf16[32,8,2,16,256]{4,3,2,1,0:T(8,128)(2,1)} %bitcast.60), calls=%async_computation | async-start | bytes 8388608 | tf_op jit(solution)/shard_map/all_to_all | solution.py:218
  24.0 0.8 fusion.17
  24.9 4.8 %copy.35 = bf16[2048,3,256]{0,2,1:T(8,128)(2,1)} copy(bf16[2048,3,256]{2,0,1:T(8,128)(2,1)} %param.18) | data formatting | bytes 6291456 | tf_op args[5]
  31.6 23.9 %all-gather.2.cloned.1.call-done = bf16[512,2048]{1,0:T(8,128)(2,1)} async-done(((bf16[64,2048]{1,0:T(8,128)(2,1)}), bf16[512,2048]{1,0:T(8,128)(2,1)}) %all-gather.2.cloned.1.call-update) | async-done | bytes 2097168 | tf_op jit(solution)/shard_map/all_gather | solution.py:198
  55.5 4.3 %fusion = f32[512,3,2,128]{0,3,2,1:T(8,128)S(1)} fusion(bf16[3,2,128,2048]{3,2,1,0:T(8,128)(2,1)} %bitcast.63, bf16[512,2048]{1,0:T(8,128)(2,1)} %all-gather.2.cloned.1.call-done), kind=kOutput, calls=%fused_computation.5 | convolution fusion | flops 1610612736 | bytes 6815744 | tf_op jit(solution)/shard_map/dot_general | solution.py:197
  60.6 57.7 %all-to-all-done = bf16[32,8,2,16,256]{4,3,2,1,0:T(8,128)(2,1)} async-done(((bf16[32,8,2,16,256]{4,3,2,1,0:T(8,128)(2,1)}), bf16[32,8,2,16,256]{4,3,2,1,0:T(8,128)(2,1)}, u32[]{:S(2)}, u32[]{:S(2)}) %all-to-all-start) | async-done | bytes 4194336 | tf_op jit(solution)/shard_map/all_to_all | solution.py:218
  118.3 25.7 %shard_map.127 = bf16[512,256]{1,0:T(8,128)(2,1)S(1)} custom-call(s32[128]{0:T(128)S(1)} %multiply_add_fusion.1.slots_ref, s32[1]{0:T(128)} %dynamic_slice.7.len_ref, bf16[512,256]{1,0:T(8,128)(2,1)S(1)} %copy.44.q_ref, bf16[512,256]{1,0:T(8,128)(2,1)S(1)} %copy.45.nk_ref, bf16[512,256]{1,0:T(8,128)(2,1)S(1)} %copy.46.nv_ref, ...), custom_call_target="tpu_custom_call" | custom-call | flops 1342177280 | bytes 5242880 | tf_op jit(solution)/shard_map/pallas_call | solution.py:143
  144.0 0.7 convolution_convert_fusion
  145.0 6.3 %all_to_all.25 = bf16[4,2,64,2048]{3,2,0,1:T(8,128)(2,1)} all-to-all(bf16[4,2,64,2048]{3,2,0,1:T(8,128)(2,1)S(1)} %copy.39), channel_id=1, replica_groups=mesh['group'=32,'ey'=4,'ec'=2] {'ec'}, dimensions={1} | all-to-all | bytes 4194304 | tf_op jit(solution)/shard_map/all_to_all | solution.py:238
  151.3 3.3 %reduce_sum.92 = bf16[4,64,2048]{2,1,0:T(8,128)(2,1)} reduce(bf16[4,2,64,2048]{3,2,0,1:T(8,128)(2,1)} %all_to_all.25, bf16[]{:T(256)} %constant.78.clone.1), dimensions={1}, to_apply=%region_4.5 | reduce | flops 524288 | bytes 3145730 | tf_op jit(solution)/shard_map/reduce_sum | solution.py:239
  154.6 4.6 %all-to-all-start.2 = ((bf16[4,64,2048]{2,1,0:T(8,128)(2,1)}), bf16[4,64,2048]{2,1,0:T(8,128)(2,1)S(1)}, u32[]{:S(2)}, u32[]{:S(2)}) async-start(bf16[4,64,2048]{2,1,0:T(8,128)(2,1)} %reduce_sum.92), calls=%async_computation.2 | async-start | bytes 2097152 | tf_op jit(solution)/shard_map/all_to_all | solution.py:240
  159.9 14.7 %all-to-all-done.2 = bf16[4,64,2048]{2,1,0:T(8,128)(2,1)S(1)} async-done(((bf16[4,64,2048]{2,1,0:T(8,128)(2,1)}), bf16[4,64,2048]{2,1,0:T(8,128)(2,1)S(1)}, u32[]{:S(2)}, u32[]{:S(2)}) %all-to-all-start.2) | async-done | bytes 1048608 | tf_op jit(solution)/shard_map/all_to_all | solution.py:240
  175.5 18.5 %all_to_all.26 = bf16[8,32,2048]{2,1,0:T(8,128)(2,1)S(1)} all-to-all(bf16[8,32,2048]{2,1,0:T(8,128)(2,1)S(1)} %bitcast.62), channel_id=1, replica_groups=mesh['group'=32,'ey'=4,'ec'=2] {'ey','ec'}, dimensions={0} | all-to-all | bytes 2097152 | tf_op jit(solution)/shard_map/all_to_all | solution.py:265
  194.0 1.5 fusion.5
  195.5 4.7 %convolution_convert_fusion.1 = bf16[256,2048]{1,0:T(8,128)(2,1)} fusion(bf16[1,512,2048]{2,1,0:T(8,128)(2,1)} %param.23, bf16[256,2048]{1,0:T(8,128)(2,1)S(1)} %bitcast.66, bf16[1,2048,512]{2,1,0:T(8,128)(2,1)} %param.22, f32[256,512]{1,0:T(8,128)} %fusion.5), kind=kOutput, calls=%fused_computation.3 | convolution fusion | flops 1075052544 | bytes 6815744 | tf_op jit(solution)/shard_map/dot_general | solution.py:271
  200.3 3.9 %all-to-all-start.4 = ((bf16[8,32,2048]{2,1,0:T(8,128)(2,1)}), bf16[8,32,2048]{2,1,0:T(8,128)(2,1)S(1)}, u32[]{:S(2)}, u32[]{:S(2)}) async-start(bf16[8,32,2048]{2,1,0:T(8,128)(2,1)} %bitcast.64), calls=%async_computation.4 | async-start | bytes 2097152 | tf_op jit(solution)/shard_map/all_to_all | solution.py:275
  204.5 15.3 %all-to-all-done.4 = bf16[8,32,2048]{2,1,0:T(8,128)(2,1)S(1)} async-done(((bf16[8,32,2048]{2,1,0:T(8,128)(2,1)}), bf16[8,32,2048]{2,1,0:T(8,128)(2,1)S(1)}, u32[]{:S(2)}, u32[]{:S(2)}) %all-to-all-start.4) | async-done | bytes 1048608 | tf_op jit(solution)/shard_map/all_to_all | solution.py:275
  219.8 1.7 gather_fusion.1
  221.5 2.7 %reshape.195 = f32[64,2,2048]{2,1,0:T(2,128)} reshape(bf16[128,2048]{1,0:T(8,128)(2,1)} %gather_fusion.1) | data formatting | bytes 1572864 | tf_op jit(solution)/shard_map/convert_element_type | solution.py:280
  224.3 2.8 %multiply_reduce_fusion = f32[64,2048]{1,0:T(8,128)S(1)} fusion(f32[64,2,2048]{2,1,0:T(2,128)} %reshape.195, f32[64,2]{1,0:T(8,128)S(1)} %copy.42), kind=kLoop, calls=%fused_computation.15 | loop fusion | flops 393216 | bytes 1573376 | tf_op jit(solution)/shard_map/reduce_sum | solution.py:279
  227.1 0.9 fusion.26
  (63 shorter events, 6.0 us)
Async XLA Ops:
  6.5 2.7 %copy-start = (bf16[128,2,16,256]{3,2,1,0:T(8,128)(2,1)S(1)}, bf16[128,2,16,256]{3,2,1,0:T(8,128)(2,1)}, u32[]{:S(2)}) copy-start(bf16[128,2,16,256]{3,2,1,0:T(8,128)(2,1)} %param.16) | copy-start | bytes 6291460
  12.0 11.9 %copy-start.3 = (bf16[64,2048]{1,0:T(8,128)(2,1)S(1)}, bf16[64,2048]{1,0:T(8,128)(2,1)}, u32[]{:S(2)}) copy-start(bf16[64,2048]{1,0:T(8,128)(2,1)} %param.13) | copy-start | bytes 786436
  12.0 12.0 %copy-start.5 = (f32[2048]{0:T(1024)S(1)}, f32[2048]{0:T(1024)}, u32[]{:S(2)}) copy-start(f32[2048]{0:T(1024)} %param.17) | copy-start | bytes 24580
  12.0 106.3 %all-to-all-start = ((bf16[32,8,2,16,256]{4,3,2,1,0:T(8,128)(2,1)}), bf16[32,8,2,16,256]{4,3,2,1,0:T(8,128)(2,1)}, u32[]{:S(2)}, u32[]{:S(2)}) async-start(bf16[32,8,2,16,256]{4,3,2,1,0:T(8,128)(2,1)} %bitcast.60), calls=%async_computation | async-start | bytes 8388608 | tf_op jit(solution)/shard_map/all_to_all | solution.py:218
  23.8 31.7 %all-gather.2.cloned.1.call-start = ((), (), s32[]{:S(2)}) async-start(), calls=%async_computation.5 | async-start | bytes 2359296 | tf_op jit(solution)/shard_map/all_gather | solution.py:198
  24.9 4.8 %copy-start.10 = (s32[32]{0:T(128)S(1)}, s32[32]{0:T(128)}, u32[]{:S(2)}) copy-start(s32[32]{0:T(128)} %param.14) | copy-start | bytes 388
  118.3 25.7 %copy-start.4 = (bf16[256,2048]{1,0:T(8,128)(2,1)S(1)}, bf16[256,2048]{1,0:T(8,128)(2,1)}, u32[]{:S(2)}) copy-start(bf16[256,2048]{1,0:T(8,128)(2,1)} %param.19) | copy-start | bytes 3145732
  151.3 7.9 %copy-start.7 = (s32[64,2]{0,1:T(2,128)S(1)}, s32[64,2]{0,1:T(2,128)}, u32[]{:S(2)}) copy-start(s32[64,2]{0,1:T(2,128)} %param.24) | copy-start | bytes 1540
  154.6 20.4 %copy-start.6 = (f32[2048]{0:T(1024)S(1)}, f32[2048]{0:T(1024)}, u32[]{:S(2)}) copy-start(f32[2048]{0:T(1024)} %param.20) | copy-start | bytes 24580
  154.6 20.0 %all-to-all-start.2 = ((bf16[4,64,2048]{2,1,0:T(8,128)(2,1)}), bf16[4,64,2048]{2,1,0:T(8,128)(2,1)S(1)}, u32[]{:S(2)}, u32[]{:S(2)}) async-start(bf16[4,64,2048]{2,1,0:T(8,128)(2,1)} %reduce_sum.92), calls=%async_computation.2 | async-start | bytes 2097152 | tf_op jit(solution)/shard_map/all_to_all | solution.py:240
  174.8 19.2 %copy-start.1 = (f32[64,2048]{1,0:T(8,128)}, f32[64,2048]{1,0:T(8,128)S(1)}, u32[]{:S(2)}) copy-start(f32[64,2048]{1,0:T(8,128)S(1)} %convert_reduce_fusion) | copy-start | bytes 1572868
  175.0 19.1 %copy-start.9 = (bf16[1,2048,512]{2,1,0:T(8,128)(2,1)S(1)}, bf16[1,2048,512]{2,1,0:T(8,128)(2,1)}, u32[]{:S(2)}) copy-start(bf16[1,2048,512]{2,1,0:T(8,128)(2,1)} %param.21) | copy-start | bytes 6291460
  200.3 4.1 %copy-start.8 = (f32[64,2]{0,1:T(2,128)S(1)}, f32[64,2]{0,1:T(2,128)}, u32[]{:S(2)}) copy-start(f32[64,2]{0,1:T(2,128)} %param.25) | copy-start | bytes 1540
  200.3 19.6 %all-to-all-start.4 = ((bf16[8,32,2048]{2,1,0:T(8,128)(2,1)}), bf16[8,32,2048]{2,1,0:T(8,128)(2,1)S(1)}, u32[]{:S(2)}, u32[]{:S(2)}) async-start(bf16[8,32,2048]{2,1,0:T(8,128)(2,1)} %bitcast.64), calls=%async_computation.4 | async-start | bytes 2097152 | tf_op jit(solution)/shard_map/all_to_all | solution.py:275
  221.5 5.5 %copy-start.2 = (f32[64,2048]{1,0:T(8,128)S(1)}, f32[64,2048]{1,0:T(8,128)}, u32[]{:S(2)}) copy-start(f32[64,2048]{1,0:T(8,128)} %copy-done.1) | copy-start | bytes 1572868
Sparse Core Ops, SparseCore 0:
  26.5 28.9 all-gather.1

commit v4 on v3

--- a/solution.py
+++ b/solution.py
@@ -1,3 +1,5 @@
+import functools
+
 import jax
 import jax.numpy as jnp
 from jax import lax
@@ -7,6 +9,8 @@
 
 HEAD_DIM = 128
 EXPERT = ("ey", "ec")
+MESH_AXES = ("group", "ey", "ec")
+MESH_IDS = pl.DeviceIdType.MESH
 NBLK = 8
 CTX = 2048
 
@@ -78,6 +82,65 @@
         return attend_block(running, queries, key_block, value_block, key_valid)
 
     return lax.fori_loop(0, turn_count, step_once, softmax_state)
+
+
+def exchange_kernel(axes, x_ref, o_ref, send_sems, recv_sems, own_sem):
+    sizes = [lax.axis_size(a) for a in axes]
+    count = 1
+    for size in sizes:
+        count *= size
+    me = 0
+    for a, size in zip(axes, sizes):
+        me = me * size + lax.axis_index(a)
+
+    def device_of(peer):
+        coords = {}
+        rest = peer
+        for a, size in reversed(list(zip(axes, sizes))):
+            coords[a] = rest % size
+            rest = rest // size
+        return tuple(coords.get(a, lax.axis_index(a)) for a in MESH_AXES)
+
+    barrier = pltpu.get_barrier_semaphore()
+    for k in range(1, count):
+        pl.semaphore_signal(
+            barrier, inc=1, device_id=device_of((me + k) % count), device_id_type=MESH_IDS
+        )
+    pl.semaphore_wait(barrier, count - 1)
+    own = pltpu.make_async_copy(x_ref.at[me], o_ref.at[me], own_sem)
+    own.start()
+    copies = []
+    for k in range(1, count):
+        peer = (me + k) % count
+        copy = pltpu.make_async_remote_copy(
+            src_ref=x_ref.at[peer],
+            dst_ref=o_ref.at[me],
+            send_sem=send_sems.at[k],
+            recv_sem=recv_sems.at[k],
+            device_id=device_of(peer),
+            device_id_type=MESH_IDS,
+        )
+        copy.start()
+        copies.append(copy)
+    own.wait()
+    for copy in copies:
+        copy.wait()
+
+
+def exchange(x, axes, ident):
+    count = x.shape[0]
+    return pl.pallas_call(
+        functools.partial(exchange_kernel, axes),
+        out_shape=jax.ShapeDtypeStruct(x.shape, x.dtype),
+        in_specs=[pl.BlockSpec(memory_space=pl.ANY)],
+        out_specs=pl.BlockSpec(memory_space=pl.ANY),
+        scratch_shapes=[
+            pltpu.SemaphoreType.DMA((count,)),
+            pltpu.SemaphoreType.DMA((count,)),
+            pltpu.SemaphoreType.DMA(()),
+        ],
+        compiler_params=pltpu.CompilerParams(collective_id=ident, has_side_effects=True),
+    )(x)
 
 
 def attention_kernel(
@@ -262,7 +325,7 @@
         .astype(jnp.bfloat16)
         .reshape(expert_lanes, capacity, model_width)
     )
-    rows_piece = lax.all_to_all(outgoing_rows, EXPERT, split_axis=0, concat_axis=0, tiled=True)
+    rows_piece = exchange(outgoing_rows, EXPERT, 0)
     flat_rows = rows_piece.reshape(-1, rows_piece.shape[-1])
     gate_part = jnp.dot(flat_rows, w_gate[0], preferred_element_type=jnp.float32)
     up_part = jnp.dot(flat_rows, w_up[0], preferred_element_type=jnp.float32)
@@ -272,7 +335,7 @@
         .astype(jnp.bfloat16)
         .reshape(rows_piece.shape)
     )
-    returned = lax.all_to_all(result, EXPERT, split_axis=0, concat_axis=0, tiled=True)
+    returned = exchange(result, EXPERT, 1)
     picked = returned.reshape(expert_lanes * capacity, model_width)[
         flat_expert * capacity + slot_index
     ]

time: 235 us -> 236 us (level)
  the two profiles are of different devices: /device:TPU:2 before, /device:TPU:1 now
where the time goes in v4:
time: 236 us; the launch traced here: 235 us
  waiting for transfers between devices  93.3 us (40%)
  Pallas kernels  58.2 us (25%)
  starting transfers between devices  16.7 us (7%)
  local copies, waits for them, and re-layouts  14.1 us (6%)
  other arithmetic  14.1 us (6%)
  matrix products  14.1 us (6%)
  between operations  13.7 us (6%)
  blocking collectives  11.3 us (5%)
    all_to_all x1, waiting for transfers between devices, shards(): lax.all_to_all(outgoing, 'group', split_axis=0, concat_axis=0, tiled=True)  54.8 us
    pallas_call x2, Pallas kernels, exchange(): pl.pallas_call(functools.partial(exchange_kernel, axes), out_shape=jax.Sh...  32.5 us
    pallas_call x1, Pallas kernels, paged_attention(): pl.pallas_call(attention_kernel, out_shape=jax.ShapeDtypeStruct((rows, lo...  25.7 us
    all_gather x1, waiting for transfers between devices, shards(): lax.all_gather(normed, EXPERT, axis=0, tiled=True)  24 us
    all_to_all x1, waiting for transfers between devices, shards(): lax.all_to_all(head_parts, 'ey', split_axis=0, concat_axis=0, tiled=True)  14.4 us
    all_to_all x1, starting transfers between devices, shards(): lax.all_to_all(outgoing, 'group', split_axis=0, concat_axis=0, tiled=True)  12.1 us
    all_to_all x1, blocking collectives, shards(): lax.all_to_all(head_parts, 'ec', split_axis=1, concat_axis=1, tiled=True)  11.3 us
    unnamed x19, local copies, waits for them, and re-layouts  5.03 us
  transfers between devices with their start and end apart: 3, of which 3 were waited for; matrix products, arithmetic and copies ran while one was open for 6% of the time, Pallas kernels for 0%

profile of v4, /device:TPU:1, one launch (start us, length us, event | category | flops | bytes accessed | tf_op | source)
XLA Modules:
  0.0 235.5 jit_solution(2860691304009611355)
XLA Ops:
  6.5 0.9 add_select_fusion
  7.4 0.7 broadcast_compare_fusion
  9.2 2.8 %gather_fusion = bf16[256,2,16,256]{3,2,1,0:T(8,128)(2,1)} fusion(bf16[128,2,16,256]{3,2,1,0:T(8,128)(2,1)S(1)} %copy-done, s32[1024]{0:T(1024)S(1)} %pad_clamp_fusion.1), kind=kCustom, calls=%fused_computation | custom fusion | bytes 8389632 | tf_op jit(solution)/shard_map/gather | solution.py:280
  12.0 12.1 %all-to-all-start = ((bf16[32,8,2,16,256]{4,3,2,1,0:T(8,128)(2,1)}), bf16[32,8,2,16,256]{4,3,2,1,0:T(8,128)(2,1)}, u32[]{:S(2)}, u32[]{:S(2)}) async-start(bf16[32,8,2,16,256]{4,3,2,1,0:T(8,128)(2,1)} %bitcast.60), calls=%async_computation | async-start | bytes 8388608 | tf_op jit(solution)/shard_map/all_to_all | solution.py:281
  24.3 0.8 fusion.17
  25.2 4.8 %copy.35 = bf16[2048,3,256]{0,2,1:T(8,128)(2,1)} copy(bf16[2048,3,256]{2,0,1:T(8,128)(2,1)} %param.18) | data formatting | bytes 6291456 | tf_op args[5]
  32.7 24.0 %all-gather.2.cloned.1.call-done = bf16[512,2048]{1,0:T(8,128)(2,1)} async-done(((bf16[64,2048]{1,0:T(8,128)(2,1)}), bf16[512,2048]{1,0:T(8,128)(2,1)}) %all-gather.2.cloned.1.call-update) | async-done | bytes 2097168 | tf_op jit(solution)/shard_map/all_gather | solution.py:261
  56.7 4.3 %fusion = f32[512,3,2,128]{0,3,2,1:T(8,128)S(1)} fusion(bf16[3,2,128,2048]{3,2,1,0:T(8,128)(2,1)} %bitcast.63, bf16[512,2048]{1,0:T(8,128)(2,1)} %all-gather.2.cloned.1.call-done), kind=kOutput, calls=%fused_computation.5 | convolution fusion | flops 1610612736 | bytes 6815744 | tf_op jit(solution)/shard_map/dot_general | solution.py:260
  61.9 54.8 %all-to-all-done = bf16[32,8,2,16,256]{4,3,2,1,0:T(8,128)(2,1)} async-done(((bf16[32,8,2,16,256]{4,3,2,1,0:T(8,128)(2,1)}), bf16[32,8,2,16,256]{4,3,2,1,0:T(8,128)(2,1)}, u32[]{:S(2)}, u32[]{:S(2)}) %all-to-all-start) | async-done | bytes 4194336 | tf_op jit(solution)/shard_map/all_to_all | solution.py:281
  116.7 25.7 %shard_map.127 = bf16[512,256]{1,0:T(8,128)(2,1)S(1)} custom-call(s32[128]{0:T(128)S(1)} %multiply_add_fusion.1.slots_ref, s32[1]{0:T(128)} %dynamic_slice.7.len_ref, bf16[512,256]{1,0:T(8,128)(2,1)S(1)} %copy.44.q_ref, bf16[512,256]{1,0:T(8,128)(2,1)S(1)} %copy.45.nk_ref, bf16[512,256]{1,0:T(8,128)(2,1)S(1)} %copy.46.nv_ref, ...), custom_call_target="tpu_custom_call" | custom-call | flops 1342177280 | bytes 5242880 | tf_op jit(solution)/shard_map/pallas_call | solution.py:206
  143.3 11.3 %all_to_all.15 = bf16[4,2,64,2048]{3,2,0,1:T(8,128)(2,1)} all-to-all(bf16[4,2,64,2048]{3,2,0,1:T(8,128)(2,1)S(1)} %copy.39), channel_id=1, replica_groups=mesh['group'=32,'ey'=4,'ec'=2] {'ec'}, dimensions={1} | all-to-all | bytes 4194304 | tf_op jit(solution)/shard_map/all_to_all | solution.py:301
  154.7 3.3 %reduce_sum.92 = bf16[4,64,2048]{2,1,0:T(8,128)(2,1)} reduce(bf16[4,2,64,2048]{3,2,0,1:T(8,128)(2,1)} %all_to_all.15, bf16[]{:T(256)} %constant.78.clone.1), dimensions={1}, to_apply=%region_4.5 | reduce | flops 524288 | bytes 3145730 | tf_op jit(solution)/shard_map/reduce_sum | solution.py:302
  158.0 4.5 %all-to-all-start.2 = ((bf16[4,64,2048]{2,1,0:T(8,128)(2,1)}), bf16[4,64,2048]{2,1,0:T(8,128)(2,1)}, u32[]{:S(2)}, u32[]{:S(2)}) async-start(bf16[4,64,2048]{2,1,0:T(8,128)(2,1)} %reduce_sum.92), calls=%async_computation.2 | async-start | bytes 2097152 | tf_op jit(solution)/shard_map/all_to_all | solution.py:303
  162.8 14.4 %all-to-all-done.2 = bf16[4,64,2048]{2,1,0:T(8,128)(2,1)} async-done(((bf16[4,64,2048]{2,1,0:T(8,128)(2,1)}), bf16[4,64,2048]{2,1,0:T(8,128)(2,1)}, u32[]{:S(2)}, u32[]{:S(2)}) %all-to-all-start.2) | async-done | bytes 1048608 | tf_op jit(solution)/shard_map/all_to_all | solution.py:303
  177.3 1.4 convert_reduce_fusion
  178.9 1.5 convolution_convert_fusion.2
  180.4 16.9 %shard_map.128 = bf16[8,32,2048]{2,1,0:T(8,128)(2,1)} custom-call(bf16[8,32,2048]{2,1,0:T(8,128)(2,1)} %bitcast.62), custom_call_target="tpu_custom_call" | custom-call | tf_op jit(solution)/shard_map/pallas_call | solution.py:132
  197.3 2.6 %fusion.5 = f32[256,512]{1,0:T(8,128)S(1)} fusion(bf16[256,2048]{1,0:T(8,128)(2,1)} %bitcast.64, bf16[1,2048,512]{2,1,0:T(8,128)(2,1)} %param.21), kind=kOutput, calls=%fused_computation.10 | convolution fusion | flops 536870912 | bytes 3670016 | tf_op jit(solution)/shard_map/dot_general | solution.py:330
  200.0 4.9 %convolution_convert_fusion.1 = bf16[256,2048]{1,0:T(8,128)(2,1)} fusion(bf16[1,512,2048]{2,1,0:T(8,128)(2,1)} %param.23, bf16[256,2048]{1,0:T(8,128)(2,1)} %bitcast.65, bf16[1,2048,512]{2,1,0:T(8,128)(2,1)} %param.22, f32[256,512]{1,0:T(8,128)S(1)} %fusion.5), kind=kOutput, calls=%fused_computation.3 | convolution fusion | flops 1075052544 | bytes 6815744 | tf_op jit(solution)/shard_map/dot_general | solution.py:334
  204.9 15.6 %shard_map.129 = bf16[8,32,2048]{2,1,0:T(8,128)(2,1)} custom-call(bf16[8,32,2048]{2,1,0:T(8,128)(2,1)} %bitcast.66), custom_call_target="tpu_custom_call" | custom-call | tf_op jit(solution)/shard_map/pallas_call | solution.py:132
  220.5 2.8 %gather_fusion.1 = bf16[128,2048]{1,0:T(8,128)(2,1)S(1)} fusion(bf16[256,2048]{1,0:T(8,128)(2,1)} %bitcast.59, s32[1024]{0:T(1024)S(1)} %pad_clamp_fusion), kind=kCustom, calls=%fused_computation.1 | custom fusion | bytes 1049088 | tf_op jit(solution)/shard_map/gather | solution.py:339
  223.3 1.6 reshape.195
  225.0 2.8 %multiply_reduce_fusion = f32[64,2048]{1,0:T(8,128)S(1)} fusion(f32[64,2,2048]{2,1,0:T(2,128)} %reshape.195, f32[64,2]{1,0:T(8,128)S(1)} %copy.42), kind=kLoop, calls=%fused_computation.15 | loop fusion | flops 393216 | bytes 1573376 | tf_op jit(solution)/shard_map/reduce_sum | solution.py:342
  227.8 0.9 fusion.26
  (56 shorter events, 6.0 us)
Async XLA Ops:
  6.5 2.7 %copy-start = (bf16[128,2,16,256]{3,2,1,0:T(8,128)(2,1)S(1)}, bf16[128,2,16,256]{3,2,1,0:T(8,128)(2,1)}, u32[]{:S(2)}) copy-start(bf16[128,2,16,256]{3,2,1,0:T(8,128)(2,1)} %param.16) | copy-start | bytes 6291460
  12.0 12.2 %copy-start.1 = (bf16[64,2048]{1,0:T(8,128)(2,1)S(1)}, bf16[64,2048]{1,0:T(8,128)(2,1)}, u32[]{:S(2)}) copy-start(bf16[64,2048]{1,0:T(8,128)(2,1)} %param.13) | copy-start | bytes 786436
  12.0 12.4 %copy-start.3 = (f32[2048]{0:T(1024)S(1)}, f32[2048]{0:T(1024)}, u32[]{:S(2)}) copy-start(f32[2048]{0:T(1024)} %param.17) | copy-start | bytes 24580
  12.0 104.7 %all-to-all-start = ((bf16[32,8,2,16,256]{4,3,2,1,0:T(8,128)(2,1)}), bf16[32,8,2,16,256]{4,3,2,1,0:T(8,128)(2,1)}, u32[]{:S(2)}, u32[]{:S(2)}) async-start(bf16[32,8,2,16,256]{4,3,2,1,0:T(8,128)(2,1)} %bitcast.60), calls=%async_computation | async-start | bytes 8388608 | tf_op jit(solution)/shard_map/all_to_all | solution.py:281
  24.1 32.6 %all-gather.2.cloned.1.call-start = ((), (), s32[]{:S(2)}) async-start(), calls=%async_computation.3 | async-start | bytes 2359296 | tf_op jit(solution)/shard_map/all_gather | solution.py:261
  25.2 4.8 %copy-start.5 = (s32[64,2]{0,1:T(2,128)S(1)}, s32[64,2]{0,1:T(2,128)}, u32[]{:S(2)}) copy-start(s32[64,2]{0,1:T(2,128)} %param.24) | copy-start | bytes 1540
  25.2 5.3 %copy-start.6 = (f32[64,2]{0,1:T(2,128)S(1)}, f32[64,2]{0,1:T(2,128)}, u32[]{:S(2)}) copy-start(f32[64,2]{0,1:T(2,128)} %param.25) | copy-start | bytes 1540
  25.2 5.4 %copy-start.7 = (s32[32]{0:T(128)S(1)}, s32[32]{0:T(128)}, u32[]{:S(2)}) copy-start(s32[32]{0:T(128)} %param.14) | copy-start | bytes 388
  116.7 25.7 %copy-start.2 = (bf16[256,2048]{1,0:T(8,128)(2,1)S(1)}, bf16[256,2048]{1,0:T(8,128)(2,1)}, u32[]{:S(2)}) copy-start(bf16[256,2048]{1,0:T(8,128)(2,1)} %param.19) | copy-start | bytes 3145732
  158.0 20.9 %copy-start.4 = (f32[2048]{0:T(1024)S(1)}, f32[2048]{0:T(1024)}, u32[]{:S(2)}) copy-start(f32[2048]{0:T(1024)} %param.20) | copy-start | bytes 24580
  158.0 19.3 %all-to-all-start.2 = ((bf16[4,64,2048]{2,1,0:T(8,128)(2,1)}), bf16[4,64,2048]{2,1,0:T(8,128)(2,1)}, u32[]{:S(2)}, u32[]{:S(2)}) async-start(bf16[4,64,2048]{2,1,0:T(8,128)(2,1)} %reduce_sum.92), calls=%async_computation.2 | async-start | bytes 2097152 | tf_op jit(solution)/shard_map/all_to_all | solution.py:303
Sparse Core Ops, SparseCore 0:
  26.8 29.9 all-gather.1

commit v5 on v4

--- a/solution.py
+++ b/solution.py
@@ -84,7 +84,7 @@
     return lax.fori_loop(0, turn_count, step_once, softmax_state)
 
 
-def exchange_kernel(axes, x_ref, o_ref, send_sems, recv_sems, own_sem):
+def exchange_kernel(axes, split, x_ref, o_ref, send_sems, recv_sems, own_sem):
     sizes = [lax.axis_size(a) for a in axes]
     count = 1
     for size in sizes:
@@ -107,14 +107,17 @@
             barrier, inc=1, device_id=device_of((me + k) % count), device_id_type=MESH_IDS
         )
     pl.semaphore_wait(barrier, count - 1)
-    own = pltpu.make_async_copy(x_ref.at[me], o_ref.at[me], own_sem)
+    def block(ref, index):
+        return ref.at[index] if split == 0 else ref.at[:, index]
+
+    own = pltpu.make_async_copy(block(x_ref, me), block(o_ref, me), own_sem)
     own.start()
     copies = []
     for k in range(1, count):
         peer = (me + k) % count
         copy = pltpu.make_async_remote_copy(
-            src_ref=x_ref.at[peer],
-            dst_ref=o_ref.at[me],
+            src_ref=block(x_ref, peer),
+            dst_ref=block(o_ref, me),
             send_sem=send_sems.at[k],
             recv_sem=recv_sems.at[k],
             device_id=device_of(peer),
@@ -127,10 +130,10 @@
         copy.wait()
 
 
-def exchange(x, axes, ident):
-    count = x.shape[0]
+def exchange(x, axes, ident, split=0):
+    count = x.shape[split]
     return pl.pallas_call(
-        functools.partial(exchange_kernel, axes),
+        functools.partial(exchange_kernel, axes, split),
         out_shape=jax.ShapeDtypeStruct(x.shape, x.dtype),
         in_specs=[pl.BlockSpec(memory_space=pl.ANY)],
         out_specs=pl.BlockSpec(memory_space=pl.ANY),
@@ -298,9 +301,9 @@
     chips = lax.axis_size("ey")
     cores = lax.axis_size("ec")
     head_parts = head_parts.reshape(chips, cores, tok_rows, model_width)
-    head_parts = lax.all_to_all(head_parts, "ec", split_axis=1, concat_axis=1, tiled=True)
+    head_parts = exchange(head_parts, ("ec",), 2, split=1)
     head_parts = jnp.sum(head_parts.astype(jnp.float32), axis=1).astype(jnp.bfloat16)
-    head_parts = lax.all_to_all(head_parts, "ey", split_axis=0, concat_axis=0, tiled=True)
+    head_parts = exchange(head_parts, ("ey",), 3)
     head_sum = jnp.sum(head_parts.astype(jnp.float32), axis=0)
     residual = hidden_in.astype(jnp.float32) + head_sum
     moe_in = norm_rows(residual, moe_gain)

time: 236 us -> 258 us (1.093)
  the two profiles are of different devices: /device:TPU:1 before, /device:TPU:3 now
where the time goes in v5:
time: 258 us; the launch traced here: 257 us
  Pallas kernels  113 us (44%)
  waiting for transfers between devices  76.2 us (30%)
  matrix products  15.4 us (6%)
  other arithmetic  14.2 us (6%)
  local copies, waits for them, and re-layouts  13.8 us (5%)
  between operations  13.7 us (5%)
  starting transfers between devices  11.3 us (4%)
    pallas_call x4, Pallas kernels, exchange(): pl.pallas_call(functools.partial(exchange_kernel, axes, split), out_shape...  86.8 us
    all_to_all x1, waiting for transfers between devices, shards(): lax.all_to_all(outgoing, 'group', split_axis=0, concat_axis=0, tiled=True)  52.4 us
    pallas_call x1, Pallas kernels, paged_attention(): pl.pallas_call(attention_kernel, out_shape=jax.ShapeDtypeStruct((rows, lo...  25.9 us
    all_gather x1, waiting for transfers between devices, shards(): lax.all_gather(normed, EXPERT, axis=0, tiled=True)  23.8 us
    all_to_all x1, starting transfers between devices, shards(): lax.all_to_all(outgoing, 'group', split_axis=0, concat_axis=0, tiled=True)  11.2 us
  transfers between devices with their start and end apart: 2, of which 2 were waited for; matrix products, arithmetic and copies ran while one was open for 5% of the time, Pallas kernels for 0%

profile of v5, /device:TPU:3, one launch (start us, length us, event | category | flops | bytes accessed | tf_op | source)
XLA Modules:
  0.0 257.2 jit_solution(11667742791671035253)
XLA Ops:
  6.5 0.9 add_select_fusion
  7.4 0.7 broadcast_compare_fusion
  9.2 2.8 %gather_fusion = bf16[256,2,16,256]{3,2,1,0:T(8,128)(2,1)} fusion(bf16[128,2,16,256]{3,2,1,0:T(8,128)(2,1)S(1)} %copy-done, s32[1024]{0:T(1024)S(1)} %pad_clamp_fusion.1), kind=kCustom, calls=%fused_computation | custom fusion | bytes 8389632 | tf_op jit(solution)/shard_map/gather | solution.py:283
  12.0 11.2 %all-to-all-start = ((bf16[32,8,2,16,256]{4,3,2,1,0:T(8,128)(2,1)}), bf16[32,8,2,16,256]{4,3,2,1,0:T(8,128)(2,1)}, u32[]{:S(2)}, u32[]{:S(2)}) async-start(bf16[32,8,2,16,256]{4,3,2,1,0:T(8,128)(2,1)} %bitcast.60), calls=%async_computation | async-start | bytes 8388608 | tf_op jit(solution)/shard_map/all_to_all | solution.py:284
  23.5 0.8 fusion.17
  24.4 4.8 %copy.27 = bf16[2048,3,256]{0,2,1:T(8,128)(2,1)} copy(bf16[2048,3,256]{2,0,1:T(8,128)(2,1)} %param.18) | data formatting | bytes 6291456 | tf_op args[5]
  32.1 23.8 %all-gather.2.cloned.1.call-done = bf16[512,2048]{1,0:T(8,128)(2,1)} async-done(((bf16[64,2048]{1,0:T(8,128)(2,1)}), bf16[512,2048]{1,0:T(8,128)(2,1)}) %all-gather.2.cloned.1.call-update) | async-done | bytes 2097168 | tf_op jit(solution)/shard_map/all_gather | solution.py:264
  55.9 4.3 %fusion = f32[512,3,2,128]{0,3,2,1:T(8,128)S(1)} fusion(bf16[3,2,128,2048]{3,2,1,0:T(8,128)(2,1)} %bitcast.63, bf16[512,2048]{1,0:T(8,128)(2,1)} %all-gather.2.cloned.1.call-done), kind=kOutput, calls=%fused_computation.5 | convolution fusion | flops 1610612736 | bytes 6815744 | tf_op jit(solution)/shard_map/dot_general | solution.py:263
  61.0 52.4 %all-to-all-done = bf16[32,8,2,16,256]{4,3,2,1,0:T(8,128)(2,1)} async-done(((bf16[32,8,2,16,256]{4,3,2,1,0:T(8,128)(2,1)}), bf16[32,8,2,16,256]{4,3,2,1,0:T(8,128)(2,1)}, u32[]{:S(2)}, u32[]{:S(2)}) %all-to-all-start) | async-done | bytes 4194336 | tf_op jit(solution)/shard_map/all_to_all | solution.py:284
  113.4 25.9 %shard_map.127 = bf16[512,256]{1,0:T(8,128)(2,1)S(1)} custom-call(s32[128]{0:T(128)S(1)} %multiply_add_fusion.1.slots_ref, s32[1]{0:T(128)} %dynamic_slice.7.len_ref, bf16[512,256]{1,0:T(8,128)(2,1)S(1)} %copy.35.q_ref, bf16[512,256]{1,0:T(8,128)(2,1)S(1)} %copy.36.nk_ref, bf16[512,256]{1,0:T(8,128)(2,1)S(1)} %copy.37.nv_ref, ...), custom_call_target="tpu_custom_call" | custom-call | flops 1342177280 | bytes 5242880 | tf_op jit(solution)/shard_map/pallas_call | solution.py:209
  139.3 2.0 convolution_convert_fusion
  141.3 38.4 %shard_map.128 = bf16[4,2,64,2048]{3,2,1,0:T(8,128)(2,1)} custom-call(bf16[4,2,64,2048]{3,2,1,0:T(8,128)(2,1)} %bitcast.61), custom_call_target="tpu_custom_call" | custom-call | tf_op jit(solution)/shard_map/pallas_call | solution.py:135
  179.8 3.4 %reduce_sum.92.x_ref = bf16[4,64,2048]{2,1,0:T(8,128)(2,1)} reduce(bf16[4,2,64,2048]{3,2,1,0:T(8,128)(2,1)} %shard_map.128, bf16[]{:T(256)} %constant.78.clone.1), dimensions={1}, to_apply=%region_4.5 | reduce | flops 524288 | bytes 3145730 | tf_op jit(solution)/shard_map/reduce_sum | solution.py:305
  183.2 16.3 %shard_map.129 = bf16[4,64,2048]{2,1,0:T(8,128)(2,1)} custom-call(bf16[4,64,2048]{2,1,0:T(8,128)(2,1)} %reduce_sum.92.x_ref), custom_call_target="tpu_custom_call" | custom-call | tf_op jit(solution)/shard_map/pallas_call | solution.py:135
  199.5 1.4 convert_reduce_fusion
  201.2 1.5 convolution_convert_fusion.2
  202.7 16.4 %shard_map.130 = bf16[8,32,2048]{2,1,0:T(8,128)(2,1)} custom-call(bf16[8,32,2048]{2,1,0:T(8,128)(2,1)} %bitcast.62), custom_call_target="tpu_custom_call" | custom-call | tf_op jit(solution)/shard_map/pallas_call | solution.py:135
  219.1 2.6 %fusion.5 = f32[256,512]{1,0:T(8,128)S(1)} fusion(bf16[256,2048]{1,0:T(8,128)(2,1)} %bitcast.64, bf16[1,2048,512]{2,1,0:T(8,128)(2,1)} %param.21), kind=kOutput, calls=%fused_computation.10 | convolution fusion | flops 536870912 | bytes 3670016 | tf_op jit(solution)/shard_map/dot_general | solution.py:333
  221.7 4.9 %convolution_convert_fusion.1 = bf16[256,2048]{1,0:T(8,128)(2,1)} fusion(bf16[1,512,2048]{2,1,0:T(8,128)(2,1)} %param.23, bf16[256,2048]{1,0:T(8,128)(2,1)} %bitcast.65, bf16[1,2048,512]{2,1,0:T(8,128)(2,1)} %param.22, f32[256,512]{1,0:T(8,128)S(1)} %fusion.5), kind=kOutput, calls=%fused_computation.3 | convolution fusion | flops 1075052544 | bytes 6815744 | tf_op jit(solution)/shard_map/dot_general | solution.py:337
  226.6 15.6 %shard_map.131 = bf16[8,32,2048]{2,1,0:T(8,128)(2,1)} custom-call(bf16[8,32,2048]{2,1,0:T(8,128)(2,1)} %bitcast.66), custom_call_target="tpu_custom_call" | custom-call | tf_op jit(solution)/shard_map/pallas_call | solution.py:135
  242.3 2.8 %gather_fusion.1 = bf16[128,2048]{1,0:T(8,128)(2,1)S(1)} fusion(bf16[256,2048]{1,0:T(8,128)(2,1)} %bitcast.59, s32[1024]{0:T(1024)S(1)} %pad_clamp_fusion), kind=kCustom, calls=%fused_computation.1 | custom fusion | bytes 1049088 | tf_op jit(solution)/shard_map/gather | solution.py:342
  245.1 1.6 reshape.195
  246.7 2.8 %multiply_reduce_fusion = f32[64,2048]{1,0:T(8,128)S(1)} fusion(f32[64,2,2048]{2,1,0:T(2,128)} %reshape.195, f32[64,2]{1,0:T(8,128)S(1)} %copy.33), kind=kLoop, calls=%fused_computation.15 | loop fusion | flops 393216 | bytes 1573376 | tf_op jit(solution)/shard_map/reduce_sum | solution.py:345
  249.5 0.9 fusion.26
  (54 shorter events, 5.1 us)
Async XLA Ops:
  6.5 2.7 %copy-start = (bf16[128,2,16,256]{3,2,1,0:T(8,128)(2,1)S(1)}, bf16[128,2,16,256]{3,2,1,0:T(8,128)(2,1)}, u32[]{:S(2)}) copy-start(bf16[128,2,16,256]{3,2,1,0:T(8,128)(2,1)} %param.16) | copy-start | bytes 6291460
  12.0 11.3 %copy-start.1 = (bf16[64,2048]{1,0:T(8,128)(2,1)S(1)}, bf16[64,2048]{1,0:T(8,128)(2,1)}, u32[]{:S(2)}) copy-start(bf16[64,2048]{1,0:T(8,128)(2,1)} %param.13) | copy-start | bytes 786436
  12.0 11.5 %copy-start.3 = (f32[2048]{0:T(1024)S(1)}, f32[2048]{0:T(1024)}, u32[]{:S(2)}) copy-start(f32[2048]{0:T(1024)} %param.17) | copy-start | bytes 24580
  12.0 101.5 %all-to-all-start = ((bf16[32,8,2,16,256]{4,3,2,1,0:T(8,128)(2,1)}), bf16[32,8,2,16,256]{4,3,2,1,0:T(8,128)(2,1)}, u32[]{:S(2)}, u32[]{:S(2)}) async-start(bf16[32,8,2,16,256]{4,3,2,1,0:T(8,128)(2,1)} %bitcast.60), calls=%async_computation | async-start | bytes 8388608 | tf_op jit(solution)/shard_map/all_to_all | solution.py:284
  23.2 32.7 %all-gather.2.cloned.1.call-start = ((), (), s32[]{:S(2)}) async-start(), calls=%async_computation.1 | async-start | bytes 2359296 | tf_op jit(solution)/shard_map/all_gather | solution.py:264
  24.3 4.8 %copy-start.5 = (s32[64,2]{0,1:T(2,128)S(1)}, s32[64,2]{0,1:T(2,128)}, u32[]{:S(2)}) copy-start(s32[64,2]{0,1:T(2,128)} %param.24) | copy-start | bytes 1540
  24.4 5.3 %copy-start.6 = (f32[64,2]{0,1:T(2,128)S(1)}, f32[64,2]{0,1:T(2,128)}, u32[]{:S(2)}) copy-start(f32[64,2]{0,1:T(2,128)} %param.25) | copy-start | bytes 1540
  24.4 5.4 %copy-start.7 = (s32[32]{0:T(128)S(1)}, s32[32]{0:T(128)}, u32[]{:S(2)}) copy-start(s32[32]{0:T(128)} %param.14) | copy-start | bytes 388
  113.4 25.9 %copy-start.2 = (bf16[256,2048]{1,0:T(8,128)(2,1)S(1)}, bf16[256,2048]{1,0:T(8,128)(2,1)}, u32[]{:S(2)}) copy-start(bf16[256,2048]{1,0:T(8,128)(2,1)} %param.19) | copy-start | bytes 3145732
  183.2 18.0 %copy-start.4 = (f32[2048]{0:T(1024)S(1)}, f32[2048]{0:T(1024)}, u32[]{:S(2)}) copy-start(f32[2048]{0:T(1024)} %param.20) | copy-start | bytes 24580
Sparse Core Ops, SparseCore 0:
  25.9 29.9 all-gather.1

commit v6 on v5

--- a/solution.py
+++ b/solution.py
@@ -296,13 +296,15 @@
         arrived,
         block_len,
     )
-    rows_piece = attended
-    head_parts = jnp.dot(rows_piece, w_out, preferred_element_type=jnp.float32).astype(jnp.bfloat16)
     chips = lax.axis_size("ey")
     cores = lax.axis_size("ec")
-    head_parts = head_parts.reshape(chips, cores, tok_rows, model_width)
-    head_parts = exchange(head_parts, ("ec",), 2, split=1)
-    head_parts = jnp.sum(head_parts.astype(jnp.float32), axis=1).astype(jnp.bfloat16)
+    rows_piece = jnp.transpose(
+        attended.reshape(chips, cores, tok_rows, local_width), (1, 0, 2, 3)
+    ).reshape(new_count, local_width)
+    head_parts = jnp.dot(rows_piece, w_out, preferred_element_type=jnp.float32).astype(jnp.bfloat16)
+    head_parts = head_parts.reshape(cores, chips, tok_rows, model_width)
+    head_parts = exchange(head_parts, ("ec",), 2)
+    head_parts = jnp.sum(head_parts.astype(jnp.float32), axis=0).astype(jnp.bfloat16)
     head_parts = exchange(head_parts, ("ey",), 3)
     head_sum = jnp.sum(head_parts.astype(jnp.float32), axis=0)
     residual = hidden_in.astype(jnp.float32) + head_sum

time: 258 us -> 258 us (level)
  the two profiles are of different devices: /device:TPU:3 before, /device:TPU:1 now
where the time goes in v6:
time: 258 us; the launch traced here: 253 us
  Pallas kernels  105 us (41%)
  waiting for transfers between devices  78.5 us (30%)
  matrix products  15.4 us (6%)
  other arithmetic  14.1 us (5%)
  local copies, waits for them, and re-layouts  13.8 us (5%)
  between operations  13.7 us (5%)
  starting transfers between devices  12.2 us (5%)
    pallas_call x4, Pallas kernels, exchange(): pl.pallas_call(functools.partial(exchange_kernel, axes, split), out_shape...  86.6 us
    all_to_all x1, waiting for transfers between devices, shards(): lax.all_to_all(outgoing, 'group', split_axis=0, concat_axis=0, tiled=True)  54.8 us
    all_gather x1, waiting for transfers between devices, shards(): lax.all_gather(normed, EXPERT, axis=0, tiled=True)  23.7 us
    pallas_call x1, Pallas kernels, paged_attention(): pl.pallas_call(attention_kernel, out_shape=jax.ShapeDtypeStruct((rows, lo...  18.3 us
    all_to_all x1, starting transfers between devices, shards(): lax.all_to_all(outgoing, 'group', split_axis=0, concat_axis=0, tiled=True)  12.1 us
  transfers between devices with their start and end apart: 2, of which 2 were waited for; matrix products, arithmetic and copies ran while one was open for 5% of the time, Pallas kernels for 0%

profile of v6, /device:TPU:1, one launch (start us, length us, event | category | flops | bytes accessed | tf_op | source)
XLA Modules:
  0.0 252.7 jit_solution(2388156152476488063)
XLA Ops:
  6.5 0.9 add_select_fusion
  7.4 0.7 broadcast_compare_fusion
  9.2 2.8 %gather_fusion = bf16[256,2,16,256]{3,2,1,0:T(8,128)(2,1)} fusion(bf16[128,2,16,256]{3,2,1,0:T(8,128)(2,1)S(1)} %copy-done, s32[1024]{0:T(1024)S(1)} %pad_clamp_fusion.1), kind=kCustom, calls=%fused_computation | custom fusion | bytes 8389632 | tf_op jit(solution)/shard_map/gather | solution.py:283
  12.0 12.1 %all-to-all-start = ((bf16[32,8,2,16,256]{4,3,2,1,0:T(8,128)(2,1)}), bf16[32,8,2,16,256]{4,3,2,1,0:T(8,128)(2,1)}, u32[]{:S(2)}, u32[]{:S(2)}) async-start(bf16[32,8,2,16,256]{4,3,2,1,0:T(8,128)(2,1)} %bitcast.65), calls=%async_computation | async-start | bytes 8388608 | tf_op jit(solution)/shard_map/all_to_all | solution.py:284
  24.3 0.8 fusion.17
  25.2 4.8 %copy.28 = bf16[2048,3,256]{0,2,1:T(8,128)(2,1)} copy(bf16[2048,3,256]{2,0,1:T(8,128)(2,1)} %param.18) | data formatting | bytes 6291456 | tf_op args[5]
  33.0 23.7 %all-gather.2.cloned.1.call-done = bf16[512,2048]{1,0:T(8,128)(2,1)} async-done(((bf16[64,2048]{1,0:T(8,128)(2,1)}), bf16[512,2048]{1,0:T(8,128)(2,1)}) %all-gather.2.cloned.1.call-update) | async-done | bytes 2097168 | tf_op jit(solution)/shard_map/all_gather | solution.py:264
  56.7 4.3 %fusion = f32[512,3,2,128]{0,3,2,1:T(8,128)S(1)} fusion(bf16[3,2,128,2048]{3,2,1,0:T(8,128)(2,1)} %bitcast.68, bf16[512,2048]{1,0:T(8,128)(2,1)} %all-gather.2.cloned.1.call-done), kind=kOutput, calls=%fused_computation.5 | convolution fusion | flops 1610612736 | bytes 6815744 | tf_op jit(solution)/shard_map/dot_general | solution.py:263
  61.9 54.8 %all-to-all-done = bf16[32,8,2,16,256]{4,3,2,1,0:T(8,128)(2,1)} async-done(((bf16[32,8,2,16,256]{4,3,2,1,0:T(8,128)(2,1)}), bf16[32,8,2,16,256]{4,3,2,1,0:T(8,128)(2,1)}, u32[]{:S(2)}, u32[]{:S(2)}) %all-to-all-start) | async-done | bytes 4194336 | tf_op jit(solution)/shard_map/all_to_all | solution.py:284
  116.7 18.3 %shard_map.127 = bf16[512,256]{1,0:T(8,128)(2,1)S(1)} custom-call(s32[128]{0:T(128)S(1)} %multiply_add_fusion.1.slots_ref, s32[1]{0:T(128)} %dynamic_slice.7.len_ref, bf16[512,256]{1,0:T(8,128)(2,1)S(1)} %copy.37.q_ref, bf16[512,256]{1,0:T(8,128)(2,1)S(1)} %copy.38.nk_ref, bf16[512,256]{1,0:T(8,128)(2,1)S(1)} %copy.39.nv_ref, ...), custom_call_target="tpu_custom_call" | custom-call | flops 1342177280 | bytes 5242880 | tf_op jit(solution)/shard_map/pallas_call | solution.py:209
  135.0 2.0 convolution_convert_fusion
  137.0 38.3 %shard_map.128 = bf16[2,4,64,2048]{3,2,1,0:T(8,128)(2,1)} custom-call(bf16[2,4,64,2048]{3,2,1,0:T(8,128)(2,1)} %bitcast.66), custom_call_target="tpu_custom_call" | custom-call | tf_op jit(solution)/shard_map/pallas_call | solution.py:135
  175.3 3.3 %reduce_sum.92.x_ref = bf16[4,64,2048]{2,1,0:T(8,128)(2,1)} reduce(bf16[2,4,64,2048]{3,2,1,0:T(8,128)(2,1)} %shard_map.128, bf16[]{:T(256)} %constant.78.clone.1), dimensions={0}, to_apply=%region_4.5 | reduce | flops 524288 | bytes 3145730 | tf_op jit(solution)/shard_map/reduce_sum | solution.py:307
  178.6 16.3 %shard_map.129 = bf16[4,64,2048]{2,1,0:T(8,128)(2,1)} custom-call(bf16[4,64,2048]{2,1,0:T(8,128)(2,1)} %reduce_sum.92.x_ref), custom_call_target="tpu_custom_call" | custom-call | tf_op jit(solution)/shard_map/pallas_call | solution.py:135
  195.0 1.4 convert_reduce_fusion
  196.6 1.5 convolution_convert_fusion.2
  198.1 16.4 %shard_map.130 = bf16[8,32,2048]{2,1,0:T(8,128)(2,1)} custom-call(bf16[8,32,2048]{2,1,0:T(8,128)(2,1)} %bitcast.67), custom_call_target="tpu_custom_call" | custom-call | tf_op jit(solution)/shard_map/pallas_call | solution.py:135
  214.5 2.6 %fusion.5 = f32[256,512]{1,0:T(8,128)S(1)} fusion(bf16[256,2048]{1,0:T(8,128)(2,1)} %bitcast.69, bf16[1,2048,512]{2,1,0:T(8,128)(2,1)} %param.21), kind=kOutput, calls=%fused_computation.10 | convolution fusion | flops 536870912 | bytes 3670016 | tf_op jit(solution)/shard_map/dot_general | solution.py:335
  217.1 4.9 %convolution_convert_fusion.1 = bf16[256,2048]{1,0:T(8,128)(2,1)} fusion(bf16[1,512,2048]{2,1,0:T(8,128)(2,1)} %param.23, bf16[256,2048]{1,0:T(8,128)(2,1)} %bitcast.70, bf16[1,2048,512]{2,1,0:T(8,128)(2,1)} %param.22, f32[256,512]{1,0:T(8,128)S(1)} %fusion.5), kind=kOutput, calls=%fused_computation.3 | convolution fusion | flops 1075052544 | bytes 6815744 | tf_op jit(solution)/shard_map/dot_general | solution.py:339
  222.1 15.6 %shard_map.131 = bf16[8,32,2048]{2,1,0:T(8,128)(2,1)} custom-call(bf16[8,32,2048]{2,1,0:T(8,128)(2,1)} %bitcast.71), custom_call_target="tpu_custom_call" | custom-call | tf_op jit(solution)/shard_map/pallas_call | solution.py:135
  237.7 2.8 %gather_fusion.1 = bf16[128,2048]{1,0:T(8,128)(2,1)S(1)} fusion(bf16[256,2048]{1,0:T(8,128)(2,1)} %bitcast.64, s32[1024]{0:T(1024)S(1)} %pad_clamp_fusion), kind=kCustom, calls=%fused_computation.1 | custom fusion | bytes 1049088 | tf_op jit(solution)/shard_map/gather | solution.py:344
  240.5 1.6 reshape.203
  242.1 2.8 %multiply_reduce_fusion = f32[64,2048]{1,0:T(8,128)S(1)} fusion(f32[64,2,2048]{2,1,0:T(2,128)} %reshape.203, f32[64,2]{1,0:T(8,128)S(1)} %copy.35), kind=kLoop, calls=%fused_computation.15 | loop fusion | flops 393216 | bytes 1573376 | tf_op jit(solution)/shard_map/reduce_sum | solution.py:347
  244.9 0.9 fusion.26
  (55 shorter events, 5.1 us)
Async XLA Ops:
  6.5 2.7 %copy-start = (bf16[128,2,16,256]{3,2,1,0:T(8,128)(2,1)S(1)}, bf16[128,2,16,256]{3,2,1,0:T(8,128)(2,1)}, u32[]{:S(2)}) copy-start(bf16[128,2,16,256]{3,2,1,0:T(8,128)(2,1)} %param.16) | copy-start | bytes 6291460
  12.0 12.2 %copy-start.1 = (bf16[64,2048]{1,0:T(8,128)(2,1)S(1)}, bf16[64,2048]{1,0:T(8,128)(2,1)}, u32[]{:S(2)}) copy-start(bf16[64,2048]{1,0:T(8,128)(2,1)} %param.13) | copy-start | bytes 786436
  12.0 12.4 %copy-start.3 = (f32[2048]{0:T(1024)S(1)}, f32[2048]{0:T(1024)}, u32[]{:S(2)}) copy-start(f32[2048]{0:T(1024)} %param.17) | copy-start | bytes 24580
  12.0 104.7 %all-to-all-start = ((bf16[32,8,2,16,256]{4,3,2,1,0:T(8,128)(2,1)}), bf16[32,8,2,16,256]{4,3,2,1,0:T(8,128)(2,1)}, u32[]{:S(2)}, u32[]{:S(2)}) async-start(bf16[32,8,2,16,256]{4,3,2,1,0:T(8,128)(2,1)} %bitcast.65), calls=%async_computation | async-start | bytes 8388608 | tf_op jit(solution)/shard_map/all_to_all | solution.py:284
  24.1 32.6 %all-gather.2.cloned.1.call-start = ((), (), s32[]{:S(2)}) async-start(), calls=%async_computation.1 | async-start | bytes 2359296 | tf_op jit(solution)/shard_map/all_gather | solution.py:264
  25.2 4.8 %copy-start.5 = (s32[64,2]{0,1:T(2,128)S(1)}, s32[64,2]{0,1:T(2,128)}, u32[]{:S(2)}) copy-start(s32[64,2]{0,1:T(2,128)} %param.24) | copy-start | bytes 1540
  25.2 5.3 %copy-start.6 = (f32[64,2]{0,1:T(2,128)S(1)}, f32[64,2]{0,1:T(2,128)}, u32[]{:S(2)}) copy-start(f32[64,2]{0,1:T(2,128)} %param.25) | copy-start | bytes 1540
  25.2 5.4 %copy-start.7 = (s32[32]{0:T(128)S(1)}, s32[32]{0:T(128)}, u32[]{:S(2)}) copy-start(s32[32]{0:T(128)} %param.14) | copy-start | bytes 388
  116.7 18.3 %copy-start.2 = (bf16[256,2048]{1,0:T(8,128)(2,1)S(1)}, bf16[256,2048]{1,0:T(8,128)(2,1)}, u32[]{:S(2)}) copy-start(bf16[256,2048]{1,0:T(8,128)(2,1)} %param.19) | copy-start | bytes 3145732
  178.6 18.0 %copy-start.4 = (f32[2048]{0:T(1024)S(1)}, f32[2048]{0:T(1024)}, u32[]{:S(2)}) copy-start(f32[2048]{0:T(1024)} %param.20) | copy-start | bytes 24580
Sparse Core Ops, SparseCore 0:
  26.8 29.9 all-gather.1

commit v7 on v5

--- a/solution.py
+++ b/solution.py
@@ -301,9 +301,9 @@
     chips = lax.axis_size("ey")
     cores = lax.axis_size("ec")
     head_parts = head_parts.reshape(chips, cores, tok_rows, model_width)
-    head_parts = exchange(head_parts, ("ec",), 2, split=1)
+    head_parts = lax.all_to_all(head_parts, "ec", split_axis=1, concat_axis=1, tiled=True)
     head_parts = jnp.sum(head_parts.astype(jnp.float32), axis=1).astype(jnp.bfloat16)
-    head_parts = exchange(head_parts, ("ey",), 3)
+    head_parts = exchange(head_parts, ("ey",), 2)
     head_sum = jnp.sum(head_parts.astype(jnp.float32), axis=0)
     residual = hidden_in.astype(jnp.float32) + head_sum
     moe_in = norm_rows(residual, moe_gain)

time: 258 us -> 230 us (0.89)
  the two profiles are of different devices: /device:TPU:3 before, /device:TPU:1 now
where the time goes in v7:
time: 230 us; the launch traced here: 227 us
  waiting for transfers between devices  78.5 us (34%)
  Pallas kernels  69 us (30%)
  local copies, waits for them, and re-layouts  14.1 us (6%)
  other arithmetic  14.1 us (6%)
  matrix products  14.1 us (6%)
  between operations  13.7 us (6%)
  starting transfers between devices  12.2 us (5%)
  blocking collectives  11.4 us (5%)
    all_to_all x1, waiting for transfers between devices, shards(): lax.all_to_all(outgoing, 'group', split_axis=0, concat_axis=0, tiled=True)  54.8 us
    pallas_call x3, Pallas kernels, exchange(): pl.pallas_call(functools.partial(exchange_kernel, axes, split), out_shape...  48.3 us
    all_gather x1, waiting for transfers between devices, shards(): lax.all_gather(normed, EXPERT, axis=0, tiled=True)  23.7 us
    pallas_call x1, Pallas kernels, paged_attention(): pl.pallas_call(attention_kernel, out_shape=jax.ShapeDtypeStruct((rows, lo...  20.6 us
    all_to_all x1, starting transfers between devices, shards(): lax.all_to_all(outgoing, 'group', split_axis=0, concat_axis=0, tiled=True)  12.1 us
    all_to_all x1, blocking collectives, shards(): lax.all_to_all(head_parts, 'ec', split_axis=1, concat_axis=1, tiled=True)  11.4 us
    unnamed x19, local copies, waits for them, and re-layouts  5.03 us
    dot_general x1, matrix products, shards(): jnp.dot(hidden, w_down[0], preferred_element_type=jnp.float32)  4.92 us
  transfers between devices with their start and end apart: 2, of which 2 were waited for; matrix products, arithmetic and copies ran while one was open for 6% of the time, Pallas kernels for 0%

profile of v7, /device:TPU:1, one launch (start us, length us, event | category | flops | bytes accessed | tf_op | source)
XLA Modules:
  0.0 227.0 jit_solution(2109897635352414534)
XLA Ops:
  6.5 0.9 add_select_fusion
  7.4 0.7 broadcast_compare_fusion
  9.2 2.8 %gather_fusion = bf16[256,2,16,256]{3,2,1,0:T(8,128)(2,1)} fusion(bf16[128,2,16,256]{3,2,1,0:T(8,128)(2,1)S(1)} %copy-done, s32[1024]{0:T(1024)S(1)} %pad_clamp_fusion.1), kind=kCustom, calls=%fused_computation | custom fusion | bytes 8389632 | tf_op jit(solution)/shard_map/gather | solution.py:283
  12.0 12.1 %all-to-all-start = ((bf16[32,8,2,16,256]{4,3,2,1,0:T(8,128)(2,1)}), bf16[32,8,2,16,256]{4,3,2,1,0:T(8,128)(2,1)}, u32[]{:S(2)}, u32[]{:S(2)}) async-start(bf16[32,8,2,16,256]{4,3,2,1,0:T(8,128)(2,1)} %bitcast.60), calls=%async_computation | async-start | bytes 8388608 | tf_op jit(solution)/shard_map/all_to_all | solution.py:284
  24.3 0.8 fusion.17
  25.2 4.8 %copy.35 = bf16[2048,3,256]{0,2,1:T(8,128)(2,1)} copy(bf16[2048,3,256]{2,0,1:T(8,128)(2,1)} %param.18) | data formatting | bytes 6291456 | tf_op args[5]
  33.0 23.7 %all-gather.2.cloned.1.call-done = bf16[512,2048]{1,0:T(8,128)(2,1)} async-done(((bf16[64,2048]{1,0:T(8,128)(2,1)}), bf16[512,2048]{1,0:T(8,128)(2,1)}) %all-gather.2.cloned.1.call-update) | async-done | bytes 2097168 | tf_op jit(solution)/shard_map/all_gather | solution.py:264
  56.7 4.3 %fusion = f32[512,3,2,128]{0,3,2,1:T(8,128)S(1)} fusion(bf16[3,2,128,2048]{3,2,1,0:T(8,128)(2,1)} %bitcast.63, bf16[512,2048]{1,0:T(8,128)(2,1)} %all-gather.2.cloned.1.call-done), kind=kOutput, calls=%fused_computation.5 | convolution fusion | flops 1610612736 | bytes 6815744 | tf_op jit(solution)/shard_map/dot_general | solution.py:263
  61.9 54.8 %all-to-all-done = bf16[32,8,2,16,256]{4,3,2,1,0:T(8,128)(2,1)} async-done(((bf16[32,8,2,16,256]{4,3,2,1,0:T(8,128)(2,1)}), bf16[32,8,2,16,256]{4,3,2,1,0:T(8,128)(2,1)}, u32[]{:S(2)}, u32[]{:S(2)}) %all-to-all-start) | async-done | bytes 4194336 | tf_op jit(solution)/shard_map/all_to_all | solution.py:284
  116.7 20.6 %shard_map.127 = bf16[512,256]{1,0:T(8,128)(2,1)S(1)} custom-call(s32[128]{0:T(128)S(1)} %multiply_add_fusion.1.slots_ref, s32[1]{0:T(128)} %dynamic_slice.7.len_ref, bf16[512,256]{1,0:T(8,128)(2,1)S(1)} %copy.44.q_ref, bf16[512,256]{1,0:T(8,128)(2,1)S(1)} %copy.45.nk_ref, bf16[512,256]{1,0:T(8,128)(2,1)S(1)} %copy.46.nv_ref, ...), custom_call_target="tpu_custom_call" | custom-call | flops 1342177280 | bytes 5242880 | tf_op jit(solution)/shard_map/pallas_call | solution.py:209
  137.3 0.7 convolution_convert_fusion
  138.3 11.4 %all_to_all.10 = bf16[4,2,64,2048]{3,2,0,1:T(8,128)(2,1)} all-to-all(bf16[4,2,64,2048]{3,2,0,1:T(8,128)(2,1)S(1)} %copy.39), channel_id=1, replica_groups=mesh['group'=32,'ey'=4,'ec'=2] {'ec'}, dimensions={1} | all-to-all | bytes 4194304 | tf_op jit(solution)/shard_map/all_to_all | solution.py:304
  149.7 3.3 %reduce_sum.92.x_ref = bf16[4,64,2048]{2,1,0:T(8,128)(2,1)} reduce(bf16[4,2,64,2048]{3,2,0,1:T(8,128)(2,1)} %all_to_all.10, bf16[]{:T(256)} %constant.78.clone.1), dimensions={1}, to_apply=%region_4.5 | reduce | flops 524288 | bytes 3145730 | tf_op jit(solution)/shard_map/reduce_sum | solution.py:305
  153.0 16.0 %shard_map.128 = bf16[4,64,2048]{2,1,0:T(8,128)(2,1)} custom-call(bf16[4,64,2048]{2,1,0:T(8,128)(2,1)} %reduce_sum.92.x_ref), custom_call_target="tpu_custom_call" | custom-call | tf_op jit(solution)/shard_map/pallas_call | solution.py:135
  169.0 1.4 convert_reduce_fusion
  170.7 1.5 convolution_convert_fusion.2
  172.2 16.7 %shard_map.129 = bf16[8,32,2048]{2,1,0:T(8,128)(2,1)} custom-call(bf16[8,32,2048]{2,1,0:T(8,128)(2,1)} %bitcast.62), custom_call_target="tpu_custom_call" | custom-call | tf_op jit(solution)/shard_map/pallas_call | solution.py:135
  188.9 2.6 %fusion.5 = f32[256,512]{1,0:T(8,128)S(1)} fusion(bf16[256,2048]{1,0:T(8,128)(2,1)} %bitcast.64, bf16[1,2048,512]{2,1,0:T(8,128)(2,1)} %param.21), kind=kOutput, calls=%fused_computation.10 | convolution fusion | flops 536870912 | bytes 3670016 | tf_op jit(solution)/shard_map/dot_general | solution.py:333
  191.5 4.9 %convolution_convert_fusion.1 = bf16[256,2048]{1,0:T(8,128)(2,1)} fusion(bf16[1,512,2048]{2,1,0:T(8,128)(2,1)} %param.23, bf16[256,2048]{1,0:T(8,128)(2,1)} %bitcast.65, bf16[1,2048,512]{2,1,0:T(8,128)(2,1)} %param.22, f32[256,512]{1,0:T(8,128)S(1)} %fusion.5), kind=kOutput, calls=%fused_computation.3 | convolution fusion | flops 1075052544 | bytes 6815744 | tf_op jit(solution)/shard_map/dot_general | solution.py:337
  196.4 15.6 %shard_map.130 = bf16[8,32,2048]{2,1,0:T(8,128)(2,1)} custom-call(bf16[8,32,2048]{2,1,0:T(8,128)(2,1)} %bitcast.66), custom_call_target="tpu_custom_call" | custom-call | tf_op jit(solution)/shard_map/pallas_call | solution.py:135
  212.1 2.8 %gather_fusion.1 = bf16[128,2048]{1,0:T(8,128)(2,1)S(1)} fusion(bf16[256,2048]{1,0:T(8,128)(2,1)} %bitcast.59, s32[1024]{0:T(1024)S(1)} %pad_clamp_fusion), kind=kCustom, calls=%fused_computation.1 | custom fusion | bytes 1049088 | tf_op jit(solution)/shard_map/gather | solution.py:342
  214.9 1.6 reshape.195
  216.5 2.8 %multiply_reduce_fusion = f32[64,2048]{1,0:T(8,128)S(1)} fusion(f32[64,2,2048]{2,1,0:T(2,128)} %reshape.195, f32[64,2]{1,0:T(8,128)S(1)} %copy.42), kind=kLoop, calls=%fused_computation.15 | loop fusion | flops 393216 | bytes 1573376 | tf_op jit(solution)/shard_map/reduce_sum | solution.py:345
  219.3 0.9 fusion.26
  (55 shorter events, 5.3 us)
Async XLA Ops:
  6.5 2.7 %copy-start = (bf16[128,2,16,256]{3,2,1,0:T(8,128)(2,1)S(1)}, bf16[128,2,16,256]{3,2,1,0:T(8,128)(2,1)}, u32[]{:S(2)}) copy-start(bf16[128,2,16,256]{3,2,1,0:T(8,128)(2,1)} %param.16) | copy-start | bytes 6291460
  12.0 12.2 %copy-start.1 = (bf16[64,2048]{1,0:T(8,128)(2,1)S(1)}, bf16[64,2048]{1,0:T(8,128)(2,1)}, u32[]{:S(2)}) copy-start(bf16[64,2048]{1,0:T(8,128)(2,1)} %param.13) | copy-start | bytes 786436
  12.0 12.4 %copy-start.3 = (f32[2048]{0:T(1024)S(1)}, f32[2048]{0:T(1024)}, u32[]{:S(2)}) copy-start(f32[2048]{0:T(1024)} %param.17) | copy-start | bytes 24580
  12.0 104.7 %all-to-all-start = ((bf16[32,8,2,16,256]{4,3,2,1,0:T(8,128)(2,1)}), bf16[32,8,2,16,256]{4,3,2,1,0:T(8,128)(2,1)}, u32[]{:S(2)}, u32[]{:S(2)}) async-start(bf16[32,8,2,16,256]{4,3,2,1,0:T(8,128)(2,1)} %bitcast.60), calls=%async_computation | async-start | bytes 8388608 | tf_op jit(solution)/shard_map/all_to_all | solution.py:284
  24.1 32.6 %all-gather.2.cloned.1.call-start = ((), (), s32[]{:S(2)}) async-start(), calls=%async_computation.2 | async-start | bytes 2359296 | tf_op jit(solution)/shard_map/all_gather | solution.py:264
  25.2 4.8 %copy-start.5 = (s32[64,2]{0,1:T(2,128)S(1)}, s32[64,2]{0,1:T(2,128)}, u32[]{:S(2)}) copy-start(s32[64,2]{0,1:T(2,128)} %param.24) | copy-start | bytes 1540
  25.2 5.3 %copy-start.6 = (f32[64,2]{0,1:T(2,128)S(1)}, f32[64,2]{0,1:T(2,128)}, u32[]{:S(2)}) copy-start(f32[64,2]{0,1:T(2,128)} %param.25) | copy-start | bytes 1540
  25.2 5.4 %copy-start.7 = (s32[32]{0:T(128)S(1)}, s32[32]{0:T(128)}, u32[]{:S(2)}) copy-start(s32[32]{0:T(128)} %param.14) | copy-start | bytes 388
  116.7 20.6 %copy-start.2 = (bf16[256,2048]{1,0:T(8,128)(2,1)S(1)}, bf16[256,2048]{1,0:T(8,128)(2,1)}, u32[]{:S(2)}) copy-start(bf16[256,2048]{1,0:T(8,128)(2,1)} %param.19) | copy-start | bytes 3145732
  153.0 17.7 %copy-start.4 = (f32[2048]{0:T(1024)S(1)}, f32[2048]{0:T(1024)}, u32[]{:S(2)}) copy-start(f32[2048]{0:T(1024)} %param.20) | copy-start | bytes 24580
Sparse Core Ops, SparseCore 0:
  26.8 29.9 all-gather.1

commit v8 on v7

--- a/solution.py
+++ b/solution.py
@@ -146,8 +146,28 @@
     )(x)
 
 
-def attention_kernel(
-    slots_ref, len_ref, q_ref, nk_ref, nv_ref, arr_ref, o_ref, kbuf, vbuf, m_sc, l_sc, acc_sc
+def fresh_kernel(q_ref, nk_ref, nv_ref, m_ref, l_ref, acc_ref):
+    rows, width = q_ref.shape
+    score_scale = width ** (-0.5)
+    dims = (((1,), (1,)), ((), ()))
+    scores = (
+        lax.dot_general(q_ref[...], nk_ref[...], dims, preferred_element_type=jnp.float32)
+        * score_scale
+    )
+    row_i = lax.broadcasted_iota(jnp.int32, (rows, rows), 0)
+    col_i = lax.broadcasted_iota(jnp.int32, (rows, rows), 1)
+    scores = jnp.where(col_i <= row_i, scores, -1e30)
+    peak = jnp.max(scores, axis=-1, keepdims=True)
+    weights = jnp.exp(scores - peak)
+    m_ref[...] = peak
+    l_ref[...] = jnp.sum(weights, axis=-1, keepdims=True)
+    acc_ref[...] = jnp.dot(
+        weights.astype(jnp.bfloat16), nv_ref[...], preferred_element_type=jnp.float32
+    )
+
+
+def cache_kernel(
+    slots_ref, len_ref, q_ref, m_in, l_in, acc_in, arr_ref, o_ref, kbuf, vbuf, m_sc, l_sc, acc_sc
 ):
     head = pl.program_id(0)
     rows, width = q_ref.shape
@@ -158,15 +178,9 @@
     lanes = pl.ds(pl.multiple_of(head * width, width), width)
     q = q_ref[...]
     dims = (((1,), (1,)), ((), ()))
-    scores = lax.dot_general(q, nk_ref[...], dims, preferred_element_type=jnp.float32) * score_scale
-    row_i = lax.broadcasted_iota(jnp.int32, (rows, rows), 0)
-    col_i = lax.broadcasted_iota(jnp.int32, (rows, rows), 1)
-    scores = jnp.where(col_i <= row_i, scores, -1e30)
-    peak = jnp.max(scores, axis=-1, keepdims=True)
-    weights = jnp.exp(scores - peak)
-    m_sc[...] = peak
-    l_sc[...] = jnp.sum(weights, axis=-1, keepdims=True)
-    acc_sc[...] = jnp.dot(weights.astype(jnp.bfloat16), nv_ref[...], preferred_element_type=jnp.float32)
+    m_sc[...] = m_in[...]
+    l_sc[...] = l_in[...]
+    acc_sc[...] = acc_in[...]
     length = len_ref[0]
     block_count = (length + block_len - 1) // block_len
 
@@ -195,27 +209,52 @@
     o_ref[...] = (acc_sc[...] / l_sc[...]).astype(o_ref.dtype)
 
 
+def fresh_attention(queries, new_keys, new_values):
+    rows, local_width = queries.shape
+    heads = local_width // HEAD_DIM
+    spec = pl.BlockSpec((rows, HEAD_DIM), lambda h: (0, h))
+    stat = pl.BlockSpec((None, rows, 1), lambda h: (h, 0, 0))
+    cost = pl.CostEstimate(
+        flops=4 * rows * rows * local_width,
+        transcendentals=rows * rows * heads,
+        bytes_accessed=3 * rows * local_width * 2 + rows * local_width * 4,
+    )
+    return pl.pallas_call(
+        fresh_kernel,
+        out_shape=(
+            jax.ShapeDtypeStruct((heads, rows, 1), jnp.float32),
+            jax.ShapeDtypeStruct((heads, rows, 1), jnp.float32),
+            jax.ShapeDtypeStruct((rows, local_width), jnp.float32),
+        ),
+        grid=(heads,),
+        in_specs=[spec, spec, spec],
+        out_specs=(stat, stat, pl.BlockSpec((rows, HEAD_DIM), lambda h: (0, h))),
+        cost_estimate=cost,
+    )(queries, new_keys, new_values)
+
+
 def paged_attention(slots, length, queries, new_keys, new_values, arrived, block_len):
     rows, local_width = queries.shape
     heads = local_width // HEAD_DIM
-    slot_count, _, page, _ = arrived.shape
-    column = lambda h, *_: (0, h)
-    spec = pl.BlockSpec((rows, HEAD_DIM), column)
+    peak, total, mixed = fresh_attention(queries, new_keys, new_values)
+    spec = pl.BlockSpec((rows, HEAD_DIM), lambda h, *_: (0, h))
+    stat = pl.BlockSpec((None, rows, 1), lambda h, *_: (h, 0, 0))
     cost = pl.CostEstimate(
-        flops=4 * rows * (rows + CTX) * local_width,
-        transcendentals=rows * (rows + CTX) * heads,
+        flops=4 * rows * CTX * local_width,
+        transcendentals=rows * CTX * heads,
         bytes_accessed=arrived.size * 2 + 4 * rows * local_width * 2,
     )
     return pl.pallas_call(
-        attention_kernel,
+        cache_kernel,
         out_shape=jax.ShapeDtypeStruct((rows, local_width), jnp.bfloat16),
         grid_spec=pltpu.PrefetchScalarGridSpec(
             num_scalar_prefetch=2,
             grid=(heads,),
             in_specs=[
                 spec,
-                spec,
-                spec,
+                stat,
+                stat,
+                pl.BlockSpec((rows, HEAD_DIM), lambda h, *_: (0, h)),
                 pl.BlockSpec(arrived.shape, lambda h, *_: (0, 0, 0, 0)),
             ],
             out_specs=spec,
@@ -229,7 +268,7 @@
         ),
         compiler_params=pltpu.CompilerParams(vmem_limit_bytes=48 * 1024 * 1024),
         cost_estimate=cost,
-    )(slots, length, queries, new_keys, new_values, arrived)
+    )(slots, length, queries, peak, total, mixed, arrived)
 
 
 def shards(

time: 230 us -> 235 us (1.022)
  Pallas kernels: 69 us -> 76 us
  waiting for transfers between devices: 78.5 us -> 73.1 us
  local copies, waits for them, and re-layouts: 14.1 us -> 19.3 us
    pallas_call x1 -> x2, Pallas kernels: 20.6 us -> 27.6 us  [the longest x1 24.3 us: paged_attention(): pl.pallas_call(cache_kernel, out_shape=jax.ShapeDtypeStruct((rows, local_...]
    all_to_all x1, waiting for transfers between devices: 54.8 us -> 49.3 us  [shards(): lax.all_to_all(outgoing, 'group', split_axis=0, concat_axis=0, tiled=True)]
    unnamed x19 -> x27, local copies, waits for them, and re-layouts: 5.03 us -> 8.16 us
  transfers between devices with their start and end apart: 2 -> 2, of which waited for: 2 -> 2; matrix products, arithmetic and copies ran while one was open for 6% -> 7% of each run, Pallas kernels for 0% -> 1%
where the time goes in v8:
time: 235 us; the launch traced here: 234 us
  Pallas kernels  76 us (32%)
  waiting for transfers between devices  73.1 us (31%)
  local copies, waits for them, and re-layouts  19.3 us (8%)
  other arithmetic  14.1 us (6%)
  matrix products  14.1 us (6%)
  between operations  13.7 us (6%)
  starting transfers between devices  12.2 us (5%)
  blocking collectives  11.4 us (5%)
    all_to_all x1, waiting for transfers between devices, shards(): lax.all_to_all(outgoing, 'group', split_axis=0, concat_axis=0, tiled=True)  49.3 us
    pallas_call x3, Pallas kernels, exchange(): pl.pallas_call(functools.partial(exchange_kernel, axes, split), out_shape...  48.3 us
    pallas_call x1, Pallas kernels, paged_attention(): pl.pallas_call(cache_kernel, out_shape=jax.ShapeDtypeStruct((rows, local_...  24.3 us
    all_gather x1, waiting for transfers between devices, shards(): lax.all_gather(normed, EXPERT, axis=0, tiled=True)  23.7 us
    all_to_all x1, starting transfers between devices, shards(): lax.all_to_all(outgoing, 'group', split_axis=0, concat_axis=0, tiled=True)  12.1 us
    all_to_all x1, blocking collectives, shards(): lax.all_to_all(head_parts, 'ec', split_axis=1, concat_axis=1, tiled=True)  11.4 us
    unnamed x27, local copies, waits for them, and re-layouts  8.16 us
    dot_general x1, matrix products, shards(): jnp.dot(hidden, w_down[0], preferred_element_type=jnp.float32)  4.92 us
  transfers between devices with their start and end apart: 2, of which 2 were waited for; matrix products, arithmetic and copies ran while one was open for 7% of the time, Pallas kernels for 1%

profile of v8, /device:TPU:1, one launch (start us, length us, event | category | flops | bytes accessed | tf_op | source)
XLA Modules:
  0.0 233.8 jit_solution(8589823465398370343)
XLA Ops:
  9.2 2.8 %gather_fusion = bf16[256,2,16,256]{3,2,1,0:T(8,128)(2,1)} fusion(bf16[128,2,16,256]{3,2,1,0:T(8,128)(2,1)S(1)} %copy-done, s32[1024]{0:T(1024)S(1)} %pad_clamp_fusion.1), kind=kCustom, calls=%fused_computation | custom fusion | bytes 8389632 | tf_op jit(solution)/shard_map/gather | solution.py:322
  12.0 12.1 %all-to-all-start = ((bf16[32,8,2,16,256]{4,3,2,1,0:T(8,128)(2,1)}), bf16[32,8,2,16,256]{4,3,2,1,0:T(8,128)(2,1)}, u32[]{:S(2)}, u32[]{:S(2)}) async-start(bf16[32,8,2,16,256]{4,3,2,1,0:T(8,128)(2,1)} %bitcast.60), calls=%async_computation | async-start | bytes 8388608 | tf_op jit(solution)/shard_map/all_to_all | solution.py:323
  25.2 4.8 %copy.35 = bf16[2048,3,256]{0,2,1:T(8,128)(2,1)} copy(bf16[2048,3,256]{2,0,1:T(8,128)(2,1)} %param.18) | data formatting | bytes 6291456 | tf_op args[5]
  33.0 23.7 %all-gather.2.cloned.1.call-done = bf16[512,2048]{1,0:T(8,128)(2,1)} async-done(((bf16[64,2048]{1,0:T(8,128)(2,1)}), bf16[512,2048]{1,0:T(8,128)(2,1)}) %all-gather.2.cloned.1.call-update) | async-done | bytes 2097168 | tf_op jit(solution)/shard_map/all_gather | solution.py:303
  56.7 4.3 %fusion = f32[512,3,2,128]{0,3,2,1:T(8,128)S(1)} fusion(bf16[3,2,128,2048]{3,2,1,0:T(8,128)(2,1)} %bitcast.63, bf16[512,2048]{1,0:T(8,128)(2,1)} %all-gather.2.cloned.1.call-done), kind=kOutput, calls=%fused_computation.5 | convolution fusion | flops 1610612736 | bytes 6815744 | tf_op jit(solution)/shard_map/dot_general | solution.py:302
  64.0 3.3 %shard_map.127 = (f32[2,512,1]{2,1,0:T(8,128)}, f32[2,512,1]{2,1,0:T(8,128)}, f32[512,256]{1,0:T(8,128)}) custom-call(bf16[512,256]{1,0:T(8,128)(2,1)} %copy.44.q_ref, bf16[512,256]{1,0:T(8,128)(2,1)} %copy.45.nk_ref, bf16[512,256]{1,0:T(8,128)(2,1)} %copy.46.nv_ref), custom_call_target="tpu_custom_call" | custom-call | flops 268435456 | bytes 1310720 | tf_op jit(solution)/shard_map/pallas_call | solution.py:222
  67.3 49.3 %all-to-all-done = bf16[32,8,2,16,256]{4,3,2,1,0:T(8,128)(2,1)} async-done(((bf16[32,8,2,16,256]{4,3,2,1,0:T(8,128)(2,1)}), bf16[32,8,2,16,256]{4,3,2,1,0:T(8,128)(2,1)}, u32[]{:S(2)}, u32[]{:S(2)}) %all-to-all-start) | async-done | bytes 4194336 | tf_op jit(solution)/shard_map/all_to_all | solution.py:323
  116.7 1.0 copy-done.2
  117.7 1.0 copy-done.3
  118.8 1.0 copy-done.4
  119.8 24.3 %shard_map.128 = bf16[512,256]{1,0:T(8,128)(2,1)S(1)} custom-call(s32[128]{0:T(128)S(1)} %multiply_add_fusion.1.slots_ref, s32[1]{0:T(128)} %dynamic_slice.7.len_ref, bf16[512,256]{1,0:T(8,128)(2,1)S(1)} %copy-done.1, f32[2,512,1]{2,1,0:T(8,128)S(1)} %copy-done.2, f32[2,512,1]{2,1,0:T(8,128)S(1)} %copy-done.3, f32[512,256]{1,0:T(8,128)S(1)} %copy-done.4, ...), custom_call_target="tpu_custom_call" | custom-call | flops 1073741824 | bytes 5242880 | tf_op jit(solution)/shard_map/pallas_call | solution.py:247
  145.1 11.4 %all_to_all.10 = bf16[4,2,64,2048]{3,2,0,1:T(8,128)(2,1)} all-to-all(bf16[4,2,64,2048]{3,2,0,1:T(8,128)(2,1)S(1)} %copy.39), channel_id=1, replica_groups=mesh['group'=32,'ey'=4,'ec'=2] {'ec'}, dimensions={1} | all-to-all | bytes 4194304 | tf_op jit(solution)/shard_map/all_to_all | solution.py:343
  156.5 3.3 %reduce_sum.92.x_ref = bf16[4,64,2048]{2,1,0:T(8,128)(2,1)} reduce(bf16[4,2,64,2048]{3,2,0,1:T(8,128)(2,1)} %all_to_all.10, bf16[]{:T(256)} %constant.78.clone.1), dimensions={1}, to_apply=%region_4.5 | reduce | flops 524288 | bytes 3145730 | tf_op jit(solution)/shard_map/reduce_sum | solution.py:344
  159.8 16.0 %shard_map.129 = bf16[4,64,2048]{2,1,0:T(8,128)(2,1)} custom-call(bf16[4,64,2048]{2,1,0:T(8,128)(2,1)} %reduce_sum.92.x_ref), custom_call_target="tpu_custom_call" | custom-call | tf_op jit(solution)/shard_map/pallas_call | solution.py:135
  175.8 1.4 convert_reduce_fusion
  177.5 1.5 convolution_convert_fusion.2
  179.0 16.7 %shard_map.130 = bf16[8,32,2048]{2,1,0:T(8,128)(2,1)} custom-call(bf16[8,32,2048]{2,1,0:T(8,128)(2,1)} %bitcast.62), custom_call_target="tpu_custom_call" | custom-call | tf_op jit(solution)/shard_map/pallas_call | solution.py:135
  195.7 2.6 %fusion.5 = f32[256,512]{1,0:T(8,128)S(1)} fusion(bf16[256,2048]{1,0:T(8,128)(2,1)} %bitcast.64, bf16[1,2048,512]{2,1,0:T(8,128)(2,1)} %param.21), kind=kOutput, calls=%fused_computation.10 | convolution fusion | flops 536870912 | bytes 3670016 | tf_op jit(solution)/shard_map/dot_general | solution.py:372
  198.3 4.9 %convolution_convert_fusion.1 = bf16[256,2048]{1,0:T(8,128)(2,1)} fusion(bf16[1,512,2048]{2,1,0:T(8,128)(2,1)} %param.23, bf16[256,2048]{1,0:T(8,128)(2,1)} %bitcast.65, bf16[1,2048,512]{2,1,0:T(8,128)(2,1)} %param.22, f32[256,512]{1,0:T(8,128)S(1)} %fusion.5), kind=kOutput, calls=%fused_computation.3 | convolution fusion | flops 1075052544 | bytes 6815744 | tf_op jit(solution)/shard_map/dot_general | solution.py:376
  203.2 15.6 %shard_map.131 = bf16[8,32,2048]{2,1,0:T(8,128)(2,1)} custom-call(bf16[8,32,2048]{2,1,0:T(8,128)(2,1)} %bitcast.66), custom_call_target="tpu_custom_call" | custom-call | tf_op jit(solution)/shard_map/pallas_call | solution.py:135
  218.9 2.8 %gather_fusion.1 = bf16[128,2048]{1,0:T(8,128)(2,1)S(1)} fusion(bf16[256,2048]{1,0:T(8,128)(2,1)} %bitcast.59, s32[1024]{0:T(1024)S(1)} %pad_clamp_fusion), kind=kCustom, calls=%fused_computation.1 | custom fusion | bytes 1049088 | tf_op jit(solution)/shard_map/gather | solution.py:381
  221.7 1.6 reshape.195
  223.3 2.8 %multiply_reduce_fusion = f32[64,2048]{1,0:T(8,128)S(1)} fusion(f32[64,2,2048]{2,1,0:T(2,128)} %reshape.195, f32[64,2]{1,0:T(8,128)S(1)} %copy.42), kind=kLoop, calls=%fused_computation.15 | loop fusion | flops 393216 | bytes 1573376 | tf_op jit(solution)/shard_map/reduce_sum | solution.py:384
  226.1 0.9 fusion.26
  (64 shorter events, 10.6 us)
Async XLA Ops:
  6.5 2.7 %copy-start = (bf16[128,2,16,256]{3,2,1,0:T(8,128)(2,1)S(1)}, bf16[128,2,16,256]{3,2,1,0:T(8,128)(2,1)}, u32[]{:S(2)}) copy-start(bf16[128,2,16,256]{3,2,1,0:T(8,128)(2,1)} %param.16) | copy-start | bytes 6291460
  12.0 12.2 %copy-start.5 = (bf16[64,2048]{1,0:T(8,128)(2,1)S(1)}, bf16[64,2048]{1,0:T(8,128)(2,1)}, u32[]{:S(2)}) copy-start(bf16[64,2048]{1,0:T(8,128)(2,1)} %param.13) | copy-start | bytes 786436
  12.0 12.4 %copy-start.7 = (f32[2048]{0:T(1024)S(1)}, f32[2048]{0:T(1024)}, u32[]{:S(2)}) copy-start(f32[2048]{0:T(1024)} %param.17) | copy-start | bytes 24580
  12.0 104.7 %all-to-all-start = ((bf16[32,8,2,16,256]{4,3,2,1,0:T(8,128)(2,1)}), bf16[32,8,2,16,256]{4,3,2,1,0:T(8,128)(2,1)}, u32[]{:S(2)}, u32[]{:S(2)}) async-start(bf16[32,8,2,16,256]{4,3,2,1,0:T(8,128)(2,1)} %bitcast.60), calls=%async_computation | async-start | bytes 8388608 | tf_op jit(solution)/shard_map/all_to_all | solution.py:323
  24.1 32.6 %all-gather.2.cloned.1.call-start = ((), (), s32[]{:S(2)}) async-start(), calls=%async_computation.2 | async-start | bytes 2359296 | tf_op jit(solution)/shard_map/all_gather | solution.py:303
  25.2 4.8 %copy-start.9 = (s32[64,2]{0,1:T(2,128)S(1)}, s32[64,2]{0,1:T(2,128)}, u32[]{:S(2)}) copy-start(s32[64,2]{0,1:T(2,128)} %param.24) | copy-start | bytes 1540
  25.2 5.3 %copy-start.10 = (f32[64,2]{0,1:T(2,128)S(1)}, f32[64,2]{0,1:T(2,128)}, u32[]{:S(2)}) copy-start(f32[64,2]{0,1:T(2,128)} %param.25) | copy-start | bytes 1540
  25.2 5.4 %copy-start.11 = (s32[32]{0:T(128)S(1)}, s32[32]{0:T(128)}, u32[]{:S(2)}) copy-start(s32[32]{0:T(128)} %param.14) | copy-start | bytes 388
  62.3 54.4 %copy-start.1 = (bf16[512,256]{1,0:T(8,128)(2,1)S(1)}, bf16[512,256]{1,0:T(8,128)(2,1)}, u32[]{:S(2)}) copy-start(bf16[512,256]{1,0:T(8,128)(2,1)} %copy.44.q_ref) | copy-start | bytes 786436
  116.7 1.0 copy-start.2
  117.7 1.0 copy-start.3
  118.8 1.0 copy-start.4
  119.8 24.3 %copy-start.6 = (bf16[256,2048]{1,0:T(8,128)(2,1)S(1)}, bf16[256,2048]{1,0:T(8,128)(2,1)}, u32[]{:S(2)}) copy-start(bf16[256,2048]{1,0:T(8,128)(2,1)} %param.19) | copy-start | bytes 3145732
  159.8 17.7 %copy-start.8 = (f32[2048]{0:T(1024)S(1)}, f32[2048]{0:T(1024)}, u32[]{:S(2)}) copy-start(f32[2048]{0:T(1024)} %param.20) | copy-start | bytes 24580
Sparse Core Ops, SparseCore 0:
  26.8 29.9 all-gather.1

commit v9 on v7

--- a/solution.py
+++ b/solution.py
@@ -296,14 +296,14 @@
         arrived,
         block_len,
     )
-    rows_piece = attended
-    head_parts = jnp.dot(rows_piece, w_out, preferred_element_type=jnp.float32).astype(jnp.bfloat16)
-    chips = lax.axis_size("ey")
-    cores = lax.axis_size("ec")
-    head_parts = head_parts.reshape(chips, cores, tok_rows, model_width)
-    head_parts = lax.all_to_all(head_parts, "ec", split_axis=1, concat_axis=1, tiled=True)
-    head_parts = jnp.sum(head_parts.astype(jnp.float32), axis=1).astype(jnp.bfloat16)
-    head_parts = exchange(head_parts, ("ey",), 2)
+    head_weights = lax.all_gather(w_out, EXPERT, axis=0, tiled=True)
+    head_weights = head_weights.reshape(expert_lanes, local_width, model_width)
+    rows_piece = lax.all_to_all(
+        attended.reshape(expert_lanes, tok_rows, local_width), EXPERT, 0, 0, tiled=True
+    )
+    head_parts = jnp.einsum(
+        "gtc,gcd->gtd", rows_piece, head_weights, preferred_element_type=jnp.float32
+    ).astype(jnp.bfloat16)
     head_sum = jnp.sum(head_parts.astype(jnp.float32), axis=0)
     residual = hidden_in.astype(jnp.float32) + head_sum
     moe_in = norm_rows(residual, moe_gain)

time: 230 us -> 219 us (0.952)
  the two profiles are of different devices: /device:TPU:1 before, /device:TPU:99 now
where the time goes in v9:
time: 219 us
  waiting for transfers between devices  89.4 us (41%)
  Pallas kernels  58.5 us (27%)
  matrix products  18.4 us (8%)
  starting transfers between devices  15 us (7%)
  local copies, waits for them, and re-layouts  13.8 us (6%)
  between operations  13.7 us (6%)
  other arithmetic  9.87 us (5%)
    all_to_all x1, waiting for transfers between devices, shards(): lax.all_to_all(outgoing, 'group', split_axis=0, concat_axis=0, tiled=True)  74.2 us
    pallas_call x2, Pallas kernels, exchange(): pl.pallas_call(functools.partial(exchange_kernel, axes, split), out_shape...  32.2 us
    pallas_call x1, Pallas kernels, paged_attention(): pl.pallas_call(attention_kernel, out_shape=jax.ShapeDtypeStruct((rows, lo...  26.3 us
    all_to_all x1, starting transfers between devices, shards(): lax.all_to_all(outgoing, 'group', split_axis=0, concat_axis=0, tiled=True)  9.75 us
    all_gather x1, waiting for transfers between devices, shards(): lax.all_gather(normed, EXPERT, axis=0, tiled=True)  8.35 us
    all_to_all x1, waiting for transfers between devices, shards(): lax.all_to_all(attended.reshape(expert_lanes, tok_rows, local_width), EXP...  6.12 us
    all_to_all x1, starting transfers between devices, shards(): lax.all_to_all(attended.reshape(expert_lanes, tok_rows, local_width), EXP...  5.2 us
    dot_general x1, matrix products, shards(): jnp.einsum('gtc,gcd->gtd', rows_piece, head_weights, preferred_element_ty...  5.02 us
  transfers between devices with their start and end apart: 4, of which 3 were waited for; matrix products, arithmetic and copies ran while one was open for 8% of the time, Pallas kernels for 12%

profile of v9, /device:TPU:99, one launch (start us, length us, event | category | flops | bytes accessed | tf_op | source)
XLA Modules:
  0.0 218.7 jit_solution(14939812065940578622)
XLA Ops:
  6.5 1.3 fusion.15
  7.8 1.8 fusion.17
  9.7 0.7 all-gather.5.cloned.1.call-update
  11.5 2.8 %gather_fusion = bf16[256,2,16,256]{3,2,1,0:T(8,128)(2,1)} fusion(bf16[128,2,16,256]{3,2,1,0:T(8,128)(2,1)S(1)} %copy-done, s32[1024]{0:T(1024)S(1)} %pad_clamp_fusion.1), kind=kCustom, calls=%fused_computation | custom fusion | bytes 8389632 | tf_op jit(solution)/shard_map/gather | solution.py:283
  14.3 9.8 %all-to-all-start = ((bf16[32,8,2,16,256]{4,3,2,1,0:T(8,128)(2,1)}), bf16[32,8,2,16,256]{4,3,2,1,0:T(8,128)(2,1)}, u32[]{:S(2)}, u32[]{:S(2)}) async-start(bf16[32,8,2,16,256]{4,3,2,1,0:T(8,128)(2,1)} %bitcast.62), calls=%async_computation | async-start | bytes 8388608 | tf_op jit(solution)/shard_map/all_to_all | solution.py:284
  24.1 4.7 %copy.27 = bf16[2048,3,256]{0,2,1:T(8,128)(2,1)} copy(bf16[2048,3,256]{2,0,1:T(8,128)(2,1)} %param.18) | data formatting | bytes 6291456 | tf_op args[5]
  29.3 0.7 dynamic_slice.7.len_ref
  30.0 0.6 add_convert_fusion.2
  31.6 8.4 %all-gather.3.cloned.1.call-done = bf16[512,2048]{1,0:T(8,128)(2,1)} async-done(((bf16[64,2048]{1,0:T(8,128)(2,1)}), bf16[512,2048]{1,0:T(8,128)(2,1)}) %all-gather.3.cloned.1.call-update) | async-done | bytes 2097168 | tf_op jit(solution)/shard_map/all_gather | solution.py:264
  39.9 4.3 %fusion = f32[512,3,2,128]{0,3,2,1:T(8,128)S(1)} fusion(bf16[3,2,128,2048]{3,2,1,0:T(8,128)(2,1)} %bitcast.64, bf16[512,2048]{1,0:T(8,128)(2,1)} %all-gather.3.cloned.1.call-done), kind=kOutput, calls=%fused_computation.6 | convolution fusion | flops 1610612736 | bytes 6815744 | tf_op jit(solution)/shard_map/dot_general | solution.py:263
  45.0 74.2 %all-to-all-done = bf16[32,8,2,16,256]{4,3,2,1,0:T(8,128)(2,1)} async-done(((bf16[32,8,2,16,256]{4,3,2,1,0:T(8,128)(2,1)}), bf16[32,8,2,16,256]{4,3,2,1,0:T(8,128)(2,1)}, u32[]{:S(2)}, u32[]{:S(2)}) %all-to-all-start) | async-done | bytes 4194336 | tf_op jit(solution)/shard_map/all_to_all | solution.py:284
  119.3 26.3 %shard_map.127 = bf16[512,256]{1,0:T(8,128)(2,1)} custom-call(s32[128]{0:T(128)S(1)} %multiply_add_fusion.1.slots_ref, s32[1]{0:T(128)} %dynamic_slice.7.len_ref, bf16[512,256]{1,0:T(8,128)(2,1)S(1)} %copy.35.q_ref, bf16[512,256]{1,0:T(8,128)(2,1)S(1)} %copy.36.nk_ref, bf16[512,256]{1,0:T(8,128)(2,1)S(1)} %copy.37.nv_ref, ...), custom_call_target="tpu_custom_call" | custom-call | flops 1342177280 | bytes 5242880 | tf_op jit(solution)/shard_map/pallas_call | solution.py:209
  145.6 5.2 %all-to-all-start.1 = ((bf16[8,64,256]{2,1,0:T(8,128)(2,1)}), bf16[8,64,256]{2,1,0:T(8,128)(2,1)S(1)}, u32[]{:S(2)}, u32[]{:S(2)}) async-start(bf16[8,64,256]{2,1,0:T(8,128)(2,1)} %bitcast.15), calls=%async_computation.1 | async-start | bytes 524288 | tf_op jit(solution)/shard_map/all_to_all | solution.py:301
  151.1 6.1 %all-to-all-done.1 = bf16[8,64,256]{2,1,0:T(8,128)(2,1)S(1)} async-done(((bf16[8,64,256]{2,1,0:T(8,128)(2,1)}), bf16[8,64,256]{2,1,0:T(8,128)(2,1)S(1)}, u32[]{:S(2)}, u32[]{:S(2)}) %all-to-all-start.1) | async-done | bytes 262176 | tf_op jit(solution)/shard_map/all_to_all | solution.py:301
  157.2 5.0 %convert_reduce_fusion = f32[64,2048]{1,0:T(8,128)S(1)} fusion(bf16[8,64,256]{2,1,0:T(8,128)(2,1)S(1)} %all-to-all-done.1, bf16[8,256,2048]{2,1,0:T(8,128)(2,1)} %bitcast.61), kind=kOutput, calls=%fused_computation.2 | convolution fusion | flops 539885568 | bytes 9175040 | tf_op jit(solution)/shard_map/gtc,gcd->gtd/dot_general | solution.py:304
  162.5 1.5 convolution_convert_fusion.2
  164.0 16.6 %shard_map.128 = bf16[8,32,2048]{2,1,0:T(8,128)(2,1)} custom-call(bf16[8,32,2048]{2,1,0:T(8,128)(2,1)} %bitcast.63), custom_call_target="tpu_custom_call" | custom-call | tf_op jit(solution)/shard_map/pallas_call | solution.py:135
  180.6 2.6 %fusion.5 = f32[256,512]{1,0:T(8,128)S(1)} fusion(bf16[256,2048]{1,0:T(8,128)(2,1)} %bitcast.65, bf16[1,2048,512]{2,1,0:T(8,128)(2,1)} %param.21), kind=kOutput, calls=%fused_computation.11 | convolution fusion | flops 536870912 | bytes 3670016 | tf_op jit(solution)/shard_map/dot_general | solution.py:333
  183.2 4.9 %convolution_convert_fusion.1 = bf16[256,2048]{1,0:T(8,128)(2,1)} fusion(bf16[1,512,2048]{2,1,0:T(8,128)(2,1)} %param.23, bf16[256,2048]{1,0:T(8,128)(2,1)} %bitcast.66, bf16[1,2048,512]{2,1,0:T(8,128)(2,1)} %param.22, f32[256,512]{1,0:T(8,128)S(1)} %fusion.5), kind=kOutput, calls=%fused_computation.4 | convolution fusion | flops 1075052544 | bytes 6815744 | tf_op jit(solution)/shard_map/dot_general | solution.py:337
  188.1 15.6 %shard_map.129 = bf16[8,32,2048]{2,1,0:T(8,128)(2,1)} custom-call(bf16[8,32,2048]{2,1,0:T(8,128)(2,1)} %bitcast.67), custom_call_target="tpu_custom_call" | custom-call | tf_op jit(solution)/shard_map/pallas_call | solution.py:135
  203.7 2.8 %gather_fusion.1 = bf16[128,2048]{1,0:T(8,128)(2,1)S(1)} fusion(bf16[256,2048]{1,0:T(8,128)(2,1)} %bitcast.60, s32[1024]{0:T(1024)S(1)} %pad_clamp_fusion), kind=kCustom, calls=%fused_computation.1 | custom fusion | bytes 1049088 | tf_op jit(solution)/shard_map/gather | solution.py:342
  206.6 1.6 reshape.199
  208.2 2.8 %multiply_reduce_fusion = f32[64,2048]{1,0:T(8,128)S(1)} fusion(f32[64,2,2048]{2,1,0:T(2,128)} %reshape.199, f32[64,2]{1,0:T(8,128)S(1)} %copy.33), kind=kLoop, calls=%fused_computation.15 | loop fusion | flops 393216 | bytes 1573376 | tf_op jit(solution)/shard_map/reduce_sum | solution.py:345
  211.0 0.9 fusion.26
  (53 shorter events, 3.8 us)
Async XLA Ops:
  6.5 4.9 %copy-start = (bf16[128,2,16,256]{3,2,1,0:T(8,128)(2,1)S(1)}, bf16[128,2,16,256]{3,2,1,0:T(8,128)(2,1)}, u32[]{:S(2)}) copy-start(bf16[128,2,16,256]{3,2,1,0:T(8,128)(2,1)} %param.16) | copy-start | bytes 6291460
  6.5 3.9 %copy-start.2 = (s32[32,128]{1,0:T(8,128)S(1)}, s32[32,128]{1,0:T(8,128)}, u32[]{:S(2)}) copy-start(s32[32,128]{1,0:T(8,128)} %param.15) | copy-start | bytes 49156
  6.5 33.4 %all-gather.3.cloned.1.call-start = ((), (), s32[]{:S(2)}) async-start(), calls=%async_computation.2 | async-start | bytes 2359296 | tf_op jit(solution)/shard_map/all_gather | solution.py:264
  9.6 147.6 %all-gather.5.cloned.1.call-start = ((), (), s32[]{:S(2)}) async-start(), calls=%async_computation.3 | async-start | bytes 9437184 | tf_op jit(solution)/shard_map/all_gather | solution.py:299
  14.3 105.0 %all-to-all-start = ((bf16[32,8,2,16,256]{4,3,2,1,0:T(8,128)(2,1)}), bf16[32,8,2,16,256]{4,3,2,1,0:T(8,128)(2,1)}, u32[]{:S(2)}, u32[]{:S(2)}) async-start(bf16[32,8,2,16,256]{4,3,2,1,0:T(8,128)(2,1)} %bitcast.62), calls=%async_computation | async-start | bytes 8388608 | tf_op jit(solution)/shard_map/all_to_all | solution.py:284
  24.0 4.8 %copy-start.4 = (s32[64,2]{0,1:T(2,128)S(1)}, s32[64,2]{0,1:T(2,128)}, u32[]{:S(2)}) copy-start(s32[64,2]{0,1:T(2,128)} %param.24) | copy-start | bytes 1540
  24.0 5.2 %copy-start.6 = (s32[32]{0:T(128)S(1)}, s32[32]{0:T(128)}, u32[]{:S(2)}) copy-start(s32[32]{0:T(128)} %param.14) | copy-start | bytes 388
  119.3 31.5 %copy-start.5 = (f32[64,2]{0,1:T(2,128)S(1)}, f32[64,2]{0,1:T(2,128)}, u32[]{:S(2)}) copy-start(f32[64,2]{0,1:T(2,128)} %param.25) | copy-start | bytes 1540
  145.6 11.7 %all-to-all-start.1 = ((bf16[8,64,256]{2,1,0:T(8,128)(2,1)}), bf16[8,64,256]{2,1,0:T(8,128)(2,1)S(1)}, u32[]{:S(2)}, u32[]{:S(2)}) async-start(bf16[8,64,256]{2,1,0:T(8,128)(2,1)} %bitcast.15), calls=%async_computation.1 | async-start | bytes 524288 | tf_op jit(solution)/shard_map/all_to_all | solution.py:301
  157.2 5.0 %copy-start.1 = (bf16[64,2048]{1,0:T(8,128)(2,1)S(1)}, bf16[64,2048]{1,0:T(8,128)(2,1)}, u32[]{:S(2)}) copy-start(bf16[64,2048]{1,0:T(8,128)(2,1)} %param.13) | copy-start | bytes 786436
  157.2 5.2 %copy-start.3 = (f32[2048]{0:T(1024)S(1)}, f32[2048]{0:T(1024)}, u32[]{:S(2)}) copy-start(f32[2048]{0:T(1024)} %param.20) | copy-start | bytes 24580
Sparse Core Ops, SparseCore 0:
  9.8 30.1 all-gather.2
  41.8 52.6 all-gather.4

commit v10 on v9

--- a/solution.py
+++ b/solution.py
@@ -298,9 +298,7 @@
     )
     head_weights = lax.all_gather(w_out, EXPERT, axis=0, tiled=True)
     head_weights = head_weights.reshape(expert_lanes, local_width, model_width)
-    rows_piece = lax.all_to_all(
-        attended.reshape(expert_lanes, tok_rows, local_width), EXPERT, 0, 0, tiled=True
-    )
+    rows_piece = exchange(attended.reshape(expert_lanes, tok_rows, local_width), EXPERT, 2)
     head_parts = jnp.einsum(
         "gtc,gcd->gtd", rows_piece, head_weights, preferred_element_type=jnp.float32
     ).astype(jnp.bfloat16)

time: 219 us -> 220 us (level)
  the two profiles are of different devices: /device:TPU:99 before, /device:TPU:1 now
where the time goes in v10:
time: 220 us
  waiting for transfers between devices  80.3 us (36%)
  Pallas kernels  70.8 us (32%)
  matrix products  18.5 us (8%)
  local copies, waits for them, and re-layouts  14.5 us (7%)
  between operations  13.7 us (6%)
  starting transfers between devices  12 us (5%)
  other arithmetic  9.87 us (4%)
    all_to_all x1, waiting for transfers between devices, shards(): lax.all_to_all(outgoing, 'group', split_axis=0, concat_axis=0, tiled=True)  71.8 us
    pallas_call x3, Pallas kernels, exchange(): pl.pallas_call(functools.partial(exchange_kernel, axes, split), out_shape...  44.9 us
    pallas_call x1, Pallas kernels, paged_attention(): pl.pallas_call(attention_kernel, out_shape=jax.ShapeDtypeStruct((rows, lo...  25.8 us
    all_to_all x1, starting transfers between devices, shards(): lax.all_to_all(outgoing, 'group', split_axis=0, concat_axis=0, tiled=True)  12 us
    all_gather x1, waiting for transfers between devices, shards(): lax.all_gather(normed, EXPERT, axis=0, tiled=True)  7.73 us
    unnamed x19, local copies, waits for them, and re-layouts  5.7 us
    dot_general x1, matrix products, shards(): jnp.einsum('gtc,gcd->gtd', rows_piece, head_weights, preferred_element_ty...  5.12 us
    dot_general x1, matrix products, shards(): jnp.dot(hidden, w_down[0], preferred_element_type=jnp.float32)  4.92 us
  transfers between devices with their start and end apart: 3, of which 2 were waited for; matrix products, arithmetic and copies ran while one was open for 8% of the time, Pallas kernels for 18%

profile of v10, /device:TPU:1, one launch (start us, length us, event | category | flops | bytes accessed | tf_op | source)
XLA Modules:
  0.0 219.7 jit_solution(8642271047514064296)
XLA Ops:
  6.5 1.3 fusion.15
  7.8 1.8 fusion.17
  9.7 0.7 all-gather.5.cloned.1.call-update
  11.5 2.8 %gather_fusion = bf16[256,2,16,256]{3,2,1,0:T(8,128)(2,1)} fusion(bf16[128,2,16,256]{3,2,1,0:T(8,128)(2,1)S(1)} %copy-done, s32[1024]{0:T(1024)S(1)} %pad_clamp_fusion.1), kind=kCustom, calls=%fused_computation | custom fusion | bytes 8389632 | tf_op jit(solution)/shard_map/gather | solution.py:283
  14.3 12.0 %all-to-all-start = ((bf16[32,8,2,16,256]{4,3,2,1,0:T(8,128)(2,1)}), bf16[32,8,2,16,256]{4,3,2,1,0:T(8,128)(2,1)}, u32[]{:S(2)}, u32[]{:S(2)}) async-start(bf16[32,8,2,16,256]{4,3,2,1,0:T(8,128)(2,1)} %bitcast.63), calls=%async_computation | async-start | bytes 8388608 | tf_op jit(solution)/shard_map/all_to_all | solution.py:284
  26.3 4.8 %copy.27 = bf16[2048,3,256]{0,2,1:T(8,128)(2,1)} copy(bf16[2048,3,256]{2,0,1:T(8,128)(2,1)} %param.18) | data formatting | bytes 6291456 | tf_op args[5]
  31.7 0.7 dynamic_slice.7.len_ref
  32.3 0.6 add_convert_fusion.2
  34.2 7.7 %all-gather.3.cloned.1.call-done = bf16[512,2048]{1,0:T(8,128)(2,1)} async-done(((bf16[64,2048]{1,0:T(8,128)(2,1)}), bf16[512,2048]{1,0:T(8,128)(2,1)}) %all-gather.3.cloned.1.call-update) | async-done | bytes 2097168 | tf_op jit(solution)/shard_map/all_gather | solution.py:264
  41.9 4.3 %fusion = f32[512,3,2,128]{0,3,2,1:T(8,128)S(1)} fusion(bf16[3,2,128,2048]{3,2,1,0:T(8,128)(2,1)} %bitcast.65, bf16[512,2048]{1,0:T(8,128)(2,1)} %all-gather.3.cloned.1.call-done), kind=kOutput, calls=%fused_computation.6 | convolution fusion | flops 1610612736 | bytes 6815744 | tf_op jit(solution)/shard_map/dot_general | solution.py:263
  47.0 71.8 %all-to-all-done = bf16[32,8,2,16,256]{4,3,2,1,0:T(8,128)(2,1)} async-done(((bf16[32,8,2,16,256]{4,3,2,1,0:T(8,128)(2,1)}), bf16[32,8,2,16,256]{4,3,2,1,0:T(8,128)(2,1)}, u32[]{:S(2)}, u32[]{:S(2)}) %all-to-all-start) | async-done | bytes 4194336 | tf_op jit(solution)/shard_map/all_to_all | solution.py:284
  118.8 25.8 %shard_map.127 = bf16[512,256]{1,0:T(8,128)(2,1)S(1)} custom-call(s32[128]{0:T(128)S(1)} %multiply_add_fusion.1.slots_ref, s32[1]{0:T(128)} %dynamic_slice.7.len_ref, bf16[512,256]{1,0:T(8,128)(2,1)S(1)} %copy.35.q_ref, bf16[512,256]{1,0:T(8,128)(2,1)S(1)} %copy.36.nk_ref, bf16[512,256]{1,0:T(8,128)(2,1)S(1)} %copy.37.nv_ref, ...), custom_call_target="tpu_custom_call" | custom-call | flops 1342177280 | bytes 5242880 | tf_op jit(solution)/shard_map/pallas_call | solution.py:209
  144.7 0.7 copy-done.1
  145.4 13.4 %shard_map.128 = bf16[8,64,256]{2,1,0:T(8,128)(2,1)} custom-call(bf16[8,64,256]{2,1,0:T(8,128)(2,1)} %bitcast.60), custom_call_target="tpu_custom_call" | custom-call | tf_op jit(solution)/shard_map/pallas_call | solution.py:135
  158.9 5.1 %convert_reduce_fusion = f32[64,2048]{1,0:T(8,128)S(1)} fusion(bf16[8,64,256]{2,1,0:T(8,128)(2,1)} %shard_map.128, bf16[8,256,2048]{2,1,0:T(8,128)(2,1)} %bitcast.62), kind=kOutput, calls=%fused_computation.2 | convolution fusion | flops 539885568 | bytes 9175040 | tf_op jit(solution)/shard_map/gtc,gcd->gtd/dot_general | solution.py:302
  164.2 1.5 convolution_convert_fusion.2
  165.7 15.9 %shard_map.129 = bf16[8,32,2048]{2,1,0:T(8,128)(2,1)} custom-call(bf16[8,32,2048]{2,1,0:T(8,128)(2,1)} %bitcast.64), custom_call_target="tpu_custom_call" | custom-call | tf_op jit(solution)/shard_map/pallas_call | solution.py:135
  181.6 2.6 %fusion.5 = f32[256,512]{1,0:T(8,128)S(1)} fusion(bf16[256,2048]{1,0:T(8,128)(2,1)} %bitcast.66, bf16[1,2048,512]{2,1,0:T(8,128)(2,1)} %param.21), kind=kOutput, calls=%fused_computation.11 | convolution fusion | flops 536870912 | bytes 3670016 | tf_op jit(solution)/shard_map/dot_general | solution.py:331
  184.2 4.9 %convolution_convert_fusion.1 = bf16[256,2048]{1,0:T(8,128)(2,1)} fusion(bf16[1,512,2048]{2,1,0:T(8,128)(2,1)} %param.23, bf16[256,2048]{1,0:T(8,128)(2,1)} %bitcast.67, bf16[1,2048,512]{2,1,0:T(8,128)(2,1)} %param.22, f32[256,512]{1,0:T(8,128)S(1)} %fusion.5), kind=kOutput, calls=%fused_computation.4 | convolution fusion | flops 1075052544 | bytes 6815744 | tf_op jit(solution)/shard_map/dot_general | solution.py:335
  189.1 15.6 %shard_map.130 = bf16[8,32,2048]{2,1,0:T(8,128)(2,1)} custom-call(bf16[8,32,2048]{2,1,0:T(8,128)(2,1)} %bitcast.68), custom_call_target="tpu_custom_call" | custom-call | tf_op jit(solution)/shard_map/pallas_call | solution.py:135
  204.8 2.8 %gather_fusion.1 = bf16[128,2048]{1,0:T(8,128)(2,1)S(1)} fusion(bf16[256,2048]{1,0:T(8,128)(2,1)} %bitcast.61, s32[1024]{0:T(1024)S(1)} %pad_clamp_fusion), kind=kCustom, calls=%fused_computation.1 | custom fusion | bytes 1049088 | tf_op jit(solution)/shard_map/gather | solution.py:340
  207.6 1.6 reshape.199
  209.2 2.8 %multiply_reduce_fusion = f32[64,2048]{1,0:T(8,128)S(1)} fusion(f32[64,2,2048]{2,1,0:T(2,128)} %reshape.199, f32[64,2]{1,0:T(8,128)S(1)} %copy.33), kind=kLoop, calls=%fused_computation.15 | loop fusion | flops 393216 | bytes 1573376 | tf_op jit(solution)/shard_map/reduce_sum | solution.py:343
  212.0 0.9 fusion.26
  (54 shorter events, 3.8 us)
Async XLA Ops:
  6.5 4.9 %copy-start = (bf16[128,2,16,256]{3,2,1,0:T(8,128)(2,1)S(1)}, bf16[128,2,16,256]{3,2,1,0:T(8,128)(2,1)}, u32[]{:S(2)}) copy-start(bf16[128,2,16,256]{3,2,1,0:T(8,128)(2,1)} %param.16) | copy-start | bytes 6291460
  6.5 3.9 %copy-start.3 = (s32[32,128]{1,0:T(8,128)S(1)}, s32[32,128]{1,0:T(8,128)}, u32[]{:S(2)}) copy-start(s32[32,128]{1,0:T(8,128)} %param.15) | copy-start | bytes 49156
  6.5 35.4 %all-gather.3.cloned.1.call-start = ((), (), s32[]{:S(2)}) async-start(), calls=%async_computation.1 | async-start | bytes 2359296 | tf_op jit(solution)/shard_map/all_gather | solution.py:264
  9.6 149.2 %all-gather.5.cloned.1.call-start = ((), (), s32[]{:S(2)}) async-start(), calls=%async_computation.2 | async-start | bytes 9437184 | tf_op jit(solution)/shard_map/all_gather | solution.py:299
  14.3 104.5 %all-to-all-start = ((bf16[32,8,2,16,256]{4,3,2,1,0:T(8,128)(2,1)}), bf16[32,8,2,16,256]{4,3,2,1,0:T(8,128)(2,1)}, u32[]{:S(2)}, u32[]{:S(2)}) async-start(bf16[32,8,2,16,256]{4,3,2,1,0:T(8,128)(2,1)} %bitcast.63), calls=%async_computation | async-start | bytes 8388608 | tf_op jit(solution)/shard_map/all_to_all | solution.py:284
  26.3 4.8 %copy-start.5 = (s32[64,2]{0,1:T(2,128)S(1)}, s32[64,2]{0,1:T(2,128)}, u32[]{:S(2)}) copy-start(s32[64,2]{0,1:T(2,128)} %param.24) | copy-start | bytes 1540
  26.3 5.3 %copy-start.6 = (f32[64,2]{0,1:T(2,128)S(1)}, f32[64,2]{0,1:T(2,128)}, u32[]{:S(2)}) copy-start(f32[64,2]{0,1:T(2,128)} %param.25) | copy-start | bytes 1540
  26.3 5.4 %copy-start.7 = (s32[32]{0:T(128)S(1)}, s32[32]{0:T(128)}, u32[]{:S(2)}) copy-start(s32[32]{0:T(128)} %param.14) | copy-start | bytes 388
  144.6 0.7 copy-start.1
  158.8 5.2 %copy-start.2 = (bf16[64,2048]{1,0:T(8,128)(2,1)S(1)}, bf16[64,2048]{1,0:T(8,128)(2,1)}, u32[]{:S(2)}) copy-start(bf16[64,2048]{1,0:T(8,128)(2,1)} %param.13) | copy-start | bytes 786436
  158.8 5.3 %copy-start.4 = (f32[2048]{0:T(1024)S(1)}, f32[2048]{0:T(1024)}, u32[]{:S(2)}) copy-start(f32[2048]{0:T(1024)} %param.20) | copy-start | bytes 24580
Sparse Core Ops, SparseCore 0:
  9.8 32.0 all-gather.2
  43.7 52.5 all-gather.4

commit v11 on v9

--- a/solution.py
+++ b/solution.py
@@ -11,7 +11,7 @@
 EXPERT = ("ey", "ec")
 MESH_AXES = ("group", "ey", "ec")
 MESH_IDS = pl.DeviceIdType.MESH
-NBLK = 8
+NBLK = 4
 CTX = 2048
 
 

time: 219 us -> 211 us (0.963)
  the two profiles are of different devices: /device:TPU:99 before, /device:TPU:1 now
where the time goes in v11:
time: 211 us; the launch traced here: 208 us
  waiting for transfers between devices  86.7 us (41%)
  Pallas kernels  43.5 us (21%)
  starting transfers between devices  21.9 us (10%)
  matrix products  18.4 us (9%)
  local copies, waits for them, and re-layouts  13.8 us (7%)
  between operations  13.7 us (6%)
  other arithmetic  9.87 us (5%)
    all_to_all x1, waiting for transfers between devices, shards(): lax.all_to_all(outgoing, 'group', split_axis=0, concat_axis=0, tiled=True)  71.9 us
    pallas_call x2, Pallas kernels, exchange(): pl.pallas_call(functools.partial(exchange_kernel, axes, split), out_shape...  32.2 us
    all_to_all x1, starting transfers between devices, shards(): lax.all_to_all(outgoing, 'group', split_axis=0, concat_axis=0, tiled=True)  12 us
    pallas_call x1, Pallas kernels, paged_attention(): pl.pallas_call(attention_kernel, out_shape=jax.ShapeDtypeStruct((rows, lo...  11.3 us
    all_to_all x1, starting transfers between devices, shards(): lax.all_to_all(attended.reshape(expert_lanes, tok_rows, local_width), EXP...  9.87 us
    all_gather x1, waiting for transfers between devices, shards(): lax.all_gather(normed, EXPERT, axis=0, tiled=True)  8.02 us
    all_to_all x1, waiting for transfers between devices, shards(): lax.all_to_all(attended.reshape(expert_lanes, tok_rows, local_width), EXP...  6.12 us
    dot_general x1, matrix products, shards(): jnp.einsum('gtc,gcd->gtd', rows_piece, head_weights, preferred_element_ty...  5.02 us
  transfers between devices with their start and end apart: 4, of which 3 were waited for; matrix products, arithmetic and copies ran while one was open for 8% of the time, Pallas kernels for 5%

profile of v11, /device:TPU:1, one launch (start us, length us, event | category | flops | bytes accessed | tf_op | source)
XLA Modules:
  0.0 207.9 jit_solution(784732708269442777)
XLA Ops:
  6.5 1.3 fusion.15
  7.8 1.8 fusion.17
  9.7 0.7 all-gather.5.cloned.1.call-update
  11.5 2.8 %gather_fusion = bf16[256,2,16,256]{3,2,1,0:T(8,128)(2,1)} fusion(bf16[128,2,16,256]{3,2,1,0:T(8,128)(2,1)S(1)} %copy-done, s32[1024]{0:T(1024)S(1)} %pad_clamp_fusion.1), kind=kCustom, calls=%fused_computation | custom fusion | bytes 8389632 | tf_op jit(solution)/shard_map/gather | solution.py:283
  14.3 12.0 %all-to-all-start = ((bf16[32,8,2,16,256]{4,3,2,1,0:T(8,128)(2,1)}), bf16[32,8,2,16,256]{4,3,2,1,0:T(8,128)(2,1)}, u32[]{:S(2)}, u32[]{:S(2)}) async-start(bf16[32,8,2,16,256]{4,3,2,1,0:T(8,128)(2,1)} %bitcast.62), calls=%async_computation | async-start | bytes 8388608 | tf_op jit(solution)/shard_map/all_to_all | solution.py:284
  26.3 4.8 %copy.27 = bf16[2048,3,256]{0,2,1:T(8,128)(2,1)} copy(bf16[2048,3,256]{2,0,1:T(8,128)(2,1)} %param.18) | data formatting | bytes 6291456 | tf_op args[5]
  31.5 0.7 dynamic_slice.7.len_ref
  32.2 0.6 add_convert_fusion.2
  33.8 8.0 %all-gather.3.cloned.1.call-done = bf16[512,2048]{1,0:T(8,128)(2,1)} async-done(((bf16[64,2048]{1,0:T(8,128)(2,1)}), bf16[512,2048]{1,0:T(8,128)(2,1)}) %all-gather.3.cloned.1.call-update) | async-done | bytes 2097168 | tf_op jit(solution)/shard_map/all_gather | solution.py:264
  41.8 4.3 %fusion = f32[512,3,2,128]{0,3,2,1:T(8,128)S(1)} fusion(bf16[3,2,128,2048]{3,2,1,0:T(8,128)(2,1)} %bitcast.64, bf16[512,2048]{1,0:T(8,128)(2,1)} %all-gather.3.cloned.1.call-done), kind=kOutput, calls=%fused_computation.6 | convolution fusion | flops 1610612736 | bytes 6815744 | tf_op jit(solution)/shard_map/dot_general | solution.py:263
  46.9 71.9 %all-to-all-done = bf16[32,8,2,16,256]{4,3,2,1,0:T(8,128)(2,1)} async-done(((bf16[32,8,2,16,256]{4,3,2,1,0:T(8,128)(2,1)}), bf16[32,8,2,16,256]{4,3,2,1,0:T(8,128)(2,1)}, u32[]{:S(2)}, u32[]{:S(2)}) %all-to-all-start) | async-done | bytes 4194336 | tf_op jit(solution)/shard_map/all_to_all | solution.py:284
  118.8 11.3 %shard_map.127 = bf16[512,256]{1,0:T(8,128)(2,1)} custom-call(s32[128]{0:T(128)S(1)} %multiply_add_fusion.1.slots_ref, s32[1]{0:T(128)} %dynamic_slice.7.len_ref, bf16[512,256]{1,0:T(8,128)(2,1)S(1)} %copy.35.q_ref, bf16[512,256]{1,0:T(8,128)(2,1)S(1)} %copy.36.nk_ref, bf16[512,256]{1,0:T(8,128)(2,1)S(1)} %copy.37.nv_ref, ...), custom_call_target="tpu_custom_call" | custom-call | flops 1342177280 | bytes 5242880 | tf_op jit(solution)/shard_map/pallas_call | solution.py:209
  130.1 9.9 %all-to-all-start.1 = ((bf16[8,64,256]{2,1,0:T(8,128)(2,1)}), bf16[8,64,256]{2,1,0:T(8,128)(2,1)S(1)}, u32[]{:S(2)}, u32[]{:S(2)}) async-start(bf16[8,64,256]{2,1,0:T(8,128)(2,1)} %bitcast.15), calls=%async_computation.1 | async-start | bytes 524288 | tf_op jit(solution)/shard_map/all_to_all | solution.py:301
  140.3 6.1 %all-to-all-done.1 = bf16[8,64,256]{2,1,0:T(8,128)(2,1)S(1)} async-done(((bf16[8,64,256]{2,1,0:T(8,128)(2,1)}), bf16[8,64,256]{2,1,0:T(8,128)(2,1)S(1)}, u32[]{:S(2)}, u32[]{:S(2)}) %all-to-all-start.1) | async-done | bytes 262176 | tf_op jit(solution)/shard_map/all_to_all | solution.py:301
  146.4 5.0 %convert_reduce_fusion = f32[64,2048]{1,0:T(8,128)S(1)} fusion(bf16[8,64,256]{2,1,0:T(8,128)(2,1)S(1)} %all-to-all-done.1, bf16[8,256,2048]{2,1,0:T(8,128)(2,1)} %bitcast.61), kind=kOutput, calls=%fused_computation.2 | convolution fusion | flops 539885568 | bytes 9175040 | tf_op jit(solution)/shard_map/gtc,gcd->gtd/dot_general | solution.py:304
  151.7 1.5 convolution_convert_fusion.2
  153.2 16.6 %shard_map.128 = bf16[8,32,2048]{2,1,0:T(8,128)(2,1)} custom-call(bf16[8,32,2048]{2,1,0:T(8,128)(2,1)} %bitcast.63), custom_call_target="tpu_custom_call" | custom-call | tf_op jit(solution)/shard_map/pallas_call | solution.py:135
  169.8 2.6 %fusion.5 = f32[256,512]{1,0:T(8,128)S(1)} fusion(bf16[256,2048]{1,0:T(8,128)(2,1)} %bitcast.65, bf16[1,2048,512]{2,1,0:T(8,128)(2,1)} %param.21), kind=kOutput, calls=%fused_computation.11 | convolution fusion | flops 536870912 | bytes 3670016 | tf_op jit(solution)/shard_map/dot_general | solution.py:333
  172.4 4.9 %convolution_convert_fusion.1 = bf16[256,2048]{1,0:T(8,128)(2,1)} fusion(bf16[1,512,2048]{2,1,0:T(8,128)(2,1)} %param.23, bf16[256,2048]{1,0:T(8,128)(2,1)} %bitcast.66, bf16[1,2048,512]{2,1,0:T(8,128)(2,1)} %param.22, f32[256,512]{1,0:T(8,128)S(1)} %fusion.5), kind=kOutput, calls=%fused_computation.4 | convolution fusion | flops 1075052544 | bytes 6815744 | tf_op jit(solution)/shard_map/dot_general | solution.py:337
  177.3 15.6 %shard_map.129 = bf16[8,32,2048]{2,1,0:T(8,128)(2,1)} custom-call(bf16[8,32,2048]{2,1,0:T(8,128)(2,1)} %bitcast.67), custom_call_target="tpu_custom_call" | custom-call | tf_op jit(solution)/shard_map/pallas_call | solution.py:135
  193.0 2.8 %gather_fusion.1 = bf16[128,2048]{1,0:T(8,128)(2,1)S(1)} fusion(bf16[256,2048]{1,0:T(8,128)(2,1)} %bitcast.60, s32[1024]{0:T(1024)S(1)} %pad_clamp_fusion), kind=kCustom, calls=%fused_computation.1 | custom fusion | bytes 1049088 | tf_op jit(solution)/shard_map/gather | solution.py:342
  195.8 1.6 reshape.199
  197.4 2.8 %multiply_reduce_fusion = f32[64,2048]{1,0:T(8,128)S(1)} fusion(f32[64,2,2048]{2,1,0:T(2,128)} %reshape.199, f32[64,2]{1,0:T(8,128)S(1)} %copy.33), kind=kLoop, calls=%fused_computation.15 | loop fusion | flops 393216 | bytes 1573376 | tf_op jit(solution)/shard_map/reduce_sum | solution.py:345
  200.2 0.9 fusion.26
  (53 shorter events, 3.8 us)
Async XLA Ops:
  6.5 4.9 %copy-start = (bf16[128,2,16,256]{3,2,1,0:T(8,128)(2,1)S(1)}, bf16[128,2,16,256]{3,2,1,0:T(8,128)(2,1)}, u32[]{:S(2)}) copy-start(bf16[128,2,16,256]{3,2,1,0:T(8,128)(2,1)} %param.16) | copy-start | bytes 6291460
  6.5 3.9 %copy-start.2 = (s32[32,128]{1,0:T(8,128)S(1)}, s32[32,128]{1,0:T(8,128)}, u32[]{:S(2)}) copy-start(s32[32,128]{1,0:T(8,128)} %param.15) | copy-start | bytes 49156
  6.5 35.3 %all-gather.3.cloned.1.call-start = ((), (), s32[]{:S(2)}) async-start(), calls=%async_computation.2 | async-start | bytes 2359296 | tf_op jit(solution)/shard_map/all_gather | solution.py:264
  9.6 136.8 %all-gather.5.cloned.1.call-start = ((), (), s32[]{:S(2)}) async-start(), calls=%async_computation.3 | async-start | bytes 9437184 | tf_op jit(solution)/shard_map/all_gather | solution.py:299
  14.3 104.5 %all-to-all-start = ((bf16[32,8,2,16,256]{4,3,2,1,0:T(8,128)(2,1)}), bf16[32,8,2,16,256]{4,3,2,1,0:T(8,128)(2,1)}, u32[]{:S(2)}, u32[]{:S(2)}) async-start(bf16[32,8,2,16,256]{4,3,2,1,0:T(8,128)(2,1)} %bitcast.62), calls=%async_computation | async-start | bytes 8388608 | tf_op jit(solution)/shard_map/all_to_all | solution.py:284
  26.3 4.8 %copy-start.4 = (s32[64,2]{0,1:T(2,128)S(1)}, s32[64,2]{0,1:T(2,128)}, u32[]{:S(2)}) copy-start(s32[64,2]{0,1:T(2,128)} %param.24) | copy-start | bytes 1540
  26.3 5.3 %copy-start.6 = (s32[32]{0:T(128)S(1)}, s32[32]{0:T(128)}, u32[]{:S(2)}) copy-start(s32[32]{0:T(128)} %param.14) | copy-start | bytes 388
  118.8 21.2 %copy-start.5 = (f32[64,2]{0,1:T(2,128)S(1)}, f32[64,2]{0,1:T(2,128)}, u32[]{:S(2)}) copy-start(f32[64,2]{0,1:T(2,128)} %param.25) | copy-start | bytes 1540
  130.1 16.3 %all-to-all-start.1 = ((bf16[8,64,256]{2,1,0:T(8,128)(2,1)}), bf16[8,64,256]{2,1,0:T(8,128)(2,1)S(1)}, u32[]{:S(2)}, u32[]{:S(2)}) async-start(bf16[8,64,256]{2,1,0:T(8,128)(2,1)} %bitcast.15), calls=%async_computation.1 | async-start | bytes 524288 | tf_op jit(solution)/shard_map/all_to_all | solution.py:301
  146.4 5.0 %copy-start.1 = (bf16[64,2048]{1,0:T(8,128)(2,1)S(1)}, bf16[64,2048]{1,0:T(8,128)(2,1)}, u32[]{:S(2)}) copy-start(bf16[64,2048]{1,0:T(8,128)(2,1)} %param.13) | copy-start | bytes 786436
  146.4 5.2 %copy-start.3 = (f32[2048]{0:T(1024)S(1)}, f32[2048]{0:T(1024)}, u32[]{:S(2)}) copy-start(f32[2048]{0:T(1024)} %param.20) | copy-start | bytes 24580
Sparse Core Ops, SparseCore 0:
  9.8 32.0 all-gather.2
  43.7 52.6 all-gather.4

commit v12 on v11

--- a/solution.py
+++ b/solution.py
@@ -11,7 +11,7 @@
 EXPERT = ("ey", "ec")
 MESH_AXES = ("group", "ey", "ec")
 MESH_IDS = pl.DeviceIdType.MESH
-NBLK = 4
+NBLK = 2
 CTX = 2048
 
 

time: 211 us -> 207 us (0.981); the launches traced: 208 us -> 206 us
  no operation moved by 1% of the time
where the time goes in v12:
time: 207 us; the launch traced here: 206 us
  waiting for transfers between devices  86.7 us (42%)
  Pallas kernels  41.9 us (20%)
  starting transfers between devices  21.9 us (11%)
  matrix products  18.4 us (9%)
  local copies, waits for them, and re-layouts  13.8 us (7%)
  between operations  13.7 us (7%)
  other arithmetic  9.87 us (5%)
    all_to_all x1, waiting for transfers between devices, shards(): lax.all_to_all(outgoing, 'group', split_axis=0, concat_axis=0, tiled=True)  71.9 us
    pallas_call x2, Pallas kernels, exchange(): pl.pallas_call(functools.partial(exchange_kernel, axes, split), out_shape...  32.2 us
    all_to_all x1, starting transfers between devices, shards(): lax.all_to_all(outgoing, 'group', split_axis=0, concat_axis=0, tiled=True)  12 us
    all_to_all x1, starting transfers between devices, shards(): lax.all_to_all(attended.reshape(expert_lanes, tok_rows, local_width), EXP...  9.87 us
    pallas_call x1, Pallas kernels, paged_attention(): pl.pallas_call(attention_kernel, out_shape=jax.ShapeDtypeStruct((rows, lo...  9.69 us
    all_gather x1, waiting for transfers between devices, shards(): lax.all_gather(normed, EXPERT, axis=0, tiled=True)  8.02 us
    all_to_all x1, waiting for transfers between devices, shards(): lax.all_to_all(attended.reshape(expert_lanes, tok_rows, local_width), EXP...  6.12 us
    dot_general x1, matrix products, shards(): jnp.einsum('gtc,gcd->gtd', rows_piece, head_weights, preferred_element_ty...  5.02 us
  transfers between devices with their start and end apart: 4, of which 3 were waited for; matrix products, arithmetic and copies ran while one was open for 8% of the time, Pallas kernels for 5%

profile of v12, /device:TPU:1, one launch (start us, length us, event | category | flops | bytes accessed | tf_op | source)
XLA Modules:
  0.0 206.3 jit_solution(13061217243279255686)
XLA Ops:
  6.5 1.3 fusion.15
  7.8 1.8 fusion.17
  9.7 0.7 all-gather.5.cloned.1.call-update
  11.5 2.8 %gather_fusion = bf16[256,2,16,256]{3,2,1,0:T(8,128)(2,1)} fusion(bf16[128,2,16,256]{3,2,1,0:T(8,128)(2,1)S(1)} %copy-done, s32[1024]{0:T(1024)S(1)} %pad_clamp_fusion.1), kind=kCustom, calls=%fused_computation | custom fusion | bytes 8389632 | tf_op jit(solution)/shard_map/gather | solution.py:283
  14.3 12.0 %all-to-all-start = ((bf16[32,8,2,16,256]{4,3,2,1,0:T(8,128)(2,1)}), bf16[32,8,2,16,256]{4,3,2,1,0:T(8,128)(2,1)}, u32[]{:S(2)}, u32[]{:S(2)}) async-start(bf16[32,8,2,16,256]{4,3,2,1,0:T(8,128)(2,1)} %bitcast.62), calls=%async_computation | async-start | bytes 8388608 | tf_op jit(solution)/shard_map/all_to_all | solution.py:284
  26.3 4.8 %copy.27 = bf16[2048,3,256]{0,2,1:T(8,128)(2,1)} copy(bf16[2048,3,256]{2,0,1:T(8,128)(2,1)} %param.18) | data formatting | bytes 6291456 | tf_op args[5]
  31.5 0.7 dynamic_slice.7.len_ref
  32.2 0.6 add_convert_fusion.2
  33.8 8.0 %all-gather.3.cloned.1.call-done = bf16[512,2048]{1,0:T(8,128)(2,1)} async-done(((bf16[64,2048]{1,0:T(8,128)(2,1)}), bf16[512,2048]{1,0:T(8,128)(2,1)}) %all-gather.3.cloned.1.call-update) | async-done | bytes 2097168 | tf_op jit(solution)/shard_map/all_gather | solution.py:264
  41.8 4.3 %fusion = f32[512,3,2,128]{0,3,2,1:T(8,128)S(1)} fusion(bf16[3,2,128,2048]{3,2,1,0:T(8,128)(2,1)} %bitcast.64, bf16[512,2048]{1,0:T(8,128)(2,1)} %all-gather.3.cloned.1.call-done), kind=kOutput, calls=%fused_computation.6 | convolution fusion | flops 1610612736 | bytes 6815744 | tf_op jit(solution)/shard_map/dot_general | solution.py:263
  46.9 71.9 %all-to-all-done = bf16[32,8,2,16,256]{4,3,2,1,0:T(8,128)(2,1)} async-done(((bf16[32,8,2,16,256]{4,3,2,1,0:T(8,128)(2,1)}), bf16[32,8,2,16,256]{4,3,2,1,0:T(8,128)(2,1)}, u32[]{:S(2)}, u32[]{:S(2)}) %all-to-all-start) | async-done | bytes 4194336 | tf_op jit(solution)/shard_map/all_to_all | solution.py:284
  118.8 9.7 %shard_map.127 = bf16[512,256]{1,0:T(8,128)(2,1)} custom-call(s32[128]{0:T(128)S(1)} %multiply_add_fusion.1.slots_ref, s32[1]{0:T(128)} %dynamic_slice.7.len_ref, bf16[512,256]{1,0:T(8,128)(2,1)S(1)} %copy.35.q_ref, bf16[512,256]{1,0:T(8,128)(2,1)S(1)} %copy.36.nk_ref, bf16[512,256]{1,0:T(8,128)(2,1)S(1)} %copy.37.nv_ref, ...), custom_call_target="tpu_custom_call" | custom-call | flops 1342177280 | bytes 5242880 | tf_op jit(solution)/shard_map/pallas_call | solution.py:209
  128.5 9.9 %all-to-all-start.1 = ((bf16[8,64,256]{2,1,0:T(8,128)(2,1)}), bf16[8,64,256]{2,1,0:T(8,128)(2,1)S(1)}, u32[]{:S(2)}, u32[]{:S(2)}) async-start(bf16[8,64,256]{2,1,0:T(8,128)(2,1)} %bitcast.15), calls=%async_computation.1 | async-start | bytes 524288 | tf_op jit(solution)/shard_map/all_to_all | solution.py:301
  138.7 6.1 %all-to-all-done.1 = bf16[8,64,256]{2,1,0:T(8,128)(2,1)S(1)} async-done(((bf16[8,64,256]{2,1,0:T(8,128)(2,1)}), bf16[8,64,256]{2,1,0:T(8,128)(2,1)S(1)}, u32[]{:S(2)}, u32[]{:S(2)}) %all-to-all-start.1) | async-done | bytes 262176 | tf_op jit(solution)/shard_map/all_to_all | solution.py:301
  144.8 5.0 %convert_reduce_fusion = f32[64,2048]{1,0:T(8,128)S(1)} fusion(bf16[8,64,256]{2,1,0:T(8,128)(2,1)S(1)} %all-to-all-done.1, bf16[8,256,2048]{2,1,0:T(8,128)(2,1)} %bitcast.61), kind=kOutput, calls=%fused_computation.2 | convolution fusion | flops 539885568 | bytes 9175040 | tf_op jit(solution)/shard_map/gtc,gcd->gtd/dot_general | solution.py:304
  150.1 1.5 convolution_convert_fusion.2
  151.6 16.6 %shard_map.128 = bf16[8,32,2048]{2,1,0:T(8,128)(2,1)} custom-call(bf16[8,32,2048]{2,1,0:T(8,128)(2,1)} %bitcast.63), custom_call_target="tpu_custom_call" | custom-call | tf_op jit(solution)/shard_map/pallas_call | solution.py:135
  168.2 2.6 %fusion.5 = f32[256,512]{1,0:T(8,128)S(1)} fusion(bf16[256,2048]{1,0:T(8,128)(2,1)} %bitcast.65, bf16[1,2048,512]{2,1,0:T(8,128)(2,1)} %param.21), kind=kOutput, calls=%fused_computation.11 | convolution fusion | flops 536870912 | bytes 3670016 | tf_op jit(solution)/shard_map/dot_general | solution.py:333
  170.8 4.9 %convolution_convert_fusion.1 = bf16[256,2048]{1,0:T(8,128)(2,1)} fusion(bf16[1,512,2048]{2,1,0:T(8,128)(2,1)} %param.23, bf16[256,2048]{1,0:T(8,128)(2,1)} %bitcast.66, bf16[1,2048,512]{2,1,0:T(8,128)(2,1)} %param.22, f32[256,512]{1,0:T(8,128)S(1)} %fusion.5), kind=kOutput, calls=%fused_computation.4 | convolution fusion | flops 1075052544 | bytes 6815744 | tf_op jit(solution)/shard_map/dot_general | solution.py:337
  175.7 15.6 %shard_map.129 = bf16[8,32,2048]{2,1,0:T(8,128)(2,1)} custom-call(bf16[8,32,2048]{2,1,0:T(8,128)(2,1)} %bitcast.67), custom_call_target="tpu_custom_call" | custom-call | tf_op jit(solution)/shard_map/pallas_call | solution.py:135
  191.4 2.8 %gather_fusion.1 = bf16[128,2048]{1,0:T(8,128)(2,1)S(1)} fusion(bf16[256,2048]{1,0:T(8,128)(2,1)} %bitcast.60, s32[1024]{0:T(1024)S(1)} %pad_clamp_fusion), kind=kCustom, calls=%fused_computation.1 | custom fusion | bytes 1049088 | tf_op jit(solution)/shard_map/gather | solution.py:342
  194.2 1.6 reshape.199
  195.8 2.8 %multiply_reduce_fusion = f32[64,2048]{1,0:T(8,128)S(1)} fusion(f32[64,2,2048]{2,1,0:T(2,128)} %reshape.199, f32[64,2]{1,0:T(8,128)S(1)} %copy.33), kind=kLoop, calls=%fused_computation.15 | loop fusion | flops 393216 | bytes 1573376 | tf_op jit(solution)/shard_map/reduce_sum | solution.py:345
  198.6 0.9 fusion.26
  (53 shorter events, 3.8 us)
Async XLA Ops:
  6.5 4.9 %copy-start = (bf16[128,2,16,256]{3,2,1,0:T(8,128)(2,1)S(1)}, bf16[128,2,16,256]{3,2,1,0:T(8,128)(2,1)}, u32[]{:S(2)}) copy-start(bf16[128,2,16,256]{3,2,1,0:T(8,128)(2,1)} %param.16) | copy-start | bytes 6291460
  6.5 3.9 %copy-start.2 = (s32[32,128]{1,0:T(8,128)S(1)}, s32[32,128]{1,0:T(8,128)}, u32[]{:S(2)}) copy-start(s32[32,128]{1,0:T(8,128)} %param.15) | copy-start | bytes 49156
  6.5 35.3 %all-gather.3.cloned.1.call-start = ((), (), s32[]{:S(2)}) async-start(), calls=%async_computation.2 | async-start | bytes 2359296 | tf_op jit(solution)/shard_map/all_gather | solution.py:264
  9.6 135.2 %all-gather.5.cloned.1.call-start = ((), (), s32[]{:S(2)}) async-start(), calls=%async_computation.3 | async-start | bytes 9437184 | tf_op jit(solution)/shard_map/all_gather | solution.py:299
  14.3 104.5 %all-to-all-start = ((bf16[32,8,2,16,256]{4,3,2,1,0:T(8,128)(2,1)}), bf16[32,8,2,16,256]{4,3,2,1,0:T(8,128)(2,1)}, u32[]{:S(2)}, u32[]{:S(2)}) async-start(bf16[32,8,2,16,256]{4,3,2,1,0:T(8,128)(2,1)} %bitcast.62), calls=%async_computation | async-start | bytes 8388608 | tf_op jit(solution)/shard_map/all_to_all | solution.py:284
  26.3 4.8 %copy-start.4 = (s32[64,2]{0,1:T(2,128)S(1)}, s32[64,2]{0,1:T(2,128)}, u32[]{:S(2)}) copy-start(s32[64,2]{0,1:T(2,128)} %param.24) | copy-start | bytes 1540
  26.3 5.3 %copy-start.6 = (s32[32]{0:T(128)S(1)}, s32[32]{0:T(128)}, u32[]{:S(2)}) copy-start(s32[32]{0:T(128)} %param.14) | copy-start | bytes 388
  118.8 19.6 %copy-start.5 = (f32[64,2]{0,1:T(2,128)S(1)}, f32[64,2]{0,1:T(2,128)}, u32[]{:S(2)}) copy-start(f32[64,2]{0,1:T(2,128)} %param.25) | copy-start | bytes 1540
  128.5 16.3 %all-to-all-start.1 = ((bf16[8,64,256]{2,1,0:T(8,128)(2,1)}), bf16[8,64,256]{2,1,0:T(8,128)(2,1)S(1)}, u32[]{:S(2)}, u32[]{:S(2)}) async-start(bf16[8,64,256]{2,1,0:T(8,128)(2,1)} %bitcast.15), calls=%async_computation.1 | async-start | bytes 524288 | tf_op jit(solution)/shard_map/all_to_all | solution.py:301
  144.8 5.0 %copy-start.1 = (bf16[64,2048]{1,0:T(8,128)(2,1)S(1)}, bf16[64,2048]{1,0:T(8,128)(2,1)}, u32[]{:S(2)}) copy-start(bf16[64,2048]{1,0:T(8,128)(2,1)} %param.13) | copy-start | bytes 786436
  144.8 5.2 %copy-start.3 = (f32[2048]{0:T(1024)S(1)}, f32[2048]{0:T(1024)}, u32[]{:S(2)}) copy-start(f32[2048]{0:T(1024)} %param.20) | copy-start | bytes 24580
Sparse Core Ops, SparseCore 0:
  9.8 32.0 all-gather.2
  43.7 52.6 all-gather.4

commit v13 on v12

--- a/solution.py
+++ b/solution.py
@@ -11,7 +11,7 @@
 EXPERT = ("ey", "ec")
 MESH_AXES = ("group", "ey", "ec")
 MESH_IDS = pl.DeviceIdType.MESH
-NBLK = 2
+NBLK = 1
 CTX = 2048
 
 

time: 207 us -> 208 us (level)
  no operation moved by 1% of the time
where the time goes in v13:
time: 208 us
  waiting for transfers between devices  86.7 us (42%)
  Pallas kernels  43.1 us (21%)
  starting transfers between devices  21.9 us (11%)
  matrix products  18.4 us (9%)
  local copies, waits for them, and re-layouts  13.8 us (7%)
  between operations  13.7 us (7%)
  other arithmetic  9.87 us (5%)
    all_to_all x1, waiting for transfers between devices, shards(): lax.all_to_all(outgoing, 'group', split_axis=0, concat_axis=0, tiled=True)  71.9 us
    pallas_call x2, Pallas kernels, exchange(): pl.pallas_call(functools.partial(exchange_kernel, axes, split), out_shape...  32.2 us
    all_to_all x1, starting transfers between devices, shards(): lax.all_to_all(outgoing, 'group', split_axis=0, concat_axis=0, tiled=True)  12 us
    pallas_call x1, Pallas kernels, paged_attention(): pl.pallas_call(attention_kernel, out_shape=jax.ShapeDtypeStruct((rows, lo...  10.9 us
    all_to_all x1, starting transfers between devices, shards(): lax.all_to_all(attended.reshape(expert_lanes, tok_rows, local_width), EXP...  9.87 us
    all_gather x1, waiting for transfers between devices, shards(): lax.all_gather(normed, EXPERT, axis=0, tiled=True)  8.02 us
    all_to_all x1, waiting for transfers between devices, shards(): lax.all_to_all(attended.reshape(expert_lanes, tok_rows, local_width), EXP...  6.12 us
    dot_general x1, matrix products, shards(): jnp.einsum('gtc,gcd->gtd', rows_piece, head_weights, preferred_element_ty...  5.02 us
  transfers between devices with their start and end apart: 4, of which 3 were waited for; matrix products, arithmetic and copies ran while one was open for 8% of the time, Pallas kernels for 5%

profile of v13, /device:TPU:1, one launch (start us, length us, event | category | flops | bytes accessed | tf_op | source)
XLA Modules:
  0.0 207.5 jit_solution(3217054025437495538)
XLA Ops:
  6.5 1.3 fusion.15
  7.8 1.8 fusion.17
  9.7 0.7 all-gather.5.cloned.1.call-update
  11.5 2.8 %gather_fusion = bf16[256,2,16,256]{3,2,1,0:T(8,128)(2,1)} fusion(bf16[128,2,16,256]{3,2,1,0:T(8,128)(2,1)S(1)} %copy-done, s32[1024]{0:T(1024)S(1)} %pad_clamp_fusion.1), kind=kCustom, calls=%fused_computation | custom fusion | bytes 8389632 | tf_op jit(solution)/shard_map/gather | solution.py:283
  14.3 12.0 %all-to-all-start = ((bf16[32,8,2,16,256]{4,3,2,1,0:T(8,128)(2,1)}), bf16[32,8,2,16,256]{4,3,2,1,0:T(8,128)(2,1)}, u32[]{:S(2)}, u32[]{:S(2)}) async-start(bf16[32,8,2,16,256]{4,3,2,1,0:T(8,128)(2,1)} %bitcast.62), calls=%async_computation | async-start | bytes 8388608 | tf_op jit(solution)/shard_map/all_to_all | solution.py:284
  26.3 4.8 %copy.27 = bf16[2048,3,256]{0,2,1:T(8,128)(2,1)} copy(bf16[2048,3,256]{2,0,1:T(8,128)(2,1)} %param.18) | data formatting | bytes 6291456 | tf_op args[5]
  31.5 0.7 dynamic_slice.7.len_ref
  32.2 0.6 add_convert_fusion.2
  33.8 8.0 %all-gather.3.cloned.1.call-done = bf16[512,2048]{1,0:T(8,128)(2,1)} async-done(((bf16[64,2048]{1,0:T(8,128)(2,1)}), bf16[512,2048]{1,0:T(8,128)(2,1)}) %all-gather.3.cloned.1.call-update) | async-done | bytes 2097168 | tf_op jit(solution)/shard_map/all_gather | solution.py:264
  41.8 4.3 %fusion = f32[512,3,2,128]{0,3,2,1:T(8,128)S(1)} fusion(bf16[3,2,128,2048]{3,2,1,0:T(8,128)(2,1)} %bitcast.64, bf16[512,2048]{1,0:T(8,128)(2,1)} %all-gather.3.cloned.1.call-done), kind=kOutput, calls=%fused_computation.6 | convolution fusion | flops 1610612736 | bytes 6815744 | tf_op jit(solution)/shard_map/dot_general | solution.py:263
  46.9 71.9 %all-to-all-done = bf16[32,8,2,16,256]{4,3,2,1,0:T(8,128)(2,1)} async-done(((bf16[32,8,2,16,256]{4,3,2,1,0:T(8,128)(2,1)}), bf16[32,8,2,16,256]{4,3,2,1,0:T(8,128)(2,1)}, u32[]{:S(2)}, u32[]{:S(2)}) %all-to-all-start) | async-done | bytes 4194336 | tf_op jit(solution)/shard_map/all_to_all | solution.py:284
  118.8 10.9 %shard_map.127 = bf16[512,256]{1,0:T(8,128)(2,1)} custom-call(s32[128]{0:T(128)S(1)} %multiply_add_fusion.1.slots_ref, s32[1]{0:T(128)} %dynamic_slice.7.len_ref, bf16[512,256]{1,0:T(8,128)(2,1)S(1)} %copy.35.q_ref, bf16[512,256]{1,0:T(8,128)(2,1)S(1)} %copy.36.nk_ref, bf16[512,256]{1,0:T(8,128)(2,1)S(1)} %copy.37.nv_ref, ...), custom_call_target="tpu_custom_call" | custom-call | flops 1342177280 | bytes 5242880 | tf_op jit(solution)/shard_map/pallas_call | solution.py:209
  129.7 9.9 %all-to-all-start.1 = ((bf16[8,64,256]{2,1,0:T(8,128)(2,1)}), bf16[8,64,256]{2,1,0:T(8,128)(2,1)S(1)}, u32[]{:S(2)}, u32[]{:S(2)}) async-start(bf16[8,64,256]{2,1,0:T(8,128)(2,1)} %bitcast.15), calls=%async_computation.1 | async-start | bytes 524288 | tf_op jit(solution)/shard_map/all_to_all | solution.py:301
  139.9 6.1 %all-to-all-done.1 = bf16[8,64,256]{2,1,0:T(8,128)(2,1)S(1)} async-done(((bf16[8,64,256]{2,1,0:T(8,128)(2,1)}), bf16[8,64,256]{2,1,0:T(8,128)(2,1)S(1)}, u32[]{:S(2)}, u32[]{:S(2)}) %all-to-all-start.1) | async-done | bytes 262176 | tf_op jit(solution)/shard_map/all_to_all | solution.py:301
  146.0 5.0 %convert_reduce_fusion = f32[64,2048]{1,0:T(8,128)S(1)} fusion(bf16[8,64,256]{2,1,0:T(8,128)(2,1)S(1)} %all-to-all-done.1, bf16[8,256,2048]{2,1,0:T(8,128)(2,1)} %bitcast.61), kind=kOutput, calls=%fused_computation.2 | convolution fusion | flops 539885568 | bytes 9175040 | tf_op jit(solution)/shard_map/gtc,gcd->gtd/dot_general | solution.py:304
  151.3 1.5 convolution_convert_fusion.2
  152.8 16.6 %shard_map.128 = bf16[8,32,2048]{2,1,0:T(8,128)(2,1)} custom-call(bf16[8,32,2048]{2,1,0:T(8,128)(2,1)} %bitcast.63), custom_call_target="tpu_custom_call" | custom-call | tf_op jit(solution)/shard_map/pallas_call | solution.py:135
  169.4 2.6 %fusion.5 = f32[256,512]{1,0:T(8,128)S(1)} fusion(bf16[256,2048]{1,0:T(8,128)(2,1)} %bitcast.65, bf16[1,2048,512]{2,1,0:T(8,128)(2,1)} %param.21), kind=kOutput, calls=%fused_computation.11 | convolution fusion | flops 536870912 | bytes 3670016 | tf_op jit(solution)/shard_map/dot_general | solution.py:333
  172.0 4.9 %convolution_convert_fusion.1 = bf16[256,2048]{1,0:T(8,128)(2,1)} fusion(bf16[1,512,2048]{2,1,0:T(8,128)(2,1)} %param.23, bf16[256,2048]{1,0:T(8,128)(2,1)} %bitcast.66, bf16[1,2048,512]{2,1,0:T(8,128)(2,1)} %param.22, f32[256,512]{1,0:T(8,128)S(1)} %fusion.5), kind=kOutput, calls=%fused_computation.4 | convolution fusion | flops 1075052544 | bytes 6815744 | tf_op jit(solution)/shard_map/dot_general | solution.py:337
  176.9 15.6 %shard_map.129 = bf16[8,32,2048]{2,1,0:T(8,128)(2,1)} custom-call(bf16[8,32,2048]{2,1,0:T(8,128)(2,1)} %bitcast.67), custom_call_target="tpu_custom_call" | custom-call | tf_op jit(solution)/shard_map/pallas_call | solution.py:135
  192.6 2.8 %gather_fusion.1 = bf16[128,2048]{1,0:T(8,128)(2,1)S(1)} fusion(bf16[256,2048]{1,0:T(8,128)(2,1)} %bitcast.60, s32[1024]{0:T(1024)S(1)} %pad_clamp_fusion), kind=kCustom, calls=%fused_computation.1 | custom fusion | bytes 1049088 | tf_op jit(solution)/shard_map/gather | solution.py:342
  195.4 1.6 reshape.199
  197.0 2.8 %multiply_reduce_fusion = f32[64,2048]{1,0:T(8,128)S(1)} fusion(f32[64,2,2048]{2,1,0:T(2,128)} %reshape.199, f32[64,2]{1,0:T(8,128)S(1)} %copy.33), kind=kLoop, calls=%fused_computation.15 | loop fusion | flops 393216 | bytes 1573376 | tf_op jit(solution)/shard_map/reduce_sum | solution.py:345
  199.8 0.9 fusion.26
  (53 shorter events, 3.8 us)
Async XLA Ops:
  6.5 4.9 %copy-start = (bf16[128,2,16,256]{3,2,1,0:T(8,128)(2,1)S(1)}, bf16[128,2,16,256]{3,2,1,0:T(8,128)(2,1)}, u32[]{:S(2)}) copy-start(bf16[128,2,16,256]{3,2,1,0:T(8,128)(2,1)} %param.16) | copy-start | bytes 6291460
  6.5 3.9 %copy-start.2 = (s32[32,128]{1,0:T(8,128)S(1)}, s32[32,128]{1,0:T(8,128)}, u32[]{:S(2)}) copy-start(s32[32,128]{1,0:T(8,128)} %param.15) | copy-start | bytes 49156
  6.5 35.3 %all-gather.3.cloned.1.call-start = ((), (), s32[]{:S(2)}) async-start(), calls=%async_computation.2 | async-start | bytes 2359296 | tf_op jit(solution)/shard_map/all_gather | solution.py:264
  9.6 136.4 %all-gather.5.cloned.1.call-start = ((), (), s32[]{:S(2)}) async-start(), calls=%async_computation.3 | async-start | bytes 9437184 | tf_op jit(solution)/shard_map/all_gather | solution.py:299
  14.3 104.5 %all-to-all-start = ((bf16[32,8,2,16,256]{4,3,2,1,0:T(8,128)(2,1)}), bf16[32,8,2,16,256]{4,3,2,1,0:T(8,128)(2,1)}, u32[]{:S(2)}, u32[]{:S(2)}) async-start(bf16[32,8,2,16,256]{4,3,2,1,0:T(8,128)(2,1)} %bitcast.62), calls=%async_computation | async-start | bytes 8388608 | tf_op jit(solution)/shard_map/all_to_all | solution.py:284
  26.3 4.8 %copy-start.4 = (s32[64,2]{0,1:T(2,128)S(1)}, s32[64,2]{0,1:T(2,128)}, u32[]{:S(2)}) copy-start(s32[64,2]{0,1:T(2,128)} %param.24) | copy-start | bytes 1540
  26.3 5.3 %copy-start.6 = (s32[32]{0:T(128)S(1)}, s32[32]{0:T(128)}, u32[]{:S(2)}) copy-start(s32[32]{0:T(128)} %param.14) | copy-start | bytes 388
  118.8 20.8 %copy-start.5 = (f32[64,2]{0,1:T(2,128)S(1)}, f32[64,2]{0,1:T(2,128)}, u32[]{:S(2)}) copy-start(f32[64,2]{0,1:T(2,128)} %param.25) | copy-start | bytes 1540
  129.7 16.3 %all-to-all-start.1 = ((bf16[8,64,256]{2,1,0:T(8,128)(2,1)}), bf16[8,64,256]{2,1,0:T(8,128)(2,1)S(1)}, u32[]{:S(2)}, u32[]{:S(2)}) async-start(bf16[8,64,256]{2,1,0:T(8,128)(2,1)} %bitcast.15), calls=%async_computation.1 | async-start | bytes 524288 | tf_op jit(solution)/shard_map/all_to_all | solution.py:301
  146.0 5.0 %copy-start.1 = (bf16[64,2048]{1,0:T(8,128)(2,1)S(1)}, bf16[64,2048]{1,0:T(8,128)(2,1)}, u32[]{:S(2)}) copy-start(bf16[64,2048]{1,0:T(8,128)(2,1)} %param.13) | copy-start | bytes 786436
  146.0 5.2 %copy-start.3 = (f32[2048]{0:T(1024)S(1)}, f32[2048]{0:T(1024)}, u32[]{:S(2)}) copy-start(f32[2048]{0:T(1024)} %param.20) | copy-start | bytes 24580
Sparse Core Ops, SparseCore 0:
  9.8 32.0 all-gather.2
  43.7 52.6 all-gather.4

commit v14 on v13

--- a/solution.py
+++ b/solution.py
@@ -339,14 +339,11 @@
         .reshape(rows_piece.shape)
     )
     returned = exchange(result, EXPERT, 1)
-    picked = returned.reshape(expert_lanes * capacity, model_width)[
-        flat_expert * capacity + slot_index
-    ]
-    weighted = jnp.sum(
-        picked.reshape(tok_rows, route_count, model_width).astype(jnp.float32)
-        * gate_weights[..., None],
-        axis=1,
-    )
+    flat_returned = returned.reshape(expert_lanes * capacity, model_width)
+    slot_pair = (flat_expert * capacity + slot_index).reshape(tok_rows, route_count)
+    weighted = flat_returned[slot_pair[:, 0]].astype(jnp.float32) * gate_weights[:, 0:1]
+    for k in range(1, route_count):
+        weighted = weighted + flat_returned[slot_pair[:, k]].astype(jnp.float32) * gate_weights[:, k : k + 1]
     return residual + weighted
 
 

time: 208 us -> 208 us (level)
    reduce_sum x1 -> x0, other arithmetic: 2.79 us -> none  [shards(): jnp.sum(picked.reshape(tok_rows, route_count, model_width).astype(jnp.flo...]
    gather x1 -> x2, local copies, waits for them, and re-layouts: 2.8 us -> 4.59 us  [the longest x1 3.14 us: shards(): flat_returned[slot_pair[:, k]].astype(jnp.float32)]
    unnamed x17 -> x22, local copies, waits for them, and re-layouts: 4.99 us -> 5.45 us
where the time goes in v14:
time: 208 us; the launch traced here: 207 us
  waiting for transfers between devices  86.8 us (42%)
  Pallas kernels  43.1 us (21%)
  starting transfers between devices  21.9 us (11%)
  matrix products  19.1 us (9%)
  local copies, waits for them, and re-layouts  14.4 us (7%)
  between operations  13.7 us (7%)
  other arithmetic  8.41 us (4%)
    all_to_all x1, waiting for transfers between devices, shards(): lax.all_to_all(outgoing, 'group', split_axis=0, concat_axis=0, tiled=True)  71.8 us
    pallas_call x2, Pallas kernels, exchange(): pl.pallas_call(functools.partial(exchange_kernel, axes, split), out_shape...  32.2 us
    all_to_all x1, starting transfers between devices, shards(): lax.all_to_all(outgoing, 'group', split_axis=0, concat_axis=0, tiled=True)  12 us
    pallas_call x1, Pallas kernels, paged_attention(): pl.pallas_call(attention_kernel, out_shape=jax.ShapeDtypeStruct((rows, lo...  10.9 us
    all_to_all x1, starting transfers between devices, shards(): lax.all_to_all(attended.reshape(expert_lanes, tok_rows, local_width), EXP...  9.86 us
    all_gather x1, waiting for transfers between devices, shards(): lax.all_gather(normed, EXPERT, axis=0, tiled=True)  7.86 us
    all_to_all x1, waiting for transfers between devices, shards(): lax.all_to_all(attended.reshape(expert_lanes, tok_rows, local_width), EXP...  6.44 us
    unnamed x22, local copies, waits for them, and re-layouts  5.45 us
  transfers between devices with their start and end apart: 4, of which 3 were waited for; matrix products, arithmetic and copies ran while one was open for 8% of the time, Pallas kernels for 5%

profile of v14, /device:TPU:1, one launch (start us, length us, event | category | flops | bytes accessed | tf_op | source)
XLA Modules:
  0.0 207.4 jit_solution(4438723674788984815)
XLA Ops:
  6.5 1.3 fusion.15
  7.8 1.8 fusion.17
  9.7 0.7 all-gather.5.cloned.1.call-update
  10.7 0.6 select_reduce_fusion.1
  11.5 2.8 %gather_fusion = bf16[256,2,16,256]{3,2,1,0:T(8,128)(2,1)} fusion(bf16[128,2,16,256]{3,2,1,0:T(8,128)(2,1)S(1)} %copy-done, s32[1024]{0:T(1024)S(1)} %pad_clamp_fusion.2), kind=kCustom, calls=%fused_computation | custom fusion | bytes 8389632 | tf_op jit(solution)/shard_map/gather | solution.py:283
  14.3 12.0 %all-to-all-start = ((bf16[32,8,2,16,256]{4,3,2,1,0:T(8,128)(2,1)}), bf16[32,8,2,16,256]{4,3,2,1,0:T(8,128)(2,1)}, u32[]{:S(2)}, u32[]{:S(2)}) async-start(bf16[32,8,2,16,256]{4,3,2,1,0:T(8,128)(2,1)} %bitcast.65), calls=%async_computation | async-start | bytes 8388608 | tf_op jit(solution)/shard_map/all_to_all | solution.py:284
  26.3 4.7 %copy.34 = bf16[2048,3,256]{0,2,1:T(8,128)(2,1)} copy(bf16[2048,3,256]{2,0,1:T(8,128)(2,1)} %param.18) | data formatting | bytes 6291456 | tf_op args[5]
  31.6 0.7 dynamic_slice.7.len_ref
  32.3 0.7 add_convert_fusion.2
  34.0 7.9 %all-gather.3.cloned.1.call-done = bf16[512,2048]{1,0:T(8,128)(2,1)} async-done(((bf16[64,2048]{1,0:T(8,128)(2,1)}), bf16[512,2048]{1,0:T(8,128)(2,1)}) %all-gather.3.cloned.1.call-update) | async-done | bytes 2097168 | tf_op jit(solution)/shard_map/all_gather | solution.py:264
  41.9 4.3 %fusion = f32[512,3,2,128]{0,3,2,1:T(8,128)S(1)} fusion(bf16[3,2,128,2048]{3,2,1,0:T(8,128)(2,1)} %bitcast.67, bf16[512,2048]{1,0:T(8,128)(2,1)} %all-gather.3.cloned.1.call-done), kind=kOutput, calls=%fused_computation.7 | convolution fusion | flops 1610612736 | bytes 6815744 | tf_op jit(solution)/shard_map/dot_general | solution.py:263
  47.0 71.8 %all-to-all-done = bf16[32,8,2,16,256]{4,3,2,1,0:T(8,128)(2,1)} async-done(((bf16[32,8,2,16,256]{4,3,2,1,0:T(8,128)(2,1)}), bf16[32,8,2,16,256]{4,3,2,1,0:T(8,128)(2,1)}, u32[]{:S(2)}, u32[]{:S(2)}) %all-to-all-start) | async-done | bytes 4194336 | tf_op jit(solution)/shard_map/all_to_all | solution.py:284
  118.8 10.9 %shard_map.127 = bf16[512,256]{1,0:T(8,128)(2,1)} custom-call(s32[128]{0:T(128)S(1)} %multiply_add_fusion.2.slots_ref, s32[1]{0:T(128)} %dynamic_slice.7.len_ref, bf16[512,256]{1,0:T(8,128)(2,1)S(1)} %copy.41.q_ref, bf16[512,256]{1,0:T(8,128)(2,1)S(1)} %copy.42.nk_ref, bf16[512,256]{1,0:T(8,128)(2,1)S(1)} %copy.43.nv_ref, ...), custom_call_target="tpu_custom_call" | custom-call | flops 1342177280 | bytes 5242880 | tf_op jit(solution)/shard_map/pallas_call | solution.py:209
  129.7 9.9 %all-to-all-start.1 = ((bf16[8,64,256]{2,1,0:T(8,128)(2,1)}), bf16[8,64,256]{2,1,0:T(8,128)(2,1)S(1)}, u32[]{:S(2)}, u32[]{:S(2)}) async-start(bf16[8,64,256]{2,1,0:T(8,128)(2,1)} %bitcast.15), calls=%async_computation.1 | async-start | bytes 524288 | tf_op jit(solution)/shard_map/all_to_all | solution.py:301
  139.6 6.4 %all-to-all-done.1 = bf16[8,64,256]{2,1,0:T(8,128)(2,1)S(1)} async-done(((bf16[8,64,256]{2,1,0:T(8,128)(2,1)}), bf16[8,64,256]{2,1,0:T(8,128)(2,1)S(1)}, u32[]{:S(2)}, u32[]{:S(2)}) %all-to-all-start.1) | async-done | bytes 262176 | tf_op jit(solution)/shard_map/all_to_all | solution.py:301
  146.0 5.0 %convert_reduce_fusion = f32[64,2048]{1,0:T(8,128)S(1)} fusion(bf16[8,64,256]{2,1,0:T(8,128)(2,1)S(1)} %all-to-all-done.1, bf16[8,256,2048]{2,1,0:T(8,128)(2,1)} %bitcast.64), kind=kOutput, calls=%fused_computation.3 | convolution fusion | flops 539885568 | bytes 9175040 | tf_op jit(solution)/shard_map/gtc,gcd->gtd/dot_general | solution.py:304
  151.9 1.5 convolution_convert_fusion.2
  153.3 16.6 %shard_map.128 = bf16[8,32,2048]{2,1,0:T(8,128)(2,1)} custom-call(bf16[8,32,2048]{2,1,0:T(8,128)(2,1)} %bitcast.66), custom_call_target="tpu_custom_call" | custom-call | tf_op jit(solution)/shard_map/pallas_call | solution.py:135
  169.9 3.5 %fusion.5 = f32[256,512]{1,0:T(8,128)} fusion(bf16[256,2048]{1,0:T(8,128)(2,1)} %bitcast.68, bf16[1,2048,512]{2,1,0:T(8,128)(2,1)} %param.21), kind=kOutput, calls=%fused_computation.12 | convolution fusion | flops 536870912 | bytes 3670016 | tf_op jit(solution)/shard_map/dot_general | solution.py:333
  173.4 4.8 %convolution_convert_fusion.1 = bf16[256,2048]{1,0:T(8,128)(2,1)} fusion(bf16[1,512,2048]{2,1,0:T(8,128)(2,1)} %param.23, bf16[256,2048]{1,0:T(8,128)(2,1)S(1)} %bitcast.69, bf16[1,2048,512]{2,1,0:T(8,128)(2,1)} %param.22, f32[256,512]{1,0:T(8,128)} %fusion.5), kind=kOutput, calls=%fused_computation.5 | convolution fusion | flops 1075052544 | bytes 6815744 | tf_op jit(solution)/shard_map/dot_general | solution.py:337
  178.2 15.6 %shard_map.129 = bf16[8,32,2048]{2,1,0:T(8,128)(2,1)} custom-call(bf16[8,32,2048]{2,1,0:T(8,128)(2,1)} %bitcast.70), custom_call_target="tpu_custom_call" | custom-call | tf_op jit(solution)/shard_map/pallas_call | solution.py:135
  193.8 3.1 %gather_fusion.2 = bf16[64,2048]{1,0:T(8,128)(2,1)} fusion(bf16[256,2048]{1,0:T(8,128)(2,1)} %bitcast.62, s32[1024]{0:T(1024)S(1)} %get-tuple-element.26), kind=kCustom, calls=%fused_computation.2 | custom fusion | bytes 524544 | tf_op jit(solution)/shard_map/gather | solution.py:346
  197.0 1.5 gather_fusion.1
  198.4 2.2 %add_add_fusion = f32[64,2048]{1,0:T(8,128)} fusion(bf16[64,2048]{1,0:T(8,128)(2,1)} %gather_fusion.2, bf16[64,2048]{1,0:T(8,128)(2,1)} %gather_fusion.1, f32[64]{0:T(128)S(1)} %get-tuple-element.19, f32[64]{0:T(128)S(1)} %get-tuple-element.18, f32[64,2048]{1,0:T(8,128)} %copy-done.2, bf16[64,2048]{1,0:T(8,128)(2,1)S(1)} %copy-done.3), kind=kLoop, calls=%fused_computation.25 | loop fusion | flops 1048576 | bytes 1835520 | tf_op jit(solution)/shard_map/add | solution.py:347
  (58 shorter events, 3.6 us)
Async XLA Ops:
  6.5 4.9 %copy-start = (bf16[128,2,16,256]{3,2,1,0:T(8,128)(2,1)S(1)}, bf16[128,2,16,256]{3,2,1,0:T(8,128)(2,1)}, u32[]{:S(2)}) copy-start(bf16[128,2,16,256]{3,2,1,0:T(8,128)(2,1)} %param.16) | copy-start | bytes 6291460
  6.5 3.9 %copy-start.5 = (s32[32,128]{1,0:T(8,128)S(1)}, s32[32,128]{1,0:T(8,128)}, u32[]{:S(2)}) copy-start(s32[32,128]{1,0:T(8,128)} %param.15) | copy-start | bytes 49156
  6.5 35.3 %all-gather.3.cloned.1.call-start = ((), (), s32[]{:S(2)}) async-start(), calls=%async_computation.2 | async-start | bytes 2359296 | tf_op jit(solution)/shard_map/all_gather | solution.py:264
  9.6 136.4 %all-gather.5.cloned.1.call-start = ((), (), s32[]{:S(2)}) async-start(), calls=%async_computation.3 | async-start | bytes 9437184 | tf_op jit(solution)/shard_map/all_gather | solution.py:299
  14.3 104.5 %all-to-all-start = ((bf16[32,8,2,16,256]{4,3,2,1,0:T(8,128)(2,1)}), bf16[32,8,2,16,256]{4,3,2,1,0:T(8,128)(2,1)}, u32[]{:S(2)}, u32[]{:S(2)}) async-start(bf16[32,8,2,16,256]{4,3,2,1,0:T(8,128)(2,1)} %bitcast.65), calls=%async_computation | async-start | bytes 8388608 | tf_op jit(solution)/shard_map/all_to_all | solution.py:284
  26.2 4.7 %copy-start.7 = (s32[64,2]{0,1:T(2,128)S(1)}, s32[64,2]{0,1:T(2,128)}, u32[]{:S(2)}) copy-start(s32[64,2]{0,1:T(2,128)} %param.24) | copy-start | bytes 1540
  26.3 5.4 %copy-start.9 = (s32[32]{0:T(128)S(1)}, s32[32]{0:T(128)}, u32[]{:S(2)}) copy-start(s32[32]{0:T(128)} %param.14) | copy-start | bytes 388
  118.8 20.8 %copy-start.8 = (f32[64,2]{0,1:T(2,128)S(1)}, f32[64,2]{0,1:T(2,128)}, u32[]{:S(2)}) copy-start(f32[64,2]{0,1:T(2,128)} %param.25) | copy-start | bytes 1540
  129.7 16.3 %all-to-all-start.1 = ((bf16[8,64,256]{2,1,0:T(8,128)(2,1)}), bf16[8,64,256]{2,1,0:T(8,128)(2,1)S(1)}, u32[]{:S(2)}, u32[]{:S(2)}) async-start(bf16[8,64,256]{2,1,0:T(8,128)(2,1)} %bitcast.15), calls=%async_computation.1 | async-start | bytes 524288 | tf_op jit(solution)/shard_map/all_to_all | solution.py:301
  146.0 5.0 %copy-start.3 = (bf16[64,2048]{1,0:T(8,128)(2,1)S(1)}, bf16[64,2048]{1,0:T(8,128)(2,1)}, u32[]{:S(2)}) copy-start(bf16[64,2048]{1,0:T(8,128)(2,1)} %param.13) | copy-start | bytes 786436
  146.0 5.8 %copy-start.6 = (f32[2048]{0:T(1024)S(1)}, f32[2048]{0:T(1024)}, u32[]{:S(2)}) copy-start(f32[2048]{0:T(1024)} %param.20) | copy-start | bytes 24580
  151.1 0.8 copy-start.2
  169.9 3.5 %copy-start.4 = (bf16[8,32,2048]{2,1,0:T(8,128)(2,1)S(1)}, bf16[8,32,2048]{2,1,0:T(8,128)(2,1)}, u32[]{:S(2)}) copy-start(bf16[8,32,2048]{2,1,0:T(8,128)(2,1)} %shard_map.128) | copy-start | bytes 3145732
  193.8 3.2 %copy-start.1 = (bf16[8,32,2048]{2,1,0:T(8,128)(2,1)S(1)}, bf16[8,32,2048]{2,1,0:T(8,128)(2,1)}, u32[]{:S(2)}) copy-start(bf16[8,32,2048]{2,1,0:T(8,128)(2,1)} %shard_map.129) | copy-start | bytes 3145732
Sparse Core Ops, SparseCore 0:
  9.8 32.0 all-gather.2
  43.7 52.5 all-gather.4

commit v15 on v10

--- a/solution.py
+++ b/solution.py
@@ -11,7 +11,7 @@
 EXPERT = ("ey", "ec")
 MESH_AXES = ("group", "ey", "ec")
 MESH_IDS = pl.DeviceIdType.MESH
-NBLK = 8
+NBLK = 1
 CTX = 2048
 
 

time: 220 us -> 205 us (0.932)
  Pallas kernels: 70.8 us -> 55.4 us
    pallas_call x1, Pallas kernels: 25.8 us -> 10.5 us  [paged_attention(): pl.pallas_call(attention_kernel, out_shape=jax.ShapeDtypeStruct((rows, lo...]
  transfers between devices with their start and end apart: 3 -> 3, of which waited for: 2 -> 2; matrix products, arithmetic and copies ran while one was open for 8% -> 8% of each run, Pallas kernels for 18% -> 12%
where the time goes in v15:
time: 205 us; the launch traced here: 204 us
  waiting for transfers between devices  80.3 us (39%)
  Pallas kernels  55.4 us (27%)
  matrix products  18.5 us (9%)
  local copies, waits for them, and re-layouts  14.5 us (7%)
  between operations  13.7 us (7%)
  starting transfers between devices  12 us (6%)
  other arithmetic  9.87 us (5%)
    all_to_all x1, waiting for transfers between devices, shards(): lax.all_to_all(outgoing, 'group', split_axis=0, concat_axis=0, tiled=True)  71.8 us
    pallas_call x3, Pallas kernels, exchange(): pl.pallas_call(functools.partial(exchange_kernel, axes, split), out_shape...  44.9 us
    all_to_all x1, starting transfers between devices, shards(): lax.all_to_all(outgoing, 'group', split_axis=0, concat_axis=0, tiled=True)  12 us
    pallas_call x1, Pallas kernels, paged_attention(): pl.pallas_call(attention_kernel, out_shape=jax.ShapeDtypeStruct((rows, lo...  10.5 us
    all_gather x1, waiting for transfers between devices, shards(): lax.all_gather(normed, EXPERT, axis=0, tiled=True)  7.73 us
    unnamed x19, local copies, waits for them, and re-layouts  5.7 us
    dot_general x1, matrix products, shards(): jnp.einsum('gtc,gcd->gtd', rows_piece, head_weights, preferred_element_ty...  5.12 us
    dot_general x1, matrix products, shards(): jnp.dot(hidden, w_down[0], preferred_element_type=jnp.float32)  4.92 us
  transfers between devices with their start and end apart: 3, of which 2 were waited for; matrix products, arithmetic and copies ran while one was open for 8% of the time, Pallas kernels for 12%

profile of v15, /device:TPU:1, one launch (start us, length us, event | category | flops | bytes accessed | tf_op | source)
XLA Modules:
  0.0 204.4 jit_solution(13437776794145931774)
XLA Ops:
  6.5 1.3 fusion.15
  7.8 1.8 fusion.17
  9.7 0.7 all-gather.5.cloned.1.call-update
  11.5 2.8 %gather_fusion = bf16[256,2,16,256]{3,2,1,0:T(8,128)(2,1)} fusion(bf16[128,2,16,256]{3,2,1,0:T(8,128)(2,1)S(1)} %copy-done, s32[1024]{0:T(1024)S(1)} %pad_clamp_fusion.1), kind=kCustom, calls=%fused_computation | custom fusion | bytes 8389632 | tf_op jit(solution)/shard_map/gather | solution.py:283
  14.3 12.0 %all-to-all-start = ((bf16[32,8,2,16,256]{4,3,2,1,0:T(8,128)(2,1)}), bf16[32,8,2,16,256]{4,3,2,1,0:T(8,128)(2,1)}, u32[]{:S(2)}, u32[]{:S(2)}) async-start(bf16[32,8,2,16,256]{4,3,2,1,0:T(8,128)(2,1)} %bitcast.63), calls=%async_computation | async-start | bytes 8388608 | tf_op jit(solution)/shard_map/all_to_all | solution.py:284
  26.3 4.8 %copy.27 = bf16[2048,3,256]{0,2,1:T(8,128)(2,1)} copy(bf16[2048,3,256]{2,0,1:T(8,128)(2,1)} %param.18) | data formatting | bytes 6291456 | tf_op args[5]
  31.7 0.7 dynamic_slice.7.len_ref
  32.3 0.6 add_convert_fusion.2
  34.2 7.7 %all-gather.3.cloned.1.call-done = bf16[512,2048]{1,0:T(8,128)(2,1)} async-done(((bf16[64,2048]{1,0:T(8,128)(2,1)}), bf16[512,2048]{1,0:T(8,128)(2,1)}) %all-gather.3.cloned.1.call-update) | async-done | bytes 2097168 | tf_op jit(solution)/shard_map/all_gather | solution.py:264
  41.9 4.3 %fusion = f32[512,3,2,128]{0,3,2,1:T(8,128)S(1)} fusion(bf16[3,2,128,2048]{3,2,1,0:T(8,128)(2,1)} %bitcast.65, bf16[512,2048]{1,0:T(8,128)(2,1)} %all-gather.3.cloned.1.call-done), kind=kOutput, calls=%fused_computation.6 | convolution fusion | flops 1610612736 | bytes 6815744 | tf_op jit(solution)/shard_map/dot_general | solution.py:263
  47.0 71.8 %all-to-all-done = bf16[32,8,2,16,256]{4,3,2,1,0:T(8,128)(2,1)} async-done(((bf16[32,8,2,16,256]{4,3,2,1,0:T(8,128)(2,1)}), bf16[32,8,2,16,256]{4,3,2,1,0:T(8,128)(2,1)}, u32[]{:S(2)}, u32[]{:S(2)}) %all-to-all-start) | async-done | bytes 4194336 | tf_op jit(solution)/shard_map/all_to_all | solution.py:284
  118.8 10.5 %shard_map.127 = bf16[512,256]{1,0:T(8,128)(2,1)S(1)} custom-call(s32[128]{0:T(128)S(1)} %multiply_add_fusion.1.slots_ref, s32[1]{0:T(128)} %dynamic_slice.7.len_ref, bf16[512,256]{1,0:T(8,128)(2,1)S(1)} %copy.35.q_ref, bf16[512,256]{1,0:T(8,128)(2,1)S(1)} %copy.36.nk_ref, bf16[512,256]{1,0:T(8,128)(2,1)S(1)} %copy.37.nv_ref, ...), custom_call_target="tpu_custom_call" | custom-call | flops 1342177280 | bytes 5242880 | tf_op jit(solution)/shard_map/pallas_call | solution.py:209
  129.3 0.7 copy-done.1
  130.0 13.4 %shard_map.128 = bf16[8,64,256]{2,1,0:T(8,128)(2,1)} custom-call(bf16[8,64,256]{2,1,0:T(8,128)(2,1)} %bitcast.60), custom_call_target="tpu_custom_call" | custom-call | tf_op jit(solution)/shard_map/pallas_call | solution.py:135
  143.5 5.1 %convert_reduce_fusion = f32[64,2048]{1,0:T(8,128)S(1)} fusion(bf16[8,64,256]{2,1,0:T(8,128)(2,1)} %shard_map.128, bf16[8,256,2048]{2,1,0:T(8,128)(2,1)} %bitcast.62), kind=kOutput, calls=%fused_computation.2 | convolution fusion | flops 539885568 | bytes 9175040 | tf_op jit(solution)/shard_map/gtc,gcd->gtd/dot_general | solution.py:302
  148.8 1.5 convolution_convert_fusion.2
  150.3 15.9 %shard_map.129 = bf16[8,32,2048]{2,1,0:T(8,128)(2,1)} custom-call(bf16[8,32,2048]{2,1,0:T(8,128)(2,1)} %bitcast.64), custom_call_target="tpu_custom_call" | custom-call | tf_op jit(solution)/shard_map/pallas_call | solution.py:135
  166.2 2.6 %fusion.5 = f32[256,512]{1,0:T(8,128)S(1)} fusion(bf16[256,2048]{1,0:T(8,128)(2,1)} %bitcast.66, bf16[1,2048,512]{2,1,0:T(8,128)(2,1)} %param.21), kind=kOutput, calls=%fused_computation.11 | convolution fusion | flops 536870912 | bytes 3670016 | tf_op jit(solution)/shard_map/dot_general | solution.py:331
  168.8 4.9 %convolution_convert_fusion.1 = bf16[256,2048]{1,0:T(8,128)(2,1)} fusion(bf16[1,512,2048]{2,1,0:T(8,128)(2,1)} %param.23, bf16[256,2048]{1,0:T(8,128)(2,1)} %bitcast.67, bf16[1,2048,512]{2,1,0:T(8,128)(2,1)} %param.22, f32[256,512]{1,0:T(8,128)S(1)} %fusion.5), kind=kOutput, calls=%fused_computation.4 | convolution fusion | flops 1075052544 | bytes 6815744 | tf_op jit(solution)/shard_map/dot_general | solution.py:335
  173.8 15.6 %shard_map.130 = bf16[8,32,2048]{2,1,0:T(8,128)(2,1)} custom-call(bf16[8,32,2048]{2,1,0:T(8,128)(2,1)} %bitcast.68), custom_call_target="tpu_custom_call" | custom-call | tf_op jit(solution)/shard_map/pallas_call | solution.py:135
  189.4 2.8 %gather_fusion.1 = bf16[128,2048]{1,0:T(8,128)(2,1)S(1)} fusion(bf16[256,2048]{1,0:T(8,128)(2,1)} %bitcast.61, s32[1024]{0:T(1024)S(1)} %pad_clamp_fusion), kind=kCustom, calls=%fused_computation.1 | custom fusion | bytes 1049088 | tf_op jit(solution)/shard_map/gather | solution.py:340
  192.2 1.6 reshape.199
  193.8 2.8 %multiply_reduce_fusion = f32[64,2048]{1,0:T(8,128)S(1)} fusion(f32[64,2,2048]{2,1,0:T(2,128)} %reshape.199, f32[64,2]{1,0:T(8,128)S(1)} %copy.33), kind=kLoop, calls=%fused_computation.15 | loop fusion | flops 393216 | bytes 1573376 | tf_op jit(solution)/shard_map/reduce_sum | solution.py:343
  196.6 0.9 fusion.26
  (54 shorter events, 3.8 us)
Async XLA Ops:
  6.5 4.9 %copy-start = (bf16[128,2,16,256]{3,2,1,0:T(8,128)(2,1)S(1)}, bf16[128,2,16,256]{3,2,1,0:T(8,128)(2,1)}, u32[]{:S(2)}) copy-start(bf16[128,2,16,256]{3,2,1,0:T(8,128)(2,1)} %param.16) | copy-start | bytes 6291460
  6.5 3.9 %copy-start.3 = (s32[32,128]{1,0:T(8,128)S(1)}, s32[32,128]{1,0:T(8,128)}, u32[]{:S(2)}) copy-start(s32[32,128]{1,0:T(8,128)} %param.15) | copy-start | bytes 49156
  6.5 35.4 %all-gather.3.cloned.1.call-start = ((), (), s32[]{:S(2)}) async-start(), calls=%async_computation.1 | async-start | bytes 2359296 | tf_op jit(solution)/shard_map/all_gather | solution.py:264
  9.6 133.8 %all-gather.5.cloned.1.call-start = ((), (), s32[]{:S(2)}) async-start(), calls=%async_computation.2 | async-start | bytes 9437184 | tf_op jit(solution)/shard_map/all_gather | solution.py:299
  14.3 104.5 %all-to-all-start = ((bf16[32,8,2,16,256]{4,3,2,1,0:T(8,128)(2,1)}), bf16[32,8,2,16,256]{4,3,2,1,0:T(8,128)(2,1)}, u32[]{:S(2)}, u32[]{:S(2)}) async-start(bf16[32,8,2,16,256]{4,3,2,1,0:T(8,128)(2,1)} %bitcast.63), calls=%async_computation | async-start | bytes 8388608 | tf_op jit(solution)/shard_map/all_to_all | solution.py:284
  26.3 4.8 %copy-start.5 = (s32[64,2]{0,1:T(2,128)S(1)}, s32[64,2]{0,1:T(2,128)}, u32[]{:S(2)}) copy-start(s32[64,2]{0,1:T(2,128)} %param.24) | copy-start | bytes 1540
  26.3 5.3 %copy-start.6 = (f32[64,2]{0,1:T(2,128)S(1)}, f32[64,2]{0,1:T(2,128)}, u32[]{:S(2)}) copy-start(f32[64,2]{0,1:T(2,128)} %param.25) | copy-start | bytes 1540
  26.3 5.4 %copy-start.7 = (s32[32]{0:T(128)S(1)}, s32[32]{0:T(128)}, u32[]{:S(2)}) copy-start(s32[32]{0:T(128)} %param.14) | copy-start | bytes 388
  129.3 0.7 copy-start.1
  143.5 5.2 %copy-start.2 = (bf16[64,2048]{1,0:T(8,128)(2,1)S(1)}, bf16[64,2048]{1,0:T(8,128)(2,1)}, u32[]{:S(2)}) copy-start(bf16[64,2048]{1,0:T(8,128)(2,1)} %param.13) | copy-start | bytes 786436
  143.5 5.3 %copy-start.4 = (f32[2048]{0:T(1024)S(1)}, f32[2048]{0:T(1024)}, u32[]{:S(2)}) copy-start(f32[2048]{0:T(1024)} %param.20) | copy-start | bytes 24580
Sparse Core Ops, SparseCore 0:
  9.8 32.0 all-gather.2
  43.7 52.5 all-gather.4

commit v16 on v14

--- a/solution.py
+++ b/solution.py
@@ -298,9 +298,7 @@
     )
     head_weights = lax.all_gather(w_out, EXPERT, axis=0, tiled=True)
     head_weights = head_weights.reshape(expert_lanes, local_width, model_width)
-    rows_piece = lax.all_to_all(
-        attended.reshape(expert_lanes, tok_rows, local_width), EXPERT, 0, 0, tiled=True
-    )
+    rows_piece = exchange(attended.reshape(expert_lanes, tok_rows, local_width), EXPERT, 2)
     head_parts = jnp.einsum(
         "gtc,gcd->gtd", rows_piece, head_weights, preferred_element_type=jnp.float32
     ).astype(jnp.bfloat16)

time: 208 us -> 205 us (0.986)
  Pallas kernels: 43.1 us -> 55.3 us
  starting transfers between devices: 21.9 us -> 12 us
  waiting for transfers between devices: 86.8 us -> 80.5 us
    pallas_call x2 -> x3, Pallas kernels: 32.2 us -> 44.9 us  [exchange(): pl.pallas_call(functools.partial(exchange_kernel, axes, split), out_shape...]
    all_to_all x1 -> x0, starting transfers between devices: 9.86 us -> none  [shards(): lax.all_to_all(attended.reshape(expert_lanes, tok_rows, local_width), EXP...]
    all_to_all x1 -> x0, waiting for transfers between devices: 6.44 us -> none  [shards(): lax.all_to_all(attended.reshape(expert_lanes, tok_rows, local_width), EXP...]
    unnamed x22 -> x24, local copies, waits for them, and re-layouts: 5.45 us -> 6.22 us
  transfers between devices with their start and end apart: 4 -> 3, of which waited for: 3 -> 2; matrix products, arithmetic and copies ran while one was open for 8% -> 8% of each run, Pallas kernels for 5% -> 12%
where the time goes in v16:
time: 205 us; the launch traced here: 204 us
  waiting for transfers between devices  80.5 us (39%)
  Pallas kernels  55.3 us (27%)
  matrix products  19.2 us (9%)
  local copies, waits for them, and re-layouts  15.1 us (7%)
  between operations  13.8 us (7%)
  starting transfers between devices  12 us (6%)
  other arithmetic  8.3 us (4%)
    all_to_all x1, waiting for transfers between devices, shards(): lax.all_to_all(outgoing, 'group', split_axis=0, concat_axis=0, tiled=True)  71.8 us
    pallas_call x3, Pallas kernels, exchange(): pl.pallas_call(functools.partial(exchange_kernel, axes, split), out_shape...  44.9 us
    all_to_all x1, starting transfers between devices, shards(): lax.all_to_all(outgoing, 'group', split_axis=0, concat_axis=0, tiled=True)  12 us
    pallas_call x1, Pallas kernels, paged_attention(): pl.pallas_call(attention_kernel, out_shape=jax.ShapeDtypeStruct((rows, lo...  10.4 us
    all_gather x1, waiting for transfers between devices, shards(): lax.all_gather(normed, EXPERT, axis=0, tiled=True)  7.93 us
    unnamed x24, local copies, waits for them, and re-layouts  6.22 us
    dot_general x1, matrix products, shards(): jnp.einsum('gtc,gcd->gtd', rows_piece, head_weights, preferred_element_ty...  5.12 us
    dot_general x1, matrix products, shards(): jnp.dot(hidden, w_down[0], preferred_element_type=jnp.float32)  4.76 us
  transfers between devices with their start and end apart: 3, of which 2 were waited for; matrix products, arithmetic and copies ran while one was open for 8% of the time, Pallas kernels for 12%

profile of v16, /device:TPU:1, one launch (start us, length us, event | category | flops | bytes accessed | tf_op | source)
XLA Modules:
  0.0 204.2 jit_solution(8032529370204445505)
XLA Ops:
  6.5 1.3 fusion.15
  7.8 1.8 fusion.17
  9.7 0.7 all-gather.5.cloned.1.call-update
  10.7 0.6 select_reduce_fusion.1
  11.5 2.8 %gather_fusion = bf16[256,2,16,256]{3,2,1,0:T(8,128)(2,1)} fusion(bf16[128,2,16,256]{3,2,1,0:T(8,128)(2,1)S(1)} %copy-done, s32[1024]{0:T(1024)S(1)} %pad_clamp_fusion.2), kind=kCustom, calls=%fused_computation | custom fusion | bytes 8389632 | tf_op jit(solution)/shard_map/gather | solution.py:283
  14.3 12.0 %all-to-all-start = ((bf16[32,8,2,16,256]{4,3,2,1,0:T(8,128)(2,1)}), bf16[32,8,2,16,256]{4,3,2,1,0:T(8,128)(2,1)}, u32[]{:S(2)}, u32[]{:S(2)}) async-start(bf16[32,8,2,16,256]{4,3,2,1,0:T(8,128)(2,1)} %bitcast.66), calls=%async_computation | async-start | bytes 8388608 | tf_op jit(solution)/shard_map/all_to_all | solution.py:284
  26.3 4.8 %copy.34 = bf16[2048,3,256]{0,2,1:T(8,128)(2,1)} copy(bf16[2048,3,256]{2,0,1:T(8,128)(2,1)} %param.18) | data formatting | bytes 6291456 | tf_op args[5]
  31.7 0.6 dynamic_slice.7.len_ref
  33.9 7.9 %all-gather.3.cloned.1.call-done = bf16[512,2048]{1,0:T(8,128)(2,1)} async-done(((bf16[64,2048]{1,0:T(8,128)(2,1)}), bf16[512,2048]{1,0:T(8,128)(2,1)}) %all-gather.3.cloned.1.call-update) | async-done | bytes 2097168 | tf_op jit(solution)/shard_map/all_gather | solution.py:264
  41.9 4.3 %fusion = f32[512,3,2,128]{0,3,2,1:T(8,128)S(1)} fusion(bf16[3,2,128,2048]{3,2,1,0:T(8,128)(2,1)} %bitcast.68, bf16[512,2048]{1,0:T(8,128)(2,1)} %all-gather.3.cloned.1.call-done), kind=kOutput, calls=%fused_computation.7 | convolution fusion | flops 1610612736 | bytes 6815744 | tf_op jit(solution)/shard_map/dot_general | solution.py:263
  47.0 71.8 %all-to-all-done = bf16[32,8,2,16,256]{4,3,2,1,0:T(8,128)(2,1)} async-done(((bf16[32,8,2,16,256]{4,3,2,1,0:T(8,128)(2,1)}), bf16[32,8,2,16,256]{4,3,2,1,0:T(8,128)(2,1)}, u32[]{:S(2)}, u32[]{:S(2)}) %all-to-all-start) | async-done | bytes 4194336 | tf_op jit(solution)/shard_map/all_to_all | solution.py:284
  118.8 10.4 %shard_map.127 = bf16[512,256]{1,0:T(8,128)(2,1)S(1)} custom-call(s32[128]{0:T(128)S(1)} %multiply_add_fusion.2.slots_ref, s32[1]{0:T(128)} %dynamic_slice.7.len_ref, bf16[512,256]{1,0:T(8,128)(2,1)S(1)} %copy.41.q_ref, bf16[512,256]{1,0:T(8,128)(2,1)S(1)} %copy.42.nk_ref, bf16[512,256]{1,0:T(8,128)(2,1)S(1)} %copy.43.nv_ref, ...), custom_call_target="tpu_custom_call" | custom-call | flops 1342177280 | bytes 5242880 | tf_op jit(solution)/shard_map/pallas_call | solution.py:209
  129.2 0.7 copy-done.1
  129.9 13.4 %shard_map.128 = bf16[8,64,256]{2,1,0:T(8,128)(2,1)} custom-call(bf16[8,64,256]{2,1,0:T(8,128)(2,1)} %bitcast.62), custom_call_target="tpu_custom_call" | custom-call | tf_op jit(solution)/shard_map/pallas_call | solution.py:135
  143.4 5.1 %convert_reduce_fusion = f32[64,2048]{1,0:T(8,128)S(1)} fusion(bf16[8,64,256]{2,1,0:T(8,128)(2,1)} %shard_map.128, bf16[8,256,2048]{2,1,0:T(8,128)(2,1)} %bitcast.65), kind=kOutput, calls=%fused_computation.3 | convolution fusion | flops 539885568 | bytes 9175040 | tf_op jit(solution)/shard_map/gtc,gcd->gtd/dot_general | solution.py:302
  148.7 0.6 copy-done.3
  149.3 1.5 convolution_convert_fusion.2
  150.8 15.9 %shard_map.129 = bf16[8,32,2048]{2,1,0:T(8,128)(2,1)} custom-call(bf16[8,32,2048]{2,1,0:T(8,128)(2,1)} %bitcast.67), custom_call_target="tpu_custom_call" | custom-call | tf_op jit(solution)/shard_map/pallas_call | solution.py:135
  166.7 3.5 %fusion.5 = f32[256,512]{1,0:T(8,128)} fusion(bf16[256,2048]{1,0:T(8,128)(2,1)} %bitcast.69, bf16[1,2048,512]{2,1,0:T(8,128)(2,1)} %param.21), kind=kOutput, calls=%fused_computation.12 | convolution fusion | flops 536870912 | bytes 3670016 | tf_op jit(solution)/shard_map/dot_general | solution.py:331
  170.2 4.8 %convolution_convert_fusion.1 = bf16[256,2048]{1,0:T(8,128)(2,1)} fusion(bf16[1,512,2048]{2,1,0:T(8,128)(2,1)} %param.23, bf16[256,2048]{1,0:T(8,128)(2,1)S(1)} %bitcast.70, bf16[1,2048,512]{2,1,0:T(8,128)(2,1)} %param.22, f32[256,512]{1,0:T(8,128)} %fusion.5), kind=kOutput, calls=%fused_computation.5 | convolution fusion | flops 1075052544 | bytes 6815744 | tf_op jit(solution)/shard_map/dot_general | solution.py:335
  174.9 15.6 %shard_map.130 = bf16[8,32,2048]{2,1,0:T(8,128)(2,1)} custom-call(bf16[8,32,2048]{2,1,0:T(8,128)(2,1)} %bitcast.71), custom_call_target="tpu_custom_call" | custom-call | tf_op jit(solution)/shard_map/pallas_call | solution.py:135
  190.6 3.2 %gather_fusion.2 = bf16[64,2048]{1,0:T(8,128)(2,1)} fusion(bf16[256,2048]{1,0:T(8,128)(2,1)} %bitcast.63, s32[1024]{0:T(1024)S(1)} %get-tuple-element.26), kind=kCustom, calls=%fused_computation.2 | custom fusion | bytes 524544 | tf_op jit(solution)/shard_map/gather | solution.py:344
  193.7 1.5 gather_fusion.1
  195.2 2.2 %add_add_fusion = f32[64,2048]{1,0:T(8,128)} fusion(bf16[64,2048]{1,0:T(8,128)(2,1)} %gather_fusion.2, bf16[64,2048]{1,0:T(8,128)(2,1)} %gather_fusion.1, f32[64]{0:T(128)S(1)} %get-tuple-element.19, f32[64]{0:T(128)S(1)} %get-tuple-element.18, f32[64,2048]{1,0:T(8,128)} %copy-done.3, bf16[64,2048]{1,0:T(8,128)(2,1)S(1)} %copy-done.4), kind=kLoop, calls=%fused_computation.25 | loop fusion | flops 1048576 | bytes 1835520 | tf_op jit(solution)/shard_map/add | solution.py:345
  (59 shorter events, 3.6 us)
Async XLA Ops:
  6.5 4.9 %copy-start = (bf16[128,2,16,256]{3,2,1,0:T(8,128)(2,1)S(1)}, bf16[128,2,16,256]{3,2,1,0:T(8,128)(2,1)}, u32[]{:S(2)}) copy-start(bf16[128,2,16,256]{3,2,1,0:T(8,128)(2,1)} %param.16) | copy-start | bytes 6291460
  6.5 3.9 %copy-start.6 = (s32[32,128]{1,0:T(8,128)S(1)}, s32[32,128]{1,0:T(8,128)}, u32[]{:S(2)}) copy-start(s32[32,128]{1,0:T(8,128)} %param.15) | copy-start | bytes 49156
  6.5 35.3 %all-gather.3.cloned.1.call-start = ((), (), s32[]{:S(2)}) async-start(), calls=%async_computation.1 | async-start | bytes 2359296 | tf_op jit(solution)/shard_map/all_gather | solution.py:264
  9.6 133.7 %all-gather.5.cloned.1.call-start = ((), (), s32[]{:S(2)}) async-start(), calls=%async_computation.2 | async-start | bytes 9437184 | tf_op jit(solution)/shard_map/all_gather | solution.py:299
  14.3 104.5 %all-to-all-start = ((bf16[32,8,2,16,256]{4,3,2,1,0:T(8,128)(2,1)}), bf16[32,8,2,16,256]{4,3,2,1,0:T(8,128)(2,1)}, u32[]{:S(2)}, u32[]{:S(2)}) async-start(bf16[32,8,2,16,256]{4,3,2,1,0:T(8,128)(2,1)} %bitcast.66), calls=%async_computation | async-start | bytes 8388608 | tf_op jit(solution)/shard_map/all_to_all | solution.py:284
  26.2 4.8 %copy-start.8 = (s32[64,2]{0,1:T(2,128)S(1)}, s32[64,2]{0,1:T(2,128)}, u32[]{:S(2)}) copy-start(s32[64,2]{0,1:T(2,128)} %param.24) | copy-start | bytes 1540
  26.3 5.4 %copy-start.10 = (s32[32]{0:T(128)S(1)}, s32[32]{0:T(128)}, u32[]{:S(2)}) copy-start(s32[32]{0:T(128)} %param.14) | copy-start | bytes 388
  26.3 7.1 %copy-start.9 = (f32[64,2]{0,1:T(2,128)S(1)}, f32[64,2]{0,1:T(2,128)}, u32[]{:S(2)}) copy-start(f32[64,2]{0,1:T(2,128)} %param.25) | copy-start | bytes 1540
  129.2 0.7 copy-start.1
  143.4 5.2 %copy-start.4 = (bf16[64,2048]{1,0:T(8,128)(2,1)S(1)}, bf16[64,2048]{1,0:T(8,128)(2,1)}, u32[]{:S(2)}) copy-start(bf16[64,2048]{1,0:T(8,128)(2,1)} %param.13) | copy-start | bytes 786436
  143.4 5.9 %copy-start.7 = (f32[2048]{0:T(1024)S(1)}, f32[2048]{0:T(1024)}, u32[]{:S(2)}) copy-start(f32[2048]{0:T(1024)} %param.20) | copy-start | bytes 24580
  148.5 0.8 copy-start.3
  166.7 3.5 %copy-start.5 = (bf16[8,32,2048]{2,1,0:T(8,128)(2,1)S(1)}, bf16[8,32,2048]{2,1,0:T(8,128)(2,1)}, u32[]{:S(2)}) copy-start(bf16[8,32,2048]{2,1,0:T(8,128)(2,1)} %shard_map.129) | copy-start | bytes 3145732
  190.6 3.2 %copy-start.2 = (bf16[8,32,2048]{2,1,0:T(8,128)(2,1)S(1)}, bf16[8,32,2048]{2,1,0:T(8,128)(2,1)}, u32[]{:S(2)}) copy-start(bf16[8,32,2048]{2,1,0:T(8,128)(2,1)} %shard_map.130) | copy-start | bytes 3145732
Sparse Core Ops, SparseCore 0:
  9.8 32.0 all-gather.2
  43.7 52.6 all-gather.4
